TPU v7x, 512 devices: a whole 4x8x8 slice. The times are simulated.
512 devices in a mesh: lat: 32 (over y, x), lon: 16 (over z, core).
Axes of the slice: x: 4, y: 8, z: 8, core: 2. Of those that a mesh axis runs over, the one named last changes fastest.
Arguments:
- tracers: float32 [2, 2880, 24576], P(None, 'lon', 'lat'), may hold values from -6 to 6
- wind_field: float32 [2, 2, 1024, 2880], P(None, None, 'lat', 'lon'), may hold values from -4 to 4
Outputs:
- advected: float32 [2, 2880, 24576], P(None, 'lon', 'lat')
- smoothed_winds: float32 [2, 2, 1024, 2880], P(None, None, 'lat', 'lon')
All inputs are finite; a program needn't handle non-finite values.
Results may differ from a plain program's by a relative error of at most 0.00007.
Values sent between devices are 32-bit elements; how exact they have to be, the bound alone decides.
A program may use at most 64 MiB of HBM per device.

v0:
```python
import math

import jax
import jax.numpy as jnp
from jax import lax
from jax.sharding import PartitionSpec as P

COURANT = 0.3
COS_FLOOR = 0.5
EXACT_MODE = lax.Precision.HIGHEST


def extended(array, sides, width, wrap):
    for axis, dim in sides:
        devices, length = (lax.axis_size(axis), array.shape[dim])
        up = [(i, (i + 1) % devices) for i in range(devices if wrap else devices - 1)]
        down = [(j, i) for i, j in up]
        last = lax.slice_in_dim(array, length - width, length, axis=dim)
        first = lax.slice_in_dim(array, 0, width, axis=dim)
        before = lax.ppermute(last, axis, up)
        after = lax.ppermute(first, axis, down)
        array = jnp.concatenate([before, array, after], axis=dim)
    return array


def damping(row_cosine, wavenumber, lon_total):
    sine = jnp.sin(wavenumber.astype(jnp.float32) * (math.pi / lon_total))
    divisor = jnp.where(wavenumber == 0, 1.0, sine * sine)
    scaled = (row_cosine / COS_FLOOR) ** 2
    scaled = scaled.reshape(scaled.shape + (1,) * wavenumber.ndim)
    return jnp.where(wavenumber == 0, 1.0, jnp.minimum(1.0, scaled / divisor))


def face_values(padded, axis, cells, stride):

    def offset_cells(offset):
        return lax.slice_in_dim(padded, offset * stride, (offset + cells + 1) * stride, axis=axis)

    left = (
        2.0 * offset_cells(0)
        - 13.0 * offset_cells(1)
        + 47.0 * offset_cells(2)
        + 27.0 * offset_cells(3)
        - 3.0 * offset_cells(4)
    ) / 60.0
    right = (
        2.0 * offset_cells(5)
        - 13.0 * offset_cells(4)
        + 47.0 * offset_cells(3)
        + 27.0 * offset_cells(2)
        - 3.0 * offset_cells(1)
    ) / 60.0
    return (left, right)


def upwind(speed, left, right):
    return jnp.maximum(speed, 0.0) * left + jnp.minimum(speed, 0.0) * right


def apply_table(values, table):
    return jnp.einsum("rkm,mb->rkb", values, table, precision=EXACT_MODE)


def filter_modes(real_part, imag_part, lon_block, row_cosine, lon_total):
    columns = real_part.shape[-1]
    blocks = lon_total // columns
    column_ids = jnp.arange(columns, dtype=jnp.int32)
    twist = (
        2.0
        * math.pi
        * (column_ids[None, :] * lon_block[:, None] % lon_total).astype(jnp.float32)
        / lon_total
    )
    twist_cos = jnp.cos(twist)
    twist_sin = jnp.sin(twist)
    shifted_re = real_part * twist_cos + imag_part * twist_sin
    shifted_im = imag_part * twist_cos - real_part * twist_sin
    table_turn = (
        2.0
        * math.pi
        * (column_ids[:, None] * column_ids[None, :] % columns).astype(jnp.float32)
        / columns
    )
    table_cos = jnp.cos(table_turn)
    table_sin = jnp.sin(table_turn)
    modes_re = apply_table(shifted_re, table_cos) + apply_table(shifted_im, table_sin)
    modes_im = apply_table(shifted_im, table_cos) - apply_table(shifted_re, table_sin)
    wavenumber = lon_block[:, None] + blocks * column_ids[None, :]
    factor = damping(row_cosine, wavenumber, lon_total)
    modes_re = modes_re * factor
    modes_im = modes_im * factor
    back_re = apply_table(modes_re, table_cos) - apply_table(modes_im, table_sin)
    back_im = apply_table(modes_im, table_cos) + apply_table(modes_re, table_sin)
    return (back_re * twist_cos - back_im * twist_sin, back_im * twist_cos + back_re * twist_sin)


def spectral(flat_winds, row_cosine, lon_total):
    flat_rows, columns = flat_winds.shape
    lon_count = lax.axis_size("lon")
    lon_index = lax.axis_index("lon")
    row_share = flat_rows // lon_count
    full_rows = lax.all_to_all(flat_winds, "lon", split_axis=0, concat_axis=1, tiled=True)
    own_cosine = lax.dynamic_slice_in_dim(row_cosine, lon_index * row_share, row_share, 0)
    lon_grid = full_rows.reshape(row_share, lon_count, columns)
    block_ids = jnp.arange(lon_count, dtype=jnp.int32)
    phase_angle = (
        2.0
        * math.pi
        * (block_ids[:, None] * block_ids[None, :] % lon_count).astype(jnp.float32)
        / lon_count
    )
    phase_cos = jnp.cos(phase_angle)
    phase_sin = jnp.sin(phase_angle)
    real_part = jnp.einsum("rpm,pk->rkm", lon_grid, phase_cos, precision=EXACT_MODE)
    imag_part = -jnp.einsum("rpm,pk->rkm", lon_grid, phase_sin, precision=EXACT_MODE)
    out_re, out_im = filter_modes(real_part, imag_part, block_ids, own_cosine, lon_total)
    restored = (
        jnp.einsum("rkm,kp->rpm", out_re, phase_cos, precision=EXACT_MODE)
        - jnp.einsum("rkm,kp->rpm", out_im, phase_sin, precision=EXACT_MODE)
    ) / lon_total
    return lax.all_to_all(
        restored.reshape(row_share, lon_total), "lon", split_axis=1, concat_axis=0, tiled=True
    )


def local(tracers, wind_field):
    levels, lon_cols, merged = tracers.shape
    lat_rows = wind_field.shape[2]
    tracer_count = merged // lat_rows
    lon_total = lon_cols * lax.axis_size("lon")
    lat_total = lat_rows * lax.axis_size("lat")
    first_row = lax.axis_index("lat") * lat_rows
    row_ids = first_row + jnp.arange(lat_rows, dtype=jnp.int32)
    row_cosine = jnp.cos(
        (row_ids.astype(jnp.float32) + 0.5) * (math.pi / lat_total) - 0.5 * math.pi
    )
    flat_winds = wind_field.reshape(2 * levels * lat_rows, lon_cols)
    flat_cosine = jnp.tile(row_cosine, 2 * levels)
    smoothed = spectral(flat_winds, flat_cosine, lon_total)
    smoothed = smoothed.reshape(2, levels, lat_rows, lon_cols)
    east_turned = jnp.transpose(smoothed[0], (0, 2, 1))
    north_turned = jnp.transpose(smoothed[1], (0, 2, 1))
    zonal_stack = jnp.concatenate([tracers, east_turned], axis=2)
    zonal_pad = extended(zonal_stack, (("lon", 1),), 3, True)
    east_wind = zonal_pad[:, :, merged:]
    zonal_speed = 0.5 * (east_wind[:, 2 : lon_cols + 3] + east_wind[:, 3 : lon_cols + 4])
    zonal_speed = jnp.repeat(zonal_speed, tracer_count, axis=2)
    left_x, right_x = face_values(zonal_pad[:, :, :merged], 1, lon_cols, 1)
    zonal_flux = upwind(zonal_speed, left_x, right_x)
    slot_count = tracer_count + 1
    merid_stack = jnp.concatenate(
        [tracers.reshape(levels, lon_cols, lat_rows, tracer_count), north_turned[..., None]], axis=3
    )
    merid_stack = merid_stack.reshape(levels, lon_cols, lat_rows * slot_count)
    merid_pad = extended(merid_stack, (("lat", 2),), 3 * slot_count, False)
    merid_pad = merid_pad.reshape(levels, lon_cols, lat_rows + 6, slot_count)
    north_wind = merid_pad[..., tracer_count]
    tracer_pad = merid_pad[..., :tracer_count].reshape(
        levels, lon_cols, (lat_rows + 6) * tracer_count
    )
    face_ids = first_row + jnp.arange(lat_rows + 1, dtype=jnp.int32)
    face_cosine = jnp.cos(face_ids.astype(jnp.float32) * (math.pi / lat_total) - 0.5 * math.pi)
    face_cosine = jnp.where((face_ids == 0) | (face_ids == lat_total), 0.0, face_cosine)
    merid_speed = (
        0.5
        * (north_wind[:, :, 2 : lat_rows + 3] + north_wind[:, :, 3 : lat_rows + 4])
        * face_cosine[None, None, :]
    )
    merid_speed = jnp.repeat(merid_speed, tracer_count, axis=2)
    left_y, right_y = face_values(tracer_pad, 2, lat_rows, tracer_count)
    merid_flux = upwind(merid_speed, left_y, right_y)
    metric = jnp.repeat(1.0 / jnp.maximum(row_cosine, COS_FLOOR), tracer_count)
    change = COURANT * (zonal_flux[:, 1:] - zonal_flux[:, :-1]) + COURANT * (
        merid_flux[:, :, tracer_count:] - merid_flux[:, :, :-tracer_count]
    )
    advected = tracers - metric[None, None, :] * change
    return (advected, smoothed)


def solution(mesh):
    placed = (P(None, "lon", "lat"), P(None, None, "lat", "lon"))
    return jax.shard_map(
        local,
        mesh=mesh,
        in_specs=placed,
        out_specs=(P(None, "lon", "lat"), P(None, None, "lat", "lon")),
        check_vma=False,
    )
```

profile of v0, /device:TPU:33, one launch (start us, length us, event | category | flops | bytes accessed | tf_op | source)
XLA Modules:
  0.0 70.4 jit_solution(12289713134484687429)
XLA Ops:
  0.6 11.0 %all-to-all-start = ((f32[16,8,180]{2,1,0:T(8,128)}), f32[16,8,180]{2,1,0:T(8,128)S(1)}, u32[]{:S(2)}, u32[]{:S(2)}) async-start(f32[16,8,180]{2,1,0:T(8,128)} %bitcast.89), calls=%async_computation | async-start | bytes 262144 | tf_op jit(solution)/shard_map/all_to_all | solution.py:102
  12.1 8.7 %all-to-all-done = f32[16,8,180]{2,1,0:T(8,128)S(1)} async-done(((f32[16,8,180]{2,1,0:T(8,128)}), f32[16,8,180]{2,1,0:T(8,128)S(1)}, u32[]{:S(2)}, u32[]{:S(2)}) %all-to-all-start) | async-done | bytes 92192 | tf_op jit(solution)/shard_map/all_to_all | solution.py:102
  21.5 1.0 %fusion.42 = f32[8,16,180]{2,1,0:T(8,128)S(1)} fusion(f32[16,8,180]{2,0,1:T(8,128)S(1)} %fusion.67, f32[16,8,180]{2,0,1:T(8,128)S(1)} %convolution_negate_fusion, f32[16,180]{1,0:T(8,128)S(1)} %get-tuple-element.18, f32[16,180]{1,0:T(8,128)S(1)} %get-tuple-element.19), kind=kOutput, calls=%fused_computation.62 | convolution fusion | flops 50127120 | bytes 299520 | tf_op jit(solution)/shard_map/rkm,mb->rkb/dot_general | solution.py:61
  22.5 1.0 %fusion.46 = f32[8,16,180]{2,1,0:T(8,128)S(1)} fusion(f32[16,8,180]{2,0,1:T(8,128)S(1)} %convolution_negate_fusion, f32[16,8,180]{2,0,1:T(8,128)S(1)} %fusion.67, f32[16,180]{1,0:T(8,128)S(1)} %get-tuple-element.18, f32[16,180]{1,0:T(8,128)S(1)} %get-tuple-element.19), kind=kOutput, calls=%fused_computation.66 | convolution fusion | flops 50127120 | bytes 299520 | tf_op jit(solution)/shard_map/rkm,mb->rkb/dot_general | solution.py:61
  23.5 1.0 %fusion.31 = f32[8,16,180]{2,1,0:T(8,128)S(1)} fusion(f32[8,16,180]{2,1,0:T(8,128)S(1)} %fusion.42, f32[16,180]{1,0:T(8,128)S(1)} %multiply_select_fusion, f32[8]{0:T(128)S(1)} %multiply_multiply_fusion, pred[16,180]{1,0:T(8,128)(4,1)S(1)} %fusion.110, f32[16,8,180]{2,0,1:T(8,128)S(1)} %convolution_negate_fusion, f32[16,8,180]{2,0,1:T(8,128)S(1)} %fusion.67, ...), kind=kOutput, calls=%fused_computation.48 | convolution fusion | flops 50242320 | bytes 406112 | tf_op jit(solution)/shard_map/rkm,mb->rkb/dot_general | solution.py:61
  24.6 1.0 %fusion.40 = f32[8,16,180]{2,1,0:T(8,128)S(1)} fusion(f32[8,16,180]{2,1,0:T(8,128)S(1)} %fusion.31), kind=kOutput, calls=%fused_computation.60 | convolution fusion | flops 50058000 | bytes 184320 | tf_op jit(solution)/shard_map/rkm,mb->rkb/dot_general | solution.py:61
  25.6 1.0 %fusion.32 = f32[8,16,180]{2,1,0:T(8,128)S(1)} fusion(f32[8,16,180]{2,1,0:T(8,128)S(1)} %fusion.46, f32[16,180]{1,0:T(8,128)S(1)} %multiply_select_fusion, f32[8]{0:T(128)S(1)} %multiply_multiply_fusion, pred[16,180]{1,0:T(8,128)(4,1)S(1)} %fusion.110, f32[16,8,180]{2,0,1:T(8,128)S(1)} %fusion.67, f32[16,8,180]{2,0,1:T(8,128)S(1)} %convolution_negate_fusion, ...), kind=kOutput, calls=%fused_computation.50 | convolution fusion | flops 50242320 | bytes 406112 | tf_op jit(solution)/shard_map/rkm,mb->rkb/dot_general | solution.py:61
  26.6 1.0 %fusion.44 = f32[8,16,180]{2,1,0:T(8,128)S(1)} fusion(f32[8,16,180]{2,1,0:T(8,128)S(1)} %fusion.32), kind=kOutput, calls=%fused_computation.64 | convolution fusion | flops 50058000 | bytes 184320 | tf_op jit(solution)/shard_map/rkm,mb->rkb/dot_general | solution.py:61
  27.7 1.0 %convolution_add_fusion = f32[8,16,180]{2,1,0:T(8,128)S(1)} fusion(f32[8,16,180]{2,1,0:T(8,128)S(1)} %fusion.40, f32[8,16,180]{2,1,0:T(8,128)S(1)} %fusion.32), kind=kOutput, calls=%fused_computation.45 | convolution fusion | flops 50081040 | bytes 276480 | tf_op jit(solution)/shard_map/rkm,mb->rkb/dot_general | solution.py:61
  28.7 1.0 %convolution_subtract_fusion.1 = f32[8,16,180]{2,1,0:T(8,128)S(1)} fusion(f32[8,16,180]{2,1,0:T(8,128)S(1)} %fusion.44, f32[8,16,180]{2,1,0:T(8,128)S(1)} %fusion.31), kind=kOutput, calls=%fused_computation.46 | convolution fusion | flops 50081040 | bytes 276480 | tf_op jit(solution)/shard_map/rkm,mb->rkb/dot_general | solution.py:61
  29.8 0.3 fusion.72
  30.1 0.3 fusion.30
  30.4 0.7 %copy.17 = f32[8,16,180]{2,0,1:T(8,128)} copy(f32[8,16,180]{2,1,0:T(8,128)S(1)} %fusion.30) | data formatting | bytes 184320 | tf_op jit(solution)/shard_map/div | solution.py:117
  31.1 3.6 %all-to-all-start.1 = ((f32[8,16,180]{2,0,1:T(8,128)}), f32[8,16,180]{2,0,1:T(8,128)S(1)}, u32[]{:S(2)}, u32[]{:S(2)}) async-start(f32[8,16,180]{2,0,1:T(8,128)} %copy.17), calls=%async_computation.1 | async-start | bytes 262144 | tf_op jit(solution)/shard_map/all_to_all | solution.py:121
  34.9 0.7 %copy.28 = f32[2,180,768]{1,2,0:T(8,128)S(1)} copy(f32[2,180,768]{2,0,1:T(2,128)S(1)} %copy-done.2) | data formatting | bytes 2211840 | tf_op args[0]
  35.7 7.4 %all-to-all-done.1 = f32[8,16,180]{2,0,1:T(8,128)S(1)} async-done(((f32[8,16,180]{2,0,1:T(8,128)}), f32[8,16,180]{2,0,1:T(8,128)S(1)}, u32[]{:S(2)}, u32[]{:S(2)}) %all-to-all-start.1) | async-done | bytes 92192 | tf_op jit(solution)/shard_map/all_to_all | solution.py:121
  44.1 1.8 %collective-permute-start = (f32[2,3,800]{2,0,1:T(2,128)S(1)}, f32[2,3,800]{2,0,1:T(2,128)S(1)}, u32[]{:S(2)}, u32[]{:S(2)}) collective-permute-start(f32[2,3,800]{2,0,1:T(2,128)S(1)} %copy.19), channel_id=1, source_target_pairs={{0,1},{1,2},{2,3},{3,4},{4,5},{5,6},{6,7},{7,8},{8,9},{9,10},{10,1... | collective-permute-start | bytes 57608 | tf_op jit(solution)/shard_map/ppermute | solution.py:20
  46.0 1.3 %copy.25 = f32[2,180,32,25]{1,0,3,2:T(2,128)S(1)} copy(f32[2,180,32,25]{1,3,2,0:T(8,128)S(1)} %pad_maximum_fusion) | data formatting | bytes 2304000 | tf_op jit(solution)/shard_map/concatenate | solution.py:151
  47.4 0.8 %fusion.174 = (f32[2,180,75]{1,0,2:T(2,128)}, f32[2,180,75]{1,0,2:T(2,128)}) fusion(f32[2,180,800]{1,0,2:T(2,128)S(1)} %bitcast.78), kind=kLoop, calls=%fused_computation.196 | loop fusion | bytes 432000 | tf_op jit(solution)/shard_map/slice | solution.py:18
  48.2 3.1 %collective-permute-start.2 = (f32[2,180,75]{1,0,2:T(2,128)}, f32[2,180,75]{1,0,2:T(2,128)}, u32[]{:S(2)}, u32[]{:S(2)}) collective-permute-start(f32[2,180,75]{1,0,2:T(2,128)} %get-tuple-element.12), channel_id=1, source_target_pairs={{0,16},{16,32},{32,48},{48,64},{64,80},{80,96},{96,112},{112,128},... | collective-permute-start | bytes 324008 | tf_op jit(solution)/shard_map/ppermute | solution.py:20
  51.3 5.5 %collective-permute-start.3 = (f32[2,180,75]{1,0,2:T(2,128)}, f32[2,180,75]{1,0,2:T(2,128)}, u32[]{:S(2)}, u32[]{:S(2)}) collective-permute-start(f32[2,180,75]{1,0,2:T(2,128)} %get-tuple-element.13), channel_id=1, source_target_pairs={{16,0},{32,16},{48,32},{64,48},{80,64},{96,80},{112,96},{128,112},... | collective-permute-start | bytes 324008 | tf_op jit(solution)/shard_map/ppermute | solution.py:21
  56.8 1.2 %copy.20 = f32[2,3,800]{1,2,0:T(8,128)} copy(f32[2,3,800]{2,0,1:T(2,128)S(1)} %collective-permute-done) | data formatting | bytes 38400 | tf_op jit(solution)/shard_map/ppermute | solution.py:20
  58.0 1.2 %copy.22 = f32[2,3,800]{1,2,0:T(8,128)} copy(f32[2,3,800]{2,0,1:T(2,128)S(1)} %collective-permute-done.1) | data formatting | bytes 38400 | tf_op jit(solution)/shard_map/ppermute | solution.py:21
  59.2 1.0 %broadcast_maximum_fusion.1 = (f32[2,181,32]{1,2,0:T(8,128)S(1)}, f32[2,181,32]{1,2,0:T(8,128)S(1)}) fusion(f32[2,3,800]{1,2,0:T(8,128)} %copy.22, f32[2,180,32]{1,2,0:T(8,128)S(1)} %bitcast.85, f32[2,180,768]{1,2,0:T(8,128)S(1)} %copy.28, f32[2,3,800]{1,2,0:T(8,128)} %copy.20), kind=kLoop, calls=%fused_computation.122 | loop fusion | flops 81088 | bytes 1283072 | tf_op jit(solution)/shard_map/max | solution.py:57
  60.6 0.7 %maximum_maximum_fusion = (f32[2,183,800]{1,2,0:T(8,128)S(1)}, f32[2,183,800]{1,2,0:T(8,128)S(1)}) fusion(f32[2,180,32]{1,2,0:T(8,128)S(1)} %bitcast.86, f32[2,180,768]{1,2,0:T(8,128)S(1)} %copy.28, f32[2,3,800]{1,2,0:T(8,128)S(1)} %copy-done, f32[2,3,800]{1,2,0:T(8,128)S(1)} %copy-done.1), kind=kLoop, calls=%fused_computation.4 | loop fusion | flops 1171200 | bytes 3532800 | tf_op jit(solution)/shard_map/concatenate | solution.py:22
  61.4 1.7 %fusion.22 = f32[2,181,768]{1,2,0:T(8,128)S(1)} fusion(f32[2,183,800]{1,2,0:T(8,128)S(1)} %get-tuple-element.9, f32[2,183,800]{1,2,0:T(8,128)S(1)} %get-tuple-element.8, f32[2,181,32]{1,2,0:T(8,128)S(1)} %broadcast_minimum_fusion.1, f32[2,181,32]{1,2,0:T(8,128)S(1)} %get-tuple-element.6), kind=kLoop, calls=%fused_computation.33 | loop fusion | flops 6394368 | bytes 7877120 | tf_op jit(solution)/shard_map/add | solution.py:57
  63.1 2.0 %pad_maximum_fusion.1 = f32[2,180,950]{1,0,2:T(2,128)S(1)} fusion(f32[2,180,75]{1,0,2:T(2,128)} %collective-permute-done.3, f32[2,180,800]{1,0,2:T(2,128)S(1)} %bitcast.79, f32[2,180,75]{1,0,2:T(2,128)} %collective-permute-done.2), kind=kLoop, calls=%fused_computation.1 | loop fusion | flops 684000 | bytes 2736000 | tf_op jit(solution)/shard_map/concatenate | solution.py:22
  65.1 1.0 %slice.157 = f32[2,180,38,24]{1,0,3,2:T(2,128)S(1)} slice(f32[2,180,38,25]{1,0,3,2:T(2,128)S(1)} %bitcast.81), slice={[0:2], [0:180], [0:38], [0:24]} | slice | bytes 2626560 | tf_op jit(solution)/shard_map/slice | solution.py:158
  66.4 1.2 %fusion.6 = f32[2,180,792]{1,2,0:T(8,128)S(1)} fusion(f32[2,180,912]{1,2,0:T(8,128)S(1)} %bitcast.76, f32[2,180,33]{1,2,0:T(8,128)S(1)} %get-tuple-element.17, f32[2,180,33]{1,2,0:T(8,128)S(1)} %get-tuple-element.16), kind=kLoop, calls=%fused_computation.13 | loop fusion | flops 6557760 | bytes 8078400 | tf_op jit(solution)/shard_map/add | solution.py:57
  67.6 0.7 fusion.15
  68.3 1.5 %copy.29 = f32[2,180,768]{2,0,1:T(2,128)} copy(f32[2,180,768]{1,2,0:T(8,128)S(1)} %fusion.15) | data formatting | bytes 2211840
  69.8 0.7 copy.41
  (35 shorter events, 3.1 us)
Async XLA Ops:
  0.6 20.2 %all-to-all-start = ((f32[16,8,180]{2,1,0:T(8,128)}), f32[16,8,180]{2,1,0:T(8,128)S(1)}, u32[]{:S(2)}, u32[]{:S(2)}) async-start(f32[16,8,180]{2,1,0:T(8,128)} %bitcast.89), calls=%async_computation | async-start | bytes 262144 | tf_op jit(solution)/shard_map/all_to_all | solution.py:102
  26.6 8.3 %copy-start.2 = (f32[2,180,768]{2,0,1:T(2,128)S(1)}, f32[2,180,768]{2,0,1:T(2,128)}, u32[]{:S(2)}) copy-start(f32[2,180,768]{2,0,1:T(2,128)} %param.2) | copy-start | bytes 3317764
  31.1 11.9 %all-to-all-start.1 = ((f32[8,16,180]{2,0,1:T(8,128)}), f32[8,16,180]{2,0,1:T(8,128)S(1)}, u32[]{:S(2)}, u32[]{:S(2)}) async-start(f32[8,16,180]{2,0,1:T(8,128)} %copy.17), calls=%async_computation.1 | async-start | bytes 262144 | tf_op jit(solution)/shard_map/all_to_all | solution.py:121
  44.0 13.9 %collective-permute-start.1 = (f32[2,3,800]{2,0,1:T(2,128)S(1)}, f32[2,3,800]{2,0,1:T(2,128)S(1)}, u32[]{:S(2)}, u32[]{:S(2)}) collective-permute-start(f32[2,3,800]{2,0,1:T(2,128)S(1)} %copy.21), channel_id=1, source_target_pairs={{1,0},{2,1},{3,2},{4,3},{5,4},{6,5},{7,6},{8,7},{9,8},{10,9},{11,1... | collective-permute-start | bytes 57608 | tf_op jit(solution)/shard_map/ppermute | solution.py:21
  44.1 12.7 %collective-permute-start = (f32[2,3,800]{2,0,1:T(2,128)S(1)}, f32[2,3,800]{2,0,1:T(2,128)S(1)}, u32[]{:S(2)}, u32[]{:S(2)}) collective-permute-start(f32[2,3,800]{2,0,1:T(2,128)S(1)} %copy.19), channel_id=1, source_target_pairs={{0,1},{1,2},{2,3},{3,4},{4,5},{5,6},{6,7},{7,8},{8,9},{9,10},{10,1... | collective-permute-start | bytes 57608 | tf_op jit(solution)/shard_map/ppermute | solution.py:20
  48.2 14.9 %collective-permute-start.2 = (f32[2,180,75]{1,0,2:T(2,128)}, f32[2,180,75]{1,0,2:T(2,128)}, u32[]{:S(2)}, u32[]{:S(2)}) collective-permute-start(f32[2,180,75]{1,0,2:T(2,128)} %get-tuple-element.12), channel_id=1, source_target_pairs={{0,16},{16,32},{32,48},{48,64},{64,80},{80,96},{96,112},{112,128},... | collective-permute-start | bytes 324008 | tf_op jit(solution)/shard_map/ppermute | solution.py:20
  51.3 11.8 %collective-permute-start.3 = (f32[2,180,75]{1,0,2:T(2,128)}, f32[2,180,75]{1,0,2:T(2,128)}, u32[]{:S(2)}, u32[]{:S(2)}) collective-permute-start(f32[2,180,75]{1,0,2:T(2,128)} %get-tuple-element.13), channel_id=1, source_target_pairs={{16,0},{32,16},{48,32},{64,48},{80,64},{96,80},{112,96},{128,112},... | collective-permute-start | bytes 324008 | tf_op jit(solution)/shard_map/ppermute | solution.py:21
  59.2 1.2 %copy-start = (f32[2,3,800]{1,2,0:T(8,128)S(1)}, f32[2,3,800]{1,2,0:T(8,128)}, u32[]{:S(2)}) copy-start(f32[2,3,800]{1,2,0:T(8,128)} %copy.20) | copy-start | bytes 57604
  59.2 1.4 %copy-start.1 = (f32[2,3,800]{1,2,0:T(8,128)S(1)}, f32[2,3,800]{1,2,0:T(8,128)}, u32[]{:S(2)}) copy-start(f32[2,3,800]{1,2,0:T(8,128)} %copy.22) | copy-start | bytes 57604
where the time goes:
time: 70.9 us; the launch traced here: 70.4 us
  starting transfers between devices  25 us (35%)
  waiting for transfers between devices  16.1 us (23%)
  local copies, waits for them, and re-layouts  10.7 us (15%)
  matrix products  9.48 us (13%)
  other arithmetic  8.25 us (12%)
  between operations  0.95 us (1%)
    all_to_all x1, starting transfers between devices, spectral(): lax.all_to_all(flat_winds, 'lon', split_axis=0, concat_axis=1, tiled=True)  11 us
    all_to_all x1, waiting for transfers between devices, spectral(): lax.all_to_all(flat_winds, 'lon', split_axis=0, concat_axis=1, tiled=True)  8.74 us
    dot_general x8, matrix products, apply_table(): return jnp.einsum('rkm,mb->rkb', values, table, precision=EXACT_MODE)  8.22 us
    all_to_all x1, waiting for transfers between devices, spectral(): lax.all_to_all(restored.reshape(row_share, lon_total), 'lon', split_axis=...  7.39 us
    ppermute x2, starting transfers between devices, extended(): after = lax.ppermute(first, axis, down)  5.48 us
    ppermute x2, starting transfers between devices, extended(): before = lax.ppermute(last, axis, up)  4.87 us
    all_to_all x1, starting transfers between devices, spectral(): lax.all_to_all(restored.reshape(row_share, lon_total), 'lon', split_axis=...  3.59 us
    unnamed x9, local copies, waits for them, and re-layouts  3.28 us
  transfers between devices with their start and end apart: 6, of which 2 were waited for; matrix products, arithmetic and copies ran while one was open for 14% of the time, Pallas kernels for 0%

commit v1 on v0

--- a/solution.py
+++ b/solution.py
@@ -1,9 +1,14 @@
+import functools
 import math
 
 import jax
 import jax.numpy as jnp
 from jax import lax
+from jax.experimental import pallas as pl
+from jax.experimental.pallas import tpu as pltpu
 from jax.sharding import PartitionSpec as P
+
+MESH = pl.DeviceIdType.MESH
 
 COURANT = 0.3
 COS_FLOOR = 0.5
@@ -94,14 +99,61 @@
     return (back_re * twist_cos - back_im * twist_sin, back_im * twist_cos + back_re * twist_sin)
 
 
+def exchange_kernel(n, x_ref, o_ref, send_sem, recv_sem):
+    me = lax.axis_index("lon")
+    band = lax.axis_index("lat")
+    barrier = pltpu.get_barrier_semaphore()
+    for k in range(1, n):
+        peer = lax.rem(me + k, n)
+        pl.semaphore_signal(barrier, inc=1, device_id=(band, peer), device_id_type=MESH)
+    pl.semaphore_wait(barrier, n - 1)
+    sends = []
+    for k in range(1, n):
+        peer = lax.rem(me + k, n)
+        copy = pltpu.make_async_remote_copy(
+            src_ref=x_ref.at[peer],
+            dst_ref=o_ref.at[me],
+            send_sem=send_sem.at[peer],
+            recv_sem=recv_sem.at[me],
+            device_id=(band, peer),
+            device_id_type=MESH,
+        )
+        copy.start()
+        sends.append(copy)
+    o_ref[me] = x_ref[me]
+    for k in range(1, n):
+        source = lax.rem(me + n - k, n)
+        pltpu.make_async_remote_copy(
+            src_ref=x_ref.at[source],
+            dst_ref=o_ref.at[source],
+            send_sem=send_sem.at[source],
+            recv_sem=recv_sem.at[source],
+            device_id=(band, source),
+            device_id_type=MESH,
+        ).wait_recv()
+    for copy in sends:
+        copy.wait_send()
+
+
+def exchange(blocks, collective):
+    n = blocks.shape[0]
+    return pl.pallas_call(
+        functools.partial(exchange_kernel, n),
+        out_shape=jax.ShapeDtypeStruct(blocks.shape, blocks.dtype),
+        in_specs=[pl.BlockSpec(memory_space=pltpu.VMEM)],
+        out_specs=pl.BlockSpec(memory_space=pltpu.VMEM),
+        scratch_shapes=[pltpu.SemaphoreType.DMA((n,)), pltpu.SemaphoreType.DMA((n,))],
+        compiler_params=pltpu.CompilerParams(collective_id=collective, has_side_effects=True),
+    )(blocks)
+
+
 def spectral(flat_winds, row_cosine, lon_total):
     flat_rows, columns = flat_winds.shape
     lon_count = lax.axis_size("lon")
     lon_index = lax.axis_index("lon")
     row_share = flat_rows // lon_count
-    full_rows = lax.all_to_all(flat_winds, "lon", split_axis=0, concat_axis=1, tiled=True)
+    gathered = exchange(flat_winds.reshape(lon_count, row_share, columns), 0)
     own_cosine = lax.dynamic_slice_in_dim(row_cosine, lon_index * row_share, row_share, 0)
-    lon_grid = full_rows.reshape(row_share, lon_count, columns)
     block_ids = jnp.arange(lon_count, dtype=jnp.int32)
     phase_angle = (
         2.0
@@ -111,16 +163,14 @@
     )
     phase_cos = jnp.cos(phase_angle)
     phase_sin = jnp.sin(phase_angle)
-    real_part = jnp.einsum("rpm,pk->rkm", lon_grid, phase_cos, precision=EXACT_MODE)
-    imag_part = -jnp.einsum("rpm,pk->rkm", lon_grid, phase_sin, precision=EXACT_MODE)
+    real_part = jnp.einsum("prm,pk->rkm", gathered, phase_cos, precision=EXACT_MODE)
+    imag_part = -jnp.einsum("prm,pk->rkm", gathered, phase_sin, precision=EXACT_MODE)
     out_re, out_im = filter_modes(real_part, imag_part, block_ids, own_cosine, lon_total)
     restored = (
-        jnp.einsum("rkm,kp->rpm", out_re, phase_cos, precision=EXACT_MODE)
-        - jnp.einsum("rkm,kp->rpm", out_im, phase_sin, precision=EXACT_MODE)
+        jnp.einsum("rkm,kp->prm", out_re, phase_cos, precision=EXACT_MODE)
+        - jnp.einsum("rkm,kp->prm", out_im, phase_sin, precision=EXACT_MODE)
     ) / lon_total
-    return lax.all_to_all(
-        restored.reshape(row_share, lon_total), "lon", split_axis=1, concat_axis=0, tiled=True
-    )
+    return exchange(restored, 1).reshape(flat_rows, columns)
 
 
 def local(tracers, wind_field):

time: 70.9 us -> 73 us (1.030)
  the two profiles are of different devices: /device:TPU:33 before, /device:TPU:30 now
where the time goes in v1:
time: 73 us; the launch traced here: 72.6 us
  Pallas kernels  29.6 us (41%)
  matrix products  11.3 us (15%)
  local copies, waits for them, and re-layouts  10.9 us (15%)
  other arithmetic  9.05 us (12%)
  starting transfers between devices  8.1 us (11%)
  waiting for transfers between devices  2.77 us (4%)
  between operations  0.97 us (1%)
    pallas_call x2, Pallas kernels, exchange(): pl.pallas_call(functools.partial(exchange_kernel, n), out_shape=jax.Shape...  29.6 us
    dot_general x8, matrix products, apply_table(): return jnp.einsum('rkm,mb->rkb', values, table, precision=EXACT_MODE)  8.2 us
    ppermute x2, starting transfers between devices, extended(): before = lax.ppermute(last, axis, up)  4.6 us
    ppermute x2, starting transfers between devices, extended(): after = lax.ppermute(first, axis, down)  3.5 us
    unnamed x11, local copies, waits for them, and re-layouts  3.46 us
    add x2, other arithmetic, upwind(): return jnp.maximum(speed, 0.0) * left + jnp.minimum(speed, 0.0) * right  2.9 us
    ppermute x2, waiting for transfers between devices, extended(): after = lax.ppermute(first, axis, down)  2.77 us
    concatenate x2, other arithmetic, extended(): array = jnp.concatenate([before, array, after], axis=dim)  2.69 us
  transfers between devices with their start and end apart: 4, of which 1 were waited for; matrix products, arithmetic and copies ran while one was open for 12% of the time, Pallas kernels for 0%

profile of v1, /device:TPU:30, one launch (start us, length us, event | category | flops | bytes accessed | tf_op | source)
XLA Modules:
  0.0 72.6 jit_solution(12684919924391977912)
XLA Ops:
  0.8 17.5 %shard_map.41 = f32[16,8,180]{2,1,0:T(8,128)} custom-call(f32[16,8,180]{2,1,0:T(8,128)} %bitcast.79), custom_call_target="tpu_custom_call" | custom-call | tf_op jit(solution)/shard_map/pallas_call | solution.py:140
  18.4 1.2 %convolution_negate_fusion = f32[16,8,180]{2,0,1:T(8,128)S(1)} fusion(f32[16,8,180]{2,1,0:T(8,128)} %shard_map.41), kind=kOutput, calls=%fused_computation.41 | convolution fusion | flops 4450304 | bytes 184320 | tf_op jit(solution)/shard_map/prm,pk->rkm/dot_general | solution.py:167
  19.6 1.2 %fusion.74 = f32[16,8,180]{2,0,1:T(8,128)S(1)} fusion(f32[16,8,180]{2,1,0:T(8,128)} %shard_map.41), kind=kOutput, calls=%fused_computation.90 | convolution fusion | flops 4427264 | bytes 184320 | tf_op jit(solution)/shard_map/prm,pk->rkm/dot_general | solution.py:166
  20.8 1.0 %fusion.40 = f32[8,16,180]{2,1,0:T(8,128)S(1)} fusion(f32[16,8,180]{2,0,1:T(8,128)S(1)} %fusion.74, f32[16,8,180]{2,0,1:T(8,128)S(1)} %convolution_negate_fusion, f32[16,180]{1,0:T(8,128)S(1)} %get-tuple-element.18, f32[16,180]{1,0:T(8,128)S(1)} %get-tuple-element.19), kind=kOutput, calls=%fused_computation.59 | convolution fusion | flops 50127120 | bytes 299520 | tf_op jit(solution)/shard_map/rkm,mb->rkb/dot_general | solution.py:66
  21.9 1.0 %fusion.44 = f32[8,16,180]{2,1,0:T(8,128)S(1)} fusion(f32[16,8,180]{2,0,1:T(8,128)S(1)} %convolution_negate_fusion, f32[16,8,180]{2,0,1:T(8,128)S(1)} %fusion.74, f32[16,180]{1,0:T(8,128)S(1)} %get-tuple-element.18, f32[16,180]{1,0:T(8,128)S(1)} %get-tuple-element.19), kind=kOutput, calls=%fused_computation.63 | convolution fusion | flops 50127120 | bytes 299520 | tf_op jit(solution)/shard_map/rkm,mb->rkb/dot_general | solution.py:66
  23.1 1.0 %fusion.29 = f32[8,16,180]{2,1,0:T(8,128)S(1)} fusion(f32[8,16,180]{2,1,0:T(8,128)S(1)} %fusion.40, f32[16,180]{1,0:T(8,128)S(1)} %multiply_select_fusion, f32[8]{0:T(128)S(1)} %multiply_multiply_fusion, pred[16,180]{1,0:T(8,128)(4,1)S(1)} %fusion.108, f32[16,8,180]{2,0,1:T(8,128)S(1)} %convolution_negate_fusion, f32[16,8,180]{2,0,1:T(8,128)S(1)} %fusion.74, ...), kind=kOutput, calls=%fused_computation.45 | convolution fusion | flops 50242320 | bytes 406112 | tf_op jit(solution)/shard_map/rkm,mb->rkb/dot_general | solution.py:66
  24.1 1.0 %fusion.38 = f32[8,16,180]{2,1,0:T(8,128)S(1)} fusion(f32[8,16,180]{2,1,0:T(8,128)S(1)} %fusion.29), kind=kOutput, calls=%fused_computation.57 | convolution fusion | flops 50058000 | bytes 184320 | tf_op jit(solution)/shard_map/rkm,mb->rkb/dot_general | solution.py:66
  25.2 1.0 %fusion.30 = f32[8,16,180]{2,1,0:T(8,128)S(1)} fusion(f32[8,16,180]{2,1,0:T(8,128)S(1)} %fusion.44, f32[16,180]{1,0:T(8,128)S(1)} %multiply_select_fusion, f32[8]{0:T(128)S(1)} %multiply_multiply_fusion, pred[16,180]{1,0:T(8,128)(4,1)S(1)} %fusion.108, f32[16,8,180]{2,0,1:T(8,128)S(1)} %fusion.74, f32[16,8,180]{2,0,1:T(8,128)S(1)} %convolution_negate_fusion, ...), kind=kOutput, calls=%fused_computation.47 | convolution fusion | flops 50242320 | bytes 406112 | tf_op jit(solution)/shard_map/rkm,mb->rkb/dot_general | solution.py:66
  26.2 1.0 %fusion.42 = f32[8,16,180]{2,1,0:T(8,128)S(1)} fusion(f32[8,16,180]{2,1,0:T(8,128)S(1)} %fusion.30), kind=kOutput, calls=%fused_computation.61 | convolution fusion | flops 50058000 | bytes 184320 | tf_op jit(solution)/shard_map/rkm,mb->rkb/dot_general | solution.py:66
  27.3 1.0 %convolution_add_fusion = f32[8,16,180]{2,1,0:T(8,128)S(1)} fusion(f32[8,16,180]{2,1,0:T(8,128)S(1)} %fusion.38, f32[8,16,180]{2,1,0:T(8,128)S(1)} %fusion.30), kind=kOutput, calls=%fused_computation.42 | convolution fusion | flops 50081040 | bytes 276480 | tf_op jit(solution)/shard_map/rkm,mb->rkb/dot_general | solution.py:66
  28.3 1.0 %convolution_subtract_fusion = f32[8,16,180]{2,1,0:T(8,128)S(1)} fusion(f32[8,16,180]{2,1,0:T(8,128)S(1)} %fusion.42, f32[8,16,180]{2,1,0:T(8,128)S(1)} %fusion.29), kind=kOutput, calls=%fused_computation.43 | convolution fusion | flops 50081040 | bytes 276480 | tf_op jit(solution)/shard_map/rkm,mb->rkb/dot_general | solution.py:66
  30.0 0.8 %fusion.64.x_ref = f32[16,8,180]{2,1,0:T(8,128)} fusion(f32[16,8,180]{2,0,1:T(8,128)S(1)} %fusion.65, f32[16,8,180]{2,0,1:T(8,128)S(1)} %fusion.69), kind=kLoop, calls=%fused_computation.78 | loop fusion | flops 46080 | bytes 276480 | tf_op jit(solution)/shard_map/div | solution.py:169
  30.8 12.0 %shard_map.42 = f32[16,8,180]{2,1,0:T(8,128)} custom-call(f32[16,8,180]{2,1,0:T(8,128)} %fusion.64.x_ref), custom_call_target="tpu_custom_call" | custom-call | tf_op jit(solution)/shard_map/pallas_call | solution.py:140
  42.8 0.9 %fusion.173 = (f32[8,8,180]{2,1,0:T(8,128)S(1)}, f32[8,8,180]{2,1,0:T(8,128)S(1)}) fusion(f32[16,8,180]{2,1,0:T(8,128)} %shard_map.42), kind=kLoop, calls=%fused_computation.195 | loop fusion | bytes 184320 | tf_op jit(solution)/shard_map/slice | solution.py:191
  43.7 0.9 %copy.34 = f32[2,180,768]{1,2,0:T(8,128)S(1)} copy(f32[2,180,768]{2,0,1:T(2,128)S(1)} %copy-done.3) | data formatting | bytes 2211840 | tf_op args[0]
  45.2 1.6 %collective-permute-start.1 = (f32[2,3,800]{2,0,1:T(2,128)S(1)}, f32[2,3,800]{2,0,1:T(2,128)S(1)}, u32[]{:S(2)}, u32[]{:S(2)}) collective-permute-start(f32[2,3,800]{2,0,1:T(2,128)S(1)} %copy.28), channel_id=1, source_target_pairs={{1,0},{2,1},{3,2},{4,3},{5,4},{6,5},{7,6},{8,7},{9,8},{10,9},{11,1... | collective-permute-start | bytes 57608 | tf_op jit(solution)/shard_map/ppermute | solution.py:26
  47.4 1.3 %copy.31 = f32[2,180,32,25]{1,0,3,2:T(2,128)S(1)} copy(f32[2,180,32,25]{1,3,2,0:T(8,128)S(1)} %pad_maximum_fusion) | data formatting | bytes 2304000 | tf_op jit(solution)/shard_map/concatenate | solution.py:201
  48.7 0.8 %fusion.172 = (f32[2,180,75]{1,0,2:T(2,128)}, f32[2,180,75]{1,0,2:T(2,128)S(1)}) fusion(f32[2,180,800]{1,0,2:T(2,128)S(1)} %bitcast.69), kind=kLoop, calls=%fused_computation.194 | loop fusion | bytes 432000 | tf_op jit(solution)/shard_map/slice | solution.py:23
  49.4 4.6 %collective-permute-start.2 = (f32[2,180,75]{1,0,2:T(2,128)}, f32[2,180,75]{1,0,2:T(2,128)}, u32[]{:S(2)}, u32[]{:S(2)}) collective-permute-start(f32[2,180,75]{1,0,2:T(2,128)} %get-tuple-element.12), channel_id=1, source_target_pairs={{0,16},{16,32},{32,48},{48,64},{64,80},{80,96},{96,112},{112,128},... | collective-permute-start | bytes 324008 | tf_op jit(solution)/shard_map/ppermute | solution.py:25
  54.0 1.9 %collective-permute-start.3 = (f32[2,180,75]{1,0,2:T(2,128)S(1)}, f32[2,180,75]{1,0,2:T(2,128)}, u32[]{:S(2)}, u32[]{:S(2)}) collective-permute-start(f32[2,180,75]{1,0,2:T(2,128)S(1)} %get-tuple-element.13), channel_id=1, source_target_pairs={{16,0},{32,16},{48,32},{64,48},{80,64},{96,80},{112,96},{128,112},... | collective-permute-start | bytes 324008 | tf_op jit(solution)/shard_map/ppermute | solution.py:26
  56.2 1.2 %copy.27 = f32[2,3,800]{1,2,0:T(8,128)} copy(f32[2,3,800]{2,0,1:T(2,128)S(1)} %collective-permute-done) | data formatting | bytes 38400 | tf_op jit(solution)/shard_map/ppermute | solution.py:25
  57.4 1.2 %copy.29 = f32[2,3,800]{1,2,0:T(8,128)} copy(f32[2,3,800]{2,0,1:T(2,128)S(1)} %collective-permute-done.1) | data formatting | bytes 38400 | tf_op jit(solution)/shard_map/ppermute | solution.py:26
  58.6 1.0 %broadcast_maximum_fusion.1 = (f32[2,181,32]{1,2,0:T(8,128)S(1)}, f32[2,181,32]{1,2,0:T(8,128)S(1)}) fusion(f32[2,3,800]{1,2,0:T(8,128)} %copy.29, f32[2,180,32]{1,2,0:T(8,128)S(1)} %bitcast.75, f32[2,180,768]{1,2,0:T(8,128)S(1)} %copy.34, f32[2,3,800]{1,2,0:T(8,128)} %copy.27), kind=kLoop, calls=%fused_computation.120 | loop fusion | flops 81088 | bytes 1283072 | tf_op jit(solution)/shard_map/max | solution.py:62
  60.1 0.7 maximum_maximum_fusion
  60.8 1.7 %fusion.22 = f32[2,181,768]{1,2,0:T(8,128)S(1)} fusion(f32[2,183,800]{1,2,0:T(8,128)S(1)} %get-tuple-element.9, f32[2,183,800]{1,2,0:T(8,128)S(1)} %get-tuple-element.8, f32[2,181,32]{1,2,0:T(8,128)S(1)} %broadcast_minimum_fusion.1, f32[2,181,32]{1,2,0:T(8,128)S(1)} %get-tuple-element.6), kind=kLoop, calls=%fused_computation.33 | loop fusion | flops 6394368 | bytes 7877120 | tf_op jit(solution)/shard_map/add | solution.py:62
  62.5 2.8 %collective-permute-done.3 = f32[2,180,75]{1,0,2:T(2,128)} collective-permute-done((f32[2,180,75]{1,0,2:T(2,128)S(1)}, f32[2,180,75]{1,0,2:T(2,128)}, u32[]{:S(2)}, u32[]{:S(2)}) %collective-permute-start.3) | collective-permute-done | bytes 108032 | tf_op jit(solution)/shard_map/ppermute | solution.py:26
  65.3 2.0 %pad_maximum_fusion.1 = f32[2,180,950]{1,0,2:T(2,128)S(1)} fusion(f32[2,180,75]{1,0,2:T(2,128)} %collective-permute-done.3, f32[2,180,800]{1,0,2:T(2,128)S(1)} %bitcast.70, f32[2,180,75]{1,0,2:T(2,128)} %collective-permute-done.2), kind=kLoop, calls=%fused_computation.1 | loop fusion | flops 684000 | bytes 2736000 | tf_op jit(solution)/shard_map/concatenate | solution.py:27
  67.3 1.0 %slice.155 = f32[2,180,38,24]{1,0,3,2:T(2,128)S(1)} slice(f32[2,180,38,25]{1,0,3,2:T(2,128)S(1)} %bitcast.72), slice={[0:2], [0:180], [0:38], [0:24]} | slice | bytes 2626560 | tf_op jit(solution)/shard_map/slice | solution.py:208
  68.6 1.2 %fusion.6 = f32[2,180,792]{1,2,0:T(8,128)S(1)} fusion(f32[2,180,912]{1,2,0:T(8,128)S(1)} %bitcast.67, f32[2,180,33]{1,2,0:T(8,128)S(1)} %get-tuple-element.17, f32[2,180,33]{1,2,0:T(8,128)S(1)} %get-tuple-element.16), kind=kLoop, calls=%fused_computation.13 | loop fusion | flops 6557760 | bytes 8078400 | tf_op jit(solution)/shard_map/add | solution.py:62
  69.8 0.7 fusion.15
  70.5 1.5 %copy.35 = f32[2,180,768]{2,0,1:T(2,128)} copy(f32[2,180,768]{1,2,0:T(8,128)S(1)} %fusion.15) | data formatting | bytes 2211840
  72.0 0.7 copy.47
  (35 shorter events, 3.1 us)
Async XLA Ops:
  26.2 17.5 %copy-start.3 = (f32[2,180,768]{2,0,1:T(2,128)S(1)}, f32[2,180,768]{2,0,1:T(2,128)}, u32[]{:S(2)}) copy-start(f32[2,180,768]{2,0,1:T(2,128)} %param.2) | copy-start | bytes 3317764
  45.2 12.2 %collective-permute-start.1 = (f32[2,3,800]{2,0,1:T(2,128)S(1)}, f32[2,3,800]{2,0,1:T(2,128)S(1)}, u32[]{:S(2)}, u32[]{:S(2)}) collective-permute-start(f32[2,3,800]{2,0,1:T(2,128)S(1)} %copy.28), channel_id=1, source_target_pairs={{1,0},{2,1},{3,2},{4,3},{5,4},{6,5},{7,6},{8,7},{9,8},{10,9},{11,1... | collective-permute-start | bytes 57608 | tf_op jit(solution)/shard_map/ppermute | solution.py:26
  47.1 9.1 %collective-permute-start = (f32[2,3,800]{2,0,1:T(2,128)S(1)}, f32[2,3,800]{2,0,1:T(2,128)S(1)}, u32[]{:S(2)}, u32[]{:S(2)}) collective-permute-start(f32[2,3,800]{2,0,1:T(2,128)S(1)} %copy.26), channel_id=1, source_target_pairs={{0,1},{1,2},{2,3},{3,4},{4,5},{5,6},{6,7},{7,8},{8,9},{9,10},{10,1... | collective-permute-start | bytes 57608 | tf_op jit(solution)/shard_map/ppermute | solution.py:25
  49.4 13.1 %collective-permute-start.2 = (f32[2,180,75]{1,0,2:T(2,128)}, f32[2,180,75]{1,0,2:T(2,128)}, u32[]{:S(2)}, u32[]{:S(2)}) collective-permute-start(f32[2,180,75]{1,0,2:T(2,128)} %get-tuple-element.12), channel_id=1, source_target_pairs={{0,16},{16,32},{32,48},{48,64},{64,80},{80,96},{96,112},{112,128},... | collective-permute-start | bytes 324008 | tf_op jit(solution)/shard_map/ppermute | solution.py:25
  54.0 11.2 %collective-permute-start.3 = (f32[2,180,75]{1,0,2:T(2,128)S(1)}, f32[2,180,75]{1,0,2:T(2,128)}, u32[]{:S(2)}, u32[]{:S(2)}) collective-permute-start(f32[2,180,75]{1,0,2:T(2,128)S(1)} %get-tuple-element.13), channel_id=1, source_target_pairs={{16,0},{32,16},{48,32},{64,48},{80,64},{96,80},{112,96},{128,112},... | collective-permute-start | bytes 324008 | tf_op jit(solution)/shard_map/ppermute | solution.py:26
  58.6 1.2 %copy-start = (f32[2,3,800]{1,2,0:T(8,128)S(1)}, f32[2,3,800]{1,2,0:T(8,128)}, u32[]{:S(2)}) copy-start(f32[2,3,800]{1,2,0:T(8,128)} %copy.27) | copy-start | bytes 57604
  58.6 1.4 %copy-start.1 = (f32[2,3,800]{1,2,0:T(8,128)S(1)}, f32[2,3,800]{1,2,0:T(8,128)}, u32[]{:S(2)}) copy-start(f32[2,3,800]{1,2,0:T(8,128)} %copy.29) | copy-start | bytes 57604
  70.5 1.5 %copy-start.2 = (f32[16,8,180]{2,1,0:T(8,128)S(1)}, f32[16,8,180]{2,1,0:T(8,128)}, u32[]{:S(2)}) copy-start(f32[16,8,180]{2,1,0:T(8,128)} %shard_map.42) | copy-start | bytes 276484

commit v2 on v1

--- a/solution.py
+++ b/solution.py
@@ -173,6 +173,43 @@
     return exchange(restored, 1).reshape(flat_rows, columns)
 
 
+def halo(array, axis, dim, width, wrap):
+    devices, length = (lax.axis_size(axis), array.shape[dim])
+    up = [(i, (i + 1) % devices) for i in range(devices if wrap else devices - 1)]
+    down = [(j, i) for i, j in up]
+    before = lax.ppermute(lax.slice_in_dim(array, length - width, length, axis=dim), axis, up)
+    after = lax.ppermute(lax.slice_in_dim(array, 0, width, axis=dim), axis, down)
+    return before, after
+
+
+def stencil(padded, dim, faces, stride):
+
+    def offset_cells(offset):
+        return lax.slice_in_dim(padded, offset * stride, (offset + faces) * stride, axis=dim)
+
+    left = (
+        2.0 * offset_cells(0)
+        - 13.0 * offset_cells(1)
+        + 47.0 * offset_cells(2)
+        + 27.0 * offset_cells(3)
+        - 3.0 * offset_cells(4)
+    ) / 60.0
+    right = (
+        2.0 * offset_cells(5)
+        - 13.0 * offset_cells(4)
+        + 47.0 * offset_cells(3)
+        + 27.0 * offset_cells(2)
+        - 3.0 * offset_cells(1)
+    ) / 60.0
+    return left, right
+
+
+def spread(values, rows, tracer_count):
+    lanes = jnp.arange(rows * tracer_count, dtype=jnp.int32) // tracer_count
+    pick = (jnp.arange(rows, dtype=jnp.int32)[:, None] == lanes[None, :]).astype(jnp.float32)
+    return jnp.einsum("ljc,jm->lcm", values, pick, precision=EXACT_MODE)
+
+
 def local(tracers, wind_field):
     levels, lon_cols, merged = tracers.shape
     lat_rows = wind_field.shape[2]
@@ -180,6 +217,8 @@
     lon_total = lon_cols * lax.axis_size("lon")
     lat_total = lat_rows * lax.axis_size("lat")
     first_row = lax.axis_index("lat") * lat_rows
+    west, east = halo(tracers, "lon", 1, 3, True)
+    south, north = halo(tracers, "lat", 2, 3 * tracer_count, False)
     row_ids = first_row + jnp.arange(lat_rows, dtype=jnp.int32)
     row_cosine = jnp.cos(
         (row_ids.astype(jnp.float32) + 0.5) * (math.pi / lat_total) - 0.5 * math.pi
@@ -188,37 +227,24 @@
     flat_cosine = jnp.tile(row_cosine, 2 * levels)
     smoothed = spectral(flat_winds, flat_cosine, lon_total)
     smoothed = smoothed.reshape(2, levels, lat_rows, lon_cols)
-    east_turned = jnp.transpose(smoothed[0], (0, 2, 1))
-    north_turned = jnp.transpose(smoothed[1], (0, 2, 1))
-    zonal_stack = jnp.concatenate([tracers, east_turned], axis=2)
-    zonal_pad = extended(zonal_stack, (("lon", 1),), 3, True)
-    east_wind = zonal_pad[:, :, merged:]
-    zonal_speed = 0.5 * (east_wind[:, 2 : lon_cols + 3] + east_wind[:, 3 : lon_cols + 4])
-    zonal_speed = jnp.repeat(zonal_speed, tracer_count, axis=2)
-    left_x, right_x = face_values(zonal_pad[:, :, :merged], 1, lon_cols, 1)
-    zonal_flux = upwind(zonal_speed, left_x, right_x)
-    slot_count = tracer_count + 1
-    merid_stack = jnp.concatenate(
-        [tracers.reshape(levels, lon_cols, lat_rows, tracer_count), north_turned[..., None]], axis=3
-    )
-    merid_stack = merid_stack.reshape(levels, lon_cols, lat_rows * slot_count)
-    merid_pad = extended(merid_stack, (("lat", 2),), 3 * slot_count, False)
-    merid_pad = merid_pad.reshape(levels, lon_cols, lat_rows + 6, slot_count)
-    north_wind = merid_pad[..., tracer_count]
-    tracer_pad = merid_pad[..., :tracer_count].reshape(
-        levels, lon_cols, (lat_rows + 6) * tracer_count
-    )
+    east_wind, north_wind = smoothed[0], smoothed[1]
+    u_west, u_east = halo(east_wind, "lon", 2, 1, True)
+    v_south, v_north = halo(north_wind, "lat", 1, 1, False)
+    u_pad = jnp.concatenate([u_west, east_wind, u_east], axis=2)
+    zonal_speed = 0.5 * (u_pad[:, :, : lon_cols + 1] + u_pad[:, :, 1:])
+    v_pad = jnp.concatenate([v_south, north_wind, v_north], axis=1)
     face_ids = first_row + jnp.arange(lat_rows + 1, dtype=jnp.int32)
     face_cosine = jnp.cos(face_ids.astype(jnp.float32) * (math.pi / lat_total) - 0.5 * math.pi)
     face_cosine = jnp.where((face_ids == 0) | (face_ids == lat_total), 0.0, face_cosine)
-    merid_speed = (
-        0.5
-        * (north_wind[:, :, 2 : lat_rows + 3] + north_wind[:, :, 3 : lat_rows + 4])
-        * face_cosine[None, None, :]
-    )
-    merid_speed = jnp.repeat(merid_speed, tracer_count, axis=2)
-    left_y, right_y = face_values(tracer_pad, 2, lat_rows, tracer_count)
-    merid_flux = upwind(merid_speed, left_y, right_y)
+    merid_speed = 0.5 * (v_pad[:, : lat_rows + 1] + v_pad[:, 1:]) * face_cosine[None, :, None]
+    zonal_rep = spread(zonal_speed, lat_rows, tracer_count)
+    merid_rep = spread(merid_speed, lat_rows + 1, tracer_count)
+    zonal_pad = jnp.concatenate([west, tracers, east], axis=1)
+    left_x, right_x = stencil(zonal_pad, 1, lon_cols + 1, 1)
+    zonal_flux = upwind(zonal_rep, left_x, right_x)
+    merid_pad = jnp.concatenate([south, tracers, north], axis=2)
+    left_y, right_y = stencil(merid_pad, 2, lat_rows + 1, tracer_count)
+    merid_flux = upwind(merid_rep, left_y, right_y)
     metric = jnp.repeat(1.0 / jnp.maximum(row_cosine, COS_FLOOR), tracer_count)
     change = COURANT * (zonal_flux[:, 1:] - zonal_flux[:, :-1]) + COURANT * (
         merid_flux[:, :, tracer_count:] - merid_flux[:, :, :-tracer_count]

time: 73 us -> 81.5 us (1.12)
  starting transfers between devices: 8.1 us -> 27.1 us
  other arithmetic: 9.05 us -> 1.62 us
  Pallas kernels: 29.6 us -> 22.8 us
  matrix products: 11.3 us -> 17.6 us
  local copies, waits for them, and re-layouts: 10.9 us -> 4.96 us
  waiting for transfers between devices: 2.77 us -> 6.08 us
    ppermute x4 -> x8, starting transfers between devices: 8.1 us -> 27.1 us  [the longest x4 15.1 us: halo(): lax.ppermute(lax.slice_in_dim(array, 0, width, axis=dim), axis, down)]
    pallas_call x2, Pallas kernels: 29.6 us -> 22.8 us  [exchange(): pl.pallas_call(functools.partial(exchange_kernel, n), out_shape=jax.Shape...]
    dot_general x0 -> x2, matrix products: none -> 4.16 us  [spread(): return jnp.einsum('ljc,jm->lcm', values, pick, precision=EXACT_MODE)]
    ppermute x4 -> x8, waiting for transfers between devices: 2.77 us -> 6.08 us  [the longest x4 4.73 us: halo(): lax.ppermute(lax.slice_in_dim(array, 0, width, axis=dim), axis, down)]
    concatenate x4 -> x0, other arithmetic: 3.2 us -> none  [the longest x2 2.69 us: extended(): array = jnp.concatenate([before, array, after], axis=dim)]
    add x2 -> x0, other arithmetic: 2.9 us -> none  [upwind(): return jnp.maximum(speed, 0.0) * left + jnp.minimum(speed, 0.0) * right]
    ppermute x2 -> x0, local copies, waits for them, and re-layouts: 2.42 us -> none  [the longest x1 1.22 us: extended(): after = lax.ppermute(first, axis, down)]
    slice x8 -> x5, local copies, waits for them, and re-layouts: 3.44 us -> 1.08 us  [the longest x1 0.88 us: local(): east_wind, north_wind = (smoothed[0], smoothed[1])]
  transfers between devices with their start and end apart: 4 -> 8, of which waited for: 1 -> 2; matrix products, arithmetic and copies ran while one was open for 12% -> 22% of each run, Pallas kernels for 0% -> 28%
where the time goes in v2:
time: 81.5 us; the launch traced here: 81.1 us
  starting transfers between devices  27.1 us (33%)
  Pallas kernels  22.8 us (28%)
  matrix products  17.6 us (22%)
  waiting for transfers between devices  6.08 us (7%)
  local copies, waits for them, and re-layouts  4.96 us (6%)
  other arithmetic  1.62 us (2%)
  between operations  0.94 us (1%)
    pallas_call x2, Pallas kernels, exchange(): pl.pallas_call(functools.partial(exchange_kernel, n), out_shape=jax.Shape...  22.8 us
    ppermute x4, starting transfers between devices, halo(): lax.ppermute(lax.slice_in_dim(array, 0, width, axis=dim), axis, down)  15.1 us
    ppermute x4, starting transfers between devices, halo(): lax.ppermute(lax.slice_in_dim(array, length - width, length, axis=dim), a...  12 us
    dot_general x8, matrix products, apply_table(): return jnp.einsum('rkm,mb->rkb', values, table, precision=EXACT_MODE)  10.4 us
    ppermute x4, waiting for transfers between devices, halo(): lax.ppermute(lax.slice_in_dim(array, 0, width, axis=dim), axis, down)  4.73 us
    dot_general x2, matrix products, spread(): return jnp.einsum('ljc,jm->lcm', values, pick, precision=EXACT_MODE)  4.16 us
    unnamed x9, local copies, waits for them, and re-layouts  3.62 us
  transfers between devices with their start and end apart: 8, of which 2 were waited for; matrix products, arithmetic and copies ran while one was open for 22% of the time, Pallas kernels for 28%

profile of v2, /device:TPU:30, one launch (start us, length us, event | category | flops | bytes accessed | tf_op | source)
XLA Modules:
  0.0 81.1 jit_solution(14616292684562649592)
XLA Ops:
  0.6 1.4 %constant_dynamic-update-slice_fusion.1 = (f32[2,180,840]{2,1,0:T(8,128)S(1)}, f32[2,180,768]{2,1,0:T(8,128)S(1)}) fusion(f32[2,180,768]{2,0,1:T(2,128)} %param.2), kind=kLoop, calls=%fused_computation.175 | loop fusion | bytes 3366912
  2.0 0.1 fusion.209
  2.1 4.6 %collective-permute-start.6 = (f32[2,180,72]{2,1,0:T(8,128)S(1)}, f32[2,180,72]{2,1,0:T(8,128)S(1)}, u32[]{:S(2)}, u32[]{:S(2)}) collective-permute-start(f32[2,180,72]{2,1,0:T(8,128)S(1)} %get-tuple-element.9), channel_id=1, source_target_pairs={{0,16},{16,32},{32,48},{48,64},{64,80},{80,96},{96,112},{112,128},... | collective-permute-start | bytes 311048 | tf_op jit(solution)/shard_map/ppermute | solution.py:180
  6.8 8.2 %collective-permute-start.3 = (f32[2,3,768]{2,1,0:T(4,128)S(1)}, f32[2,3,768]{2,1,0:T(4,128)S(1)}, u32[]{:S(2)}, u32[]{:S(2)}) collective-permute-start(f32[2,3,768]{2,1,0:T(4,128)S(1)} %get-tuple-element.6), channel_id=1, source_target_pairs={{1,0},{2,1},{3,2},{4,3},{5,4},{6,5},{7,6},{8,7},{9,8},{10,9},{11,1... | collective-permute-start | bytes 55304 | tf_op jit(solution)/shard_map/ppermute | solution.py:181
  15.0 11.2 %shard_map.41 = f32[16,8,180]{2,1,0:T(8,128)} custom-call(f32[16,8,180]{2,1,0:T(8,128)} %bitcast.55), custom_call_target="tpu_custom_call" | custom-call | tf_op jit(solution)/shard_map/pallas_call | solution.py:140
  26.3 1.2 %convolution_negate_fusion = f32[16,8,180]{2,0,1:T(8,128)S(1)} fusion(f32[16,8,180]{2,1,0:T(8,128)} %shard_map.41), kind=kOutput, calls=%fused_computation.26 | convolution fusion | flops 4450304 | bytes 184320 | tf_op jit(solution)/shard_map/prm,pk->rkm/dot_general | solution.py:167
  27.5 1.2 %fusion.84 = f32[16,8,180]{2,0,1:T(8,128)S(1)} fusion(f32[16,8,180]{2,1,0:T(8,128)} %shard_map.41), kind=kOutput, calls=%fused_computation.101 | convolution fusion | flops 4427264 | bytes 184320 | tf_op jit(solution)/shard_map/prm,pk->rkm/dot_general | solution.py:166
  28.9 1.7 %fusion.52 = f32[8,16,180]{2,1,0:T(8,128)} fusion(f32[16,8,180]{2,0,1:T(8,128)S(1)} %convolution_negate_fusion, f32[16,8,180]{2,0,1:T(8,128)S(1)} %fusion.84, f32[16,180]{1,0:T(8,128)S(1)} %get-tuple-element.18, f32[16,180]{1,0:T(8,128)S(1)} %get-tuple-element.19), kind=kOutput, calls=%fused_computation.72 | convolution fusion | flops 50127120 | bytes 299520 | tf_op jit(solution)/shard_map/rkm,mb->rkb/dot_general | solution.py:66
  30.6 1.7 %fusion.48 = f32[8,16,180]{2,1,0:T(8,128)} fusion(f32[16,8,180]{2,0,1:T(8,128)S(1)} %fusion.84, f32[16,8,180]{2,0,1:T(8,128)S(1)} %convolution_negate_fusion, f32[16,180]{1,0:T(8,128)S(1)} %get-tuple-element.18, f32[16,180]{1,0:T(8,128)S(1)} %get-tuple-element.19), kind=kOutput, calls=%fused_computation.68 | convolution fusion | flops 50127120 | bytes 299520 | tf_op jit(solution)/shard_map/rkm,mb->rkb/dot_general | solution.py:66
  32.5 1.9 %fusion.17 = f32[8,16,180]{2,1,0:T(8,128)S(1)} fusion(f32[8,16,180]{2,1,0:T(8,128)} %fusion.52, f32[16,180]{1,0:T(8,128)S(1)} %multiply_select_fusion, f32[8]{0:T(128)S(1)} %multiply_multiply_fusion, pred[16,180]{1,0:T(8,128)(4,1)S(1)} %fusion.136, f32[16,8,180]{2,0,1:T(8,128)S(1)} %fusion.84, f32[16,8,180]{2,0,1:T(8,128)S(1)} %convolution_negate_fusion, ...), kind=kOutput, calls=%fused_computation.32 | convolution fusion | flops 50242320 | bytes 406112 | tf_op jit(solution)/shard_map/rkm,mb->rkb/dot_general | solution.py:66
  34.4 1.0 %fusion.50 = f32[8,16,180]{2,1,0:T(8,128)S(1)} fusion(f32[8,16,180]{2,1,0:T(8,128)S(1)} %fusion.17), kind=kOutput, calls=%fused_computation.70 | convolution fusion | flops 50058000 | bytes 184320 | tf_op jit(solution)/shard_map/rkm,mb->rkb/dot_general | solution.py:66
  35.5 1.0 %fusion.16 = f32[8,16,180]{2,1,0:T(8,128)S(1)} fusion(f32[8,16,180]{2,1,0:T(8,128)S(1)} %copy-done.2, f32[16,180]{1,0:T(8,128)S(1)} %multiply_select_fusion, f32[8]{0:T(128)S(1)} %multiply_multiply_fusion, pred[16,180]{1,0:T(8,128)(4,1)S(1)} %fusion.136, f32[16,8,180]{2,0,1:T(8,128)S(1)} %convolution_negate_fusion, f32[16,8,180]{2,0,1:T(8,128)S(1)} %fusion.84, ...), kind=kOutput, calls=%fused_computation.30 | convolution fusion | flops 50242320 | bytes 406112 | tf_op jit(solution)/shard_map/rkm,mb->rkb/dot_general | solution.py:66
  36.5 1.0 %fusion.46 = f32[8,16,180]{2,1,0:T(8,128)S(1)} fusion(f32[8,16,180]{2,1,0:T(8,128)S(1)} %fusion.16), kind=kOutput, calls=%fused_computation.66 | convolution fusion | flops 50058000 | bytes 184320 | tf_op jit(solution)/shard_map/rkm,mb->rkb/dot_general | solution.py:66
  37.5 1.0 %convolution_subtract_fusion = f32[8,16,180]{2,1,0:T(8,128)S(1)} fusion(f32[8,16,180]{2,1,0:T(8,128)S(1)} %fusion.50, f32[8,16,180]{2,1,0:T(8,128)S(1)} %fusion.16), kind=kOutput, calls=%fused_computation.28 | convolution fusion | flops 50081040 | bytes 276480 | tf_op jit(solution)/shard_map/rkm,mb->rkb/dot_general | solution.py:66
  38.6 1.0 %convolution_add_fusion = f32[8,16,180]{2,1,0:T(8,128)S(1)} fusion(f32[8,16,180]{2,1,0:T(8,128)S(1)} %fusion.46, f32[8,16,180]{2,1,0:T(8,128)S(1)} %fusion.17), kind=kOutput, calls=%fused_computation.27 | convolution fusion | flops 50081040 | bytes 276480 | tf_op jit(solution)/shard_map/rkm,mb->rkb/dot_general | solution.py:66
  39.6 0.3 fusion.75
  39.9 0.3 fusion.79
  40.2 0.8 %fusion.74.x_ref = f32[16,8,180]{2,1,0:T(8,128)} fusion(f32[16,8,180]{2,0,1:T(8,128)S(1)} %fusion.75, f32[16,8,180]{2,0,1:T(8,128)S(1)} %fusion.79), kind=kLoop, calls=%fused_computation.89 | loop fusion | flops 46080 | bytes 276480 | tf_op jit(solution)/shard_map/div | solution.py:169
  41.0 11.6 %shard_map.42 = f32[16,8,180]{2,1,0:T(8,128)} custom-call(f32[16,8,180]{2,1,0:T(8,128)} %fusion.74.x_ref), custom_call_target="tpu_custom_call" | custom-call | tf_op jit(solution)/shard_map/pallas_call | solution.py:140
  52.7 0.9 %fusion.210 = (f32[8,8,180]{2,1,0:T(8,128)S(1)}, f32[8,8,180]{2,1,0:T(8,128)S(1)}) fusion(f32[16,8,180]{2,1,0:T(8,128)} %shard_map.42), kind=kLoop, calls=%fused_computation.237 | loop fusion | bytes 184320 | tf_op jit(solution)/shard_map/slice | solution.py:230
  53.6 0.1 collective-permute-start
  53.8 2.8 %collective-permute-start.1 = (f32[2,32,1]{2,1,0:T(8,128)S(1)}, f32[2,32,1]{2,1,0:T(8,128)S(1)}, u32[]{:S(2)}, u32[]{:S(2)}) collective-permute-start(f32[2,32,1]{2,1,0:T(8,128)S(1)} %get-tuple-element.14), channel_id=1, source_target_pairs={{1,0},{2,1},{3,2},{4,3},{5,4},{6,5},{7,6},{8,7},{9,8},{10,9},{11,1... | collective-permute-start | bytes 776 | tf_op jit(solution)/shard_map/ppermute | solution.py:181
  56.8 1.3 %collective-permute-done = f32[2,32,1]{2,1,0:T(8,128)S(1)} collective-permute-done((f32[2,32,1]{2,1,0:T(8,128)S(1)}, f32[2,32,1]{2,1,0:T(8,128)S(1)}, u32[]{:S(2)}, u32[]{:S(2)}) %collective-permute-start) | collective-permute-done | bytes 288 | tf_op jit(solution)/shard_map/ppermute | solution.py:180
  58.2 1.9 %collective-permute-start.7 = (f32[2,180,72]{2,1,0:T(8,128)S(1)}, f32[2,180,72]{2,1,0:T(8,128)S(1)}, u32[]{:S(2)}, u32[]{:S(2)}) collective-permute-start(f32[2,180,72]{2,1,0:T(8,128)S(1)} %get-tuple-element.8), channel_id=1, source_target_pairs={{16,0},{32,16},{48,32},{64,48},{80,64},{96,80},{112,96},{128,112},... | collective-permute-start | bytes 311048 | tf_op jit(solution)/shard_map/ppermute | solution.py:181
  60.1 7.2 %collective-permute-start.4 = (f32[2,1,180]{2,1,0:T(1,128)S(1)}, f32[2,1,180]{2,1,0:T(1,128)S(1)}, u32[]{:S(2)}, u32[]{:S(2)}) collective-permute-start(f32[2,1,180]{2,1,0:T(1,128)S(1)} %get-tuple-element.17), channel_id=1, source_target_pairs={{0,16},{16,32},{32,48},{48,64},{64,80},{80,96},{96,112},{112,128},... | collective-permute-start | bytes 4328 | tf_op jit(solution)/shard_map/ppermute | solution.py:180
  67.4 2.1 %collective-permute-start.5 = (f32[2,1,180]{2,1,0:T(1,128)S(1)}, f32[2,1,180]{2,1,0:T(1,128)S(1)}, u32[]{:S(2)}, u32[]{:S(2)}) collective-permute-start(f32[2,1,180]{2,1,0:T(1,128)S(1)} %get-tuple-element.16), channel_id=1, source_target_pairs={{16,0},{32,16},{48,32},{64,48},{80,64},{96,80},{112,96},{128,112},... | collective-permute-start | bytes 4328 | tf_op jit(solution)/shard_map/ppermute | solution.py:181
  69.5 1.9 %fusion.29 = f32[2,181,768]{2,1,0:T(8,128)S(1)} fusion(f32[2,3,768]{2,1,0:T(4,128)S(1)} %collective-permute-done.2, f32[2,3,768]{2,1,0:T(4,128)S(1)} %collective-permute-done.3, f32[2,180,768]{2,1,0:T(8,128)S(1)} %get-tuple-element.11, f32[2,32,180]{2,1,0:T(8,128)S(1)} %bitcast.54, f32[2,32,1]{2,1,0:T(8,128)S(1)} %collective-permute-done, ...), kind=kOutput, calls=%fused_computation.44 | convolution fusion | flops 115447552 | bytes 2304512 | tf_op jit(solution)/shard_map/ljc,jm->lcm/dot_general | solution.py:210
  71.5 4.7 %collective-permute-done.5 = f32[2,1,180]{2,1,0:T(1,128)S(1)} collective-permute-done((f32[2,1,180]{2,1,0:T(1,128)S(1)}, f32[2,1,180]{2,1,0:T(1,128)S(1)}, u32[]{:S(2)}, u32[]{:S(2)}) %collective-permute-start.5) | collective-permute-done | bytes 1472 | tf_op jit(solution)/shard_map/ppermute | solution.py:181
  76.2 2.3 %fusion.9 = f32[2,180,792]{2,1,0:T(8,128)S(1)} fusion(f32[2,180,768]{2,1,0:T(8,128)S(1)} %get-tuple-element.11, f32[2,180,72]{2,1,0:T(8,128)S(1)} %collective-permute-done.6, f32[2,180,840]{2,1,0:T(8,128)S(1)} %constant_dynamic-update-slice_fusion, f32[2,32,180]{2,1,0:T(8,128)S(1)} %bitcast.57, f32[2,1,180]{2,1,0:T(1,128)S(1)} %collective-permute-done.4, ...), kind=kOutput, calls=%fused_computation.17 | convolution fusion | flops 120964536 | bytes 5823780 | tf_op jit(solution)/shard_map/ljc,jm->lcm/dot_general | solution.py:210
  78.5 0.4 fusion.32
  78.9 1.6 %copy.31 = f32[2,180,768]{2,0,1:T(2,128)} copy(f32[2,180,768]{2,1,0:T(8,128)S(1)} %fusion.32) | data formatting | bytes 2211840
  80.5 0.7 copy.45
  (30 shorter events, 0.8 us)
Async XLA Ops:
  2.1 74.0 %collective-permute-start.6 = (f32[2,180,72]{2,1,0:T(8,128)S(1)}, f32[2,180,72]{2,1,0:T(8,128)S(1)}, u32[]{:S(2)}, u32[]{:S(2)}) collective-permute-start(f32[2,180,72]{2,1,0:T(8,128)S(1)} %get-tuple-element.9), channel_id=1, source_target_pairs={{0,16},{16,32},{32,48},{48,64},{64,80},{80,96},{96,112},{112,128},... | collective-permute-start | bytes 311048 | tf_op jit(solution)/shard_map/ppermute | solution.py:180
  6.8 60.6 %collective-permute-start.2 = (f32[2,3,768]{2,1,0:T(4,128)S(1)}, f32[2,3,768]{2,1,0:T(4,128)S(1)}, u32[]{:S(2)}, u32[]{:S(2)}) collective-permute-start(f32[2,3,768]{2,1,0:T(4,128)S(1)} %get-tuple-element.7), channel_id=1, source_target_pairs={{0,1},{1,2},{2,3},{3,4},{4,5},{5,6},{6,7},{7,8},{8,9},{9,10},{10,1... | collective-permute-start | bytes 55304 | tf_op jit(solution)/shard_map/ppermute | solution.py:180
  6.8 62.7 %collective-permute-start.3 = (f32[2,3,768]{2,1,0:T(4,128)S(1)}, f32[2,3,768]{2,1,0:T(4,128)S(1)}, u32[]{:S(2)}, u32[]{:S(2)}) collective-permute-start(f32[2,3,768]{2,1,0:T(4,128)S(1)} %get-tuple-element.6), channel_id=1, source_target_pairs={{1,0},{2,1},{3,2},{4,3},{5,4},{6,5},{7,6},{8,7},{9,8},{10,9},{11,1... | collective-permute-start | bytes 55304 | tf_op jit(solution)/shard_map/ppermute | solution.py:181
  32.4 3.0 %copy-start.2 = (f32[8,16,180]{2,1,0:T(8,128)S(1)}, f32[8,16,180]{2,1,0:T(8,128)}, u32[]{:S(2)}) copy-start(f32[8,16,180]{2,1,0:T(8,128)} %fusion.48) | copy-start | bytes 276484
  53.6 4.6 %collective-permute-start = (f32[2,32,1]{2,1,0:T(8,128)S(1)}, f32[2,32,1]{2,1,0:T(8,128)S(1)}, u32[]{:S(2)}, u32[]{:S(2)}) collective-permute-start(f32[2,32,1]{2,1,0:T(8,128)S(1)} %get-tuple-element.15), channel_id=1, source_target_pairs={{0,1},{1,2},{2,3},{3,4},{4,5},{5,6},{6,7},{7,8},{8,9},{9,10},{10,1... | collective-permute-start | bytes 776 | tf_op jit(solution)/shard_map/ppermute | solution.py:180
  53.8 6.4 %collective-permute-start.1 = (f32[2,32,1]{2,1,0:T(8,128)S(1)}, f32[2,32,1]{2,1,0:T(8,128)S(1)}, u32[]{:S(2)}, u32[]{:S(2)}) collective-permute-start(f32[2,32,1]{2,1,0:T(8,128)S(1)} %get-tuple-element.14), channel_id=1, source_target_pairs={{1,0},{2,1},{3,2},{4,3},{5,4},{6,5},{7,6},{8,7},{9,8},{10,9},{11,1... | collective-permute-start | bytes 776 | tf_op jit(solution)/shard_map/ppermute | solution.py:181
  58.2 13.2 %collective-permute-start.7 = (f32[2,180,72]{2,1,0:T(8,128)S(1)}, f32[2,180,72]{2,1,0:T(8,128)S(1)}, u32[]{:S(2)}, u32[]{:S(2)}) collective-permute-start(f32[2,180,72]{2,1,0:T(8,128)S(1)} %get-tuple-element.8), channel_id=1, source_target_pairs={{16,0},{32,16},{48,32},{64,48},{80,64},{96,80},{112,96},{128,112},... | collective-permute-start | bytes 311048 | tf_op jit(solution)/shard_map/ppermute | solution.py:181
  60.1 11.3 %collective-permute-start.4 = (f32[2,1,180]{2,1,0:T(1,128)S(1)}, f32[2,1,180]{2,1,0:T(1,128)S(1)}, u32[]{:S(2)}, u32[]{:S(2)}) collective-permute-start(f32[2,1,180]{2,1,0:T(1,128)S(1)} %get-tuple-element.17), channel_id=1, source_target_pairs={{0,16},{16,32},{32,48},{48,64},{64,80},{80,96},{96,112},{112,128},... | collective-permute-start | bytes 4328 | tf_op jit(solution)/shard_map/ppermute | solution.py:180
  67.4 8.8 %collective-permute-start.5 = (f32[2,1,180]{2,1,0:T(1,128)S(1)}, f32[2,1,180]{2,1,0:T(1,128)S(1)}, u32[]{:S(2)}, u32[]{:S(2)}) collective-permute-start(f32[2,1,180]{2,1,0:T(1,128)S(1)} %get-tuple-element.16), channel_id=1, source_target_pairs={{16,0},{32,16},{48,32},{64,48},{80,64},{96,80},{112,96},{128,112},... | collective-permute-start | bytes 4328 | tf_op jit(solution)/shard_map/ppermute | solution.py:181
  71.4 7.0 %copy-start = (f32[2,180,768]{2,0,1:T(2,128)S(1)}, f32[2,180,768]{2,0,1:T(2,128)}, u32[]{:S(2)}) copy-start(f32[2,180,768]{2,0,1:T(2,128)} %param.2) | copy-start | bytes 3317764
  78.9 1.6 %copy-start.1 = (f32[16,8,180]{2,1,0:T(8,128)S(1)}, f32[16,8,180]{2,1,0:T(8,128)}, u32[]{:S(2)}) copy-start(f32[16,8,180]{2,1,0:T(8,128)} %shard_map.42) | copy-start | bytes 276484

commit v3 on v0

--- a/solution.py
+++ b/solution.py
@@ -1,9 +1,14 @@
+import functools
 import math
 
 import jax
 import jax.numpy as jnp
 from jax import lax
+from jax.experimental import pallas as pl
+from jax.experimental.pallas import tpu as pltpu
 from jax.sharding import PartitionSpec as P
+
+MESH = pl.DeviceIdType.MESH
 
 COURANT = 0.3
 COS_FLOOR = 0.5
@@ -57,69 +62,126 @@
     return jnp.maximum(speed, 0.0) * left + jnp.minimum(speed, 0.0) * right
 
 
-def apply_table(values, table):
-    return jnp.einsum("rkm,mb->rkb", values, table, precision=EXACT_MODE)
-
-
-def filter_modes(real_part, imag_part, lon_block, row_cosine, lon_total):
-    columns = real_part.shape[-1]
-    blocks = lon_total // columns
+def filter_kernel(n, rows, winds_ref, kc_ref, ks_ref, tc_ref, ts_ref, c_ref, s_ref, factor_ref,
+                  out_ref, gathered, restored, send_a, recv_a, send_b, recv_b):
+    me = lax.axis_index("lon")
+    band = lax.axis_index("lat")
+    barrier = pltpu.get_barrier_semaphore()
+    for k in range(1, n):
+        peer = lax.rem(me + k, n)
+        pl.semaphore_signal(barrier, inc=1, device_id=(band, peer), device_id_type=MESH)
+    pl.semaphore_wait(barrier, n - 1)
+
+    def block(ref, index):
+        return ref.at[pl.ds(pl.multiple_of(index * rows, rows), rows)]
+
+    def swap(source, target, send_sem, recv_sem):
+        sends = []
+        for k in range(1, n):
+            peer = lax.rem(me + k, n)
+            copy = pltpu.make_async_remote_copy(
+                src_ref=block(source, peer),
+                dst_ref=block(target, me),
+                send_sem=send_sem.at[peer],
+                recv_sem=recv_sem.at[me],
+                device_id=(band, peer),
+                device_id_type=MESH,
+            )
+            copy.start()
+            sends.append(copy)
+        block(target, me)[...] = block(source, me)[...]
+        for k in range(1, n):
+            origin = lax.rem(me + n - k, n)
+            pltpu.make_async_remote_copy(
+                src_ref=block(source, origin),
+                dst_ref=block(target, origin),
+                send_sem=send_sem.at[origin],
+                recv_sem=recv_sem.at[origin],
+                device_id=(band, origin),
+                device_id_type=MESH,
+            ).wait_recv()
+        for copy in sends:
+            copy.wait_send()
+
+    swap(winds_ref, gathered, send_a, recv_a)
+
+    def mm(a, b):
+        return jnp.dot(a, b, precision=EXACT_MODE, preferred_element_type=jnp.float32)
+
+    x = gathered[...]
+    kc, ks = kc_ref[...], ks_ref[...]
+    tc, ts = tc_ref[...], ts_ref[...]
+    c, s = c_ref[...], s_ref[...]
+    re = mm(kc, x)
+    im = -mm(ks, x)
+    shifted_re = re * tc + im * ts
+    shifted_im = im * tc - re * ts
+    modes_re = mm(shifted_re, c) + mm(shifted_im, s)
+    modes_im = mm(shifted_im, c) - mm(shifted_re, s)
+    factor = factor_ref[...]
+    modes_re = modes_re * factor
+    modes_im = modes_im * factor
+    back_re = mm(modes_re, c) - mm(modes_im, s)
+    back_im = mm(modes_im, c) + mm(modes_re, s)
+    out_re = back_re * tc - back_im * ts
+    out_im = back_im * tc + back_re * ts
+    restored[...] = (mm(kc, out_re) - mm(ks, out_im)) / (n * x.shape[1])
+    swap(restored, out_ref, send_b, recv_b)
+
+
+def spectral(flat_winds, row_cosine, lon_total):
+    flat_rows, columns = flat_winds.shape
+    n = lax.axis_size("lon")
+    lon_index = lax.axis_index("lon")
+    rows = flat_rows // n
+    own_cosine = lax.dynamic_slice_in_dim(row_cosine, lon_index * rows, rows, 0)
+    block_ids = jnp.arange(n, dtype=jnp.int32)
+    phase = 2.0 * math.pi * (block_ids[:, None] * block_ids[None, :] % n).astype(jnp.float32) / n
+    eye = jnp.eye(rows, dtype=jnp.float32)
+    kron_cos = jnp.kron(jnp.cos(phase), eye)
+    kron_sin = jnp.kron(jnp.sin(phase), eye)
     column_ids = jnp.arange(columns, dtype=jnp.int32)
     twist = (
         2.0
         * math.pi
-        * (column_ids[None, :] * lon_block[:, None] % lon_total).astype(jnp.float32)
+        * (column_ids[None, :] * block_ids[:, None] % lon_total).astype(jnp.float32)
         / lon_total
     )
-    twist_cos = jnp.cos(twist)
-    twist_sin = jnp.sin(twist)
-    shifted_re = real_part * twist_cos + imag_part * twist_sin
-    shifted_im = imag_part * twist_cos - real_part * twist_sin
+    twist_cos = jnp.repeat(jnp.cos(twist), rows, axis=0)
+    twist_sin = jnp.repeat(jnp.sin(twist), rows, axis=0)
     table_turn = (
         2.0
         * math.pi
         * (column_ids[:, None] * column_ids[None, :] % columns).astype(jnp.float32)
         / columns
     )
-    table_cos = jnp.cos(table_turn)
-    table_sin = jnp.sin(table_turn)
-    modes_re = apply_table(shifted_re, table_cos) + apply_table(shifted_im, table_sin)
-    modes_im = apply_table(shifted_im, table_cos) - apply_table(shifted_re, table_sin)
-    wavenumber = lon_block[:, None] + blocks * column_ids[None, :]
-    factor = damping(row_cosine, wavenumber, lon_total)
-    modes_re = modes_re * factor
-    modes_im = modes_im * factor
-    back_re = apply_table(modes_re, table_cos) - apply_table(modes_im, table_sin)
-    back_im = apply_table(modes_im, table_cos) + apply_table(modes_re, table_sin)
-    return (back_re * twist_cos - back_im * twist_sin, back_im * twist_cos + back_re * twist_sin)
-
-
-def spectral(flat_winds, row_cosine, lon_total):
-    flat_rows, columns = flat_winds.shape
-    lon_count = lax.axis_size("lon")
-    lon_index = lax.axis_index("lon")
-    row_share = flat_rows // lon_count
-    full_rows = lax.all_to_all(flat_winds, "lon", split_axis=0, concat_axis=1, tiled=True)
-    own_cosine = lax.dynamic_slice_in_dim(row_cosine, lon_index * row_share, row_share, 0)
-    lon_grid = full_rows.reshape(row_share, lon_count, columns)
-    block_ids = jnp.arange(lon_count, dtype=jnp.int32)
-    phase_angle = (
-        2.0
-        * math.pi
-        * (block_ids[:, None] * block_ids[None, :] % lon_count).astype(jnp.float32)
-        / lon_count
-    )
-    phase_cos = jnp.cos(phase_angle)
-    phase_sin = jnp.sin(phase_angle)
-    real_part = jnp.einsum("rpm,pk->rkm", lon_grid, phase_cos, precision=EXACT_MODE)
-    imag_part = -jnp.einsum("rpm,pk->rkm", lon_grid, phase_sin, precision=EXACT_MODE)
-    out_re, out_im = filter_modes(real_part, imag_part, block_ids, own_cosine, lon_total)
-    restored = (
-        jnp.einsum("rkm,kp->rpm", out_re, phase_cos, precision=EXACT_MODE)
-        - jnp.einsum("rkm,kp->rpm", out_im, phase_sin, precision=EXACT_MODE)
-    ) / lon_total
-    return lax.all_to_all(
-        restored.reshape(row_share, lon_total), "lon", split_axis=1, concat_axis=0, tiled=True
+    wavenumber = block_ids[:, None] + n * column_ids[None, :]
+    factor = damping(own_cosine, wavenumber, lon_total)
+    factor = jnp.transpose(factor, (1, 0, 2)).reshape(n * rows, columns)
+    vmem = pl.BlockSpec(memory_space=pltpu.VMEM)
+    return pl.pallas_call(
+        functools.partial(filter_kernel, n, rows),
+        out_shape=jax.ShapeDtypeStruct(flat_winds.shape, flat_winds.dtype),
+        in_specs=[vmem] * 8,
+        out_specs=vmem,
+        scratch_shapes=[
+            pltpu.VMEM(flat_winds.shape, jnp.float32),
+            pltpu.VMEM(flat_winds.shape, jnp.float32),
+            pltpu.SemaphoreType.DMA((n,)),
+            pltpu.SemaphoreType.DMA((n,)),
+            pltpu.SemaphoreType.DMA((n,)),
+            pltpu.SemaphoreType.DMA((n,)),
+        ],
+        compiler_params=pltpu.CompilerParams(collective_id=0, has_side_effects=True),
+    )(
+        flat_winds,
+        kron_cos,
+        kron_sin,
+        twist_cos,
+        twist_sin,
+        jnp.cos(table_turn),
+        jnp.sin(table_turn),
+        factor,
     )
 
 

time: 70.9 us -> 67.1 us (0.946)
  the two profiles are of different devices: /device:TPU:33 before, /device:TPU:31 now
where the time goes in v3:
time: 67.1 us; the launch traced here: 66.7 us
  Pallas kernels  27.6 us (41%)
  local copies, waits for them, and re-layouts  15.7 us (23%)
  other arithmetic  11.8 us (18%)
  starting transfers between devices  8.19 us (12%)
  waiting for transfers between devices  2.51 us (4%)
  between operations  0.86 us (1%)
    pallas_call x1, Pallas kernels, spectral(): pl.pallas_call(functools.partial(filter_kernel, n, rows), out_shape=jax.S...  27.6 us
    ppermute x2, starting transfers between devices, extended(): before = lax.ppermute(last, axis, up)  5.68 us
    unnamed x9, local copies, waits for them, and re-layouts  4.18 us
    add x2, other arithmetic, upwind(): return jnp.maximum(speed, 0.0) * left + jnp.minimum(speed, 0.0) * right  2.9 us
    concatenate x2, other arithmetic, extended(): array = jnp.concatenate([before, array, after], axis=dim)  2.69 us
    ppermute x2, starting transfers between devices, extended(): after = lax.ppermute(first, axis, down)  2.52 us
    ppermute x2, waiting for transfers between devices, extended(): after = lax.ppermute(first, axis, down)  2.51 us
    mul x1, local copies, waits for them, and re-layouts, spectral(): kron_sin = jnp.kron(jnp.sin(phase), eye)  2.24 us
  transfers between devices with their start and end apart: 4, of which 1 were waited for; matrix products, arithmetic and copies ran while one was open for 13% of the time, Pallas kernels for 0%

profile of v3, /device:TPU:31, one launch (start us, length us, event | category | flops | bytes accessed | tf_op | source)
XLA Modules:
  0.0 66.7 jit_solution(3773480324748078133)
XLA Ops:
  1.0 1.5 %fusion.34 = (f32[180,180]{1,0:T(8,128)}, f32[180,180]{1,0:T(8,128)}) fusion(), kind=kLoop, calls=%fused_computation.51 | loop fusion | flops 291600 | bytes 259200 | tf_op jit(solution)/shard_map/sin | solution.py:183
  2.9 1.6 %copy.22 = f32[2,180,768]{1,2,0:T(8,128)S(1)} copy(f32[2,180,768]{2,0,1:T(2,128)} %param.2) | data formatting | bytes 2211840 | tf_op args[0]
  4.5 1.1 %broadcast_multiply_fusion = (f32[16,8,16,8]{3,2,1,0:T(8,128)}, f32[16,8,16,8]{3,2,1,0:T(8,128)S(1)}) fusion(f32[16,16]{1,0:T(8,128)S(1)} %get-tuple-element.20, f32[8,8]{1,0:T(8,128)S(1)} %fusion.57, f32[16,16]{1,0:T(8,128)S(1)} %get-tuple-element.21), kind=kLoop, calls=%fused_computation.43 | loop fusion | flops 32768 | bytes 133376 | tf_op jit(solution)/shard_map/jit(kron)/mul | solution.py:142
  5.6 2.2 %mul.293.ks_ref = f32[128,128]{1,0:T(8,128)} reshape(f32[16,8,16,8]{3,2,1,0:T(8,128)} %get-tuple-element.18) | data formatting | bytes 131072 | tf_op jit(solution)/shard_map/jit(kron)/mul | solution.py:142
  7.9 1.1 %mul.290.kc_ref = f32[128,128]{1,0:T(8,128)} reshape(f32[16,8,16,8]{3,2,1,0:T(8,128)S(1)} %get-tuple-element.19) | data formatting | bytes 131072 | tf_op jit(solution)/shard_map/jit(kron)/mul | solution.py:141
  9.0 0.7 %broadcast_bitcast_fusion = (f32[128,180]{1,0:T(8,128)}, f32[128,180]{1,0:T(8,128)}) fusion(f32[16,180]{1,0:T(8,128)S(1)} %fusion.46, f32[16,180]{1,0:T(8,128)S(1)} %fusion.47), kind=kLoop, calls=%fused_computation.62 | loop fusion | bytes 207360 | tf_op jit(solution)/shard_map/reshape | solution.py:151
  9.7 0.7 %fusion.38.factor_ref = f32[128,180]{1,0:T(8,128)} fusion(f32[16,180]{1,0:T(8,128)S(1)} %multiply_select_fusion, f32[128]{0:T(128)S(1)} %div.76, pred[16,180]{1,0:T(8,128)(4,1)S(1)} %fusion.43), kind=kLoop, calls=%fused_computation.56 | loop fusion | flops 69120 | bytes 107072 | tf_op jit(solution)/shard_map/jit(_where)/select_n | solution.py:36
  10.4 27.6 %shard_map.41 = f32[128,180]{1,0:T(8,128)} custom-call(f32[128,180]{1,0:T(8,128)} %bitcast.53, f32[128,128]{1,0:T(8,128)} %mul.290.kc_ref, f32[128,128]{1,0:T(8,128)} %mul.293.ks_ref, f32[128,180]{1,0:T(8,128)} %get-tuple-element.27.tc_ref, f32[128,180]{1,0:T(8,128)} %get-tuple-element.26.ts_ref, f32[180,180]{1,0:T(8,128)} %get-tuple-element.25.c_ref, ...), custom_call_target="tpu_custom_call" | custom-call | tf_op jit(solution)/shard_map/pallas_call | solution.py:162
  38.0 0.9 %fusion.61 = (f32[64,180]{1,0:T(8,128)S(1)}, f32[64,180]{1,0:T(8,128)S(1)}) fusion(f32[128,180]{1,0:T(8,128)} %shard_map.41), kind=kLoop, calls=%fused_computation.100 | loop fusion | bytes 184320 | tf_op jit(solution)/shard_map/slice | solution.py:203
  38.9 0.3 fusion.29
  39.2 0.3 copy.16
  39.5 0.4 collective-permute-start.1
  39.9 0.3 copy.14
  40.2 1.4 %collective-permute-start = (f32[2,3,800]{2,0,1:T(2,128)S(1)}, f32[2,3,800]{2,0,1:T(2,128)S(1)}, u32[]{:S(2)}, u32[]{:S(2)}) collective-permute-start(f32[2,3,800]{2,0,1:T(2,128)S(1)} %copy.14), channel_id=1, source_target_pairs={{0,1},{1,2},{2,3},{3,4},{4,5},{5,6},{6,7},{7,8},{8,9},{9,10},{10,1... | collective-permute-start | bytes 57608 | tf_op jit(solution)/shard_map/ppermute | solution.py:25
  41.6 0.2 pad_maximum_fusion
  41.8 1.3 %copy.19 = f32[2,180,32,25]{1,0,3,2:T(2,128)S(1)} copy(f32[2,180,32,25]{1,3,2,0:T(8,128)S(1)} %pad_maximum_fusion) | data formatting | bytes 2304000 | tf_op jit(solution)/shard_map/concatenate | solution.py:213
  43.1 0.8 %fusion.60 = (f32[2,180,75]{1,0,2:T(2,128)}, f32[2,180,75]{1,0,2:T(2,128)S(1)}) fusion(f32[2,180,800]{1,0,2:T(2,128)S(1)} %bitcast.43), kind=kLoop, calls=%fused_computation.99 | loop fusion | bytes 432000 | tf_op jit(solution)/shard_map/slice | solution.py:23
  43.9 4.3 %collective-permute-start.2 = (f32[2,180,75]{1,0,2:T(2,128)}, f32[2,180,75]{1,0,2:T(2,128)}, u32[]{:S(2)}, u32[]{:S(2)}) collective-permute-start(f32[2,180,75]{1,0,2:T(2,128)} %get-tuple-element.12), channel_id=1, source_target_pairs={{0,16},{16,32},{32,48},{48,64},{64,80},{80,96},{96,112},{112,128},... | collective-permute-start | bytes 324008 | tf_op jit(solution)/shard_map/ppermute | solution.py:25
  48.2 2.1 %collective-permute-start.3 = (f32[2,180,75]{1,0,2:T(2,128)S(1)}, f32[2,180,75]{1,0,2:T(2,128)}, u32[]{:S(2)}, u32[]{:S(2)}) collective-permute-start(f32[2,180,75]{1,0,2:T(2,128)S(1)} %get-tuple-element.13), channel_id=1, source_target_pairs={{16,0},{32,16},{48,32},{64,48},{80,64},{96,80},{112,96},{128,112},... | collective-permute-start | bytes 324008 | tf_op jit(solution)/shard_map/ppermute | solution.py:26
  50.6 1.2 %copy.15 = f32[2,3,800]{1,2,0:T(8,128)} copy(f32[2,3,800]{2,0,1:T(2,128)S(1)} %collective-permute-done) | data formatting | bytes 38400 | tf_op jit(solution)/shard_map/ppermute | solution.py:25
  51.8 1.2 %copy.17 = f32[2,3,800]{1,2,0:T(8,128)} copy(f32[2,3,800]{2,0,1:T(2,128)S(1)} %collective-permute-done.1) | data formatting | bytes 38400 | tf_op jit(solution)/shard_map/ppermute | solution.py:26
  53.0 1.0 %broadcast_maximum_fusion.1 = (f32[2,181,32]{1,2,0:T(8,128)S(1)}, f32[2,181,32]{1,2,0:T(8,128)S(1)}) fusion(f32[2,3,800]{1,2,0:T(8,128)} %copy.17, f32[2,180,32]{1,2,0:T(8,128)S(1)} %bitcast.49, f32[2,180,768]{1,2,0:T(8,128)S(1)} %copy.22, f32[2,3,800]{1,2,0:T(8,128)} %copy.15), kind=kLoop, calls=%fused_computation.67 | loop fusion | flops 81088 | bytes 1283072 | tf_op jit(solution)/shard_map/max | solution.py:62
  54.2 0.2 copy-done.1
  54.4 0.7 %maximum_maximum_fusion = (f32[2,183,800]{1,2,0:T(8,128)S(1)}, f32[2,183,800]{1,2,0:T(8,128)S(1)}) fusion(f32[2,180,32]{1,2,0:T(8,128)S(1)} %bitcast.50, f32[2,180,768]{1,2,0:T(8,128)S(1)} %copy.22, f32[2,3,800]{1,2,0:T(8,128)S(1)} %copy-done, f32[2,3,800]{1,2,0:T(8,128)S(1)} %copy-done.1), kind=kLoop, calls=%fused_computation.4 | loop fusion | flops 1171200 | bytes 3532800 | tf_op jit(solution)/shard_map/concatenate | solution.py:27
  55.2 1.7 %fusion.22 = f32[2,181,768]{1,2,0:T(8,128)S(1)} fusion(f32[2,183,800]{1,2,0:T(8,128)S(1)} %get-tuple-element.9, f32[2,183,800]{1,2,0:T(8,128)S(1)} %get-tuple-element.8, f32[2,181,32]{1,2,0:T(8,128)S(1)} %broadcast_minimum_fusion.1, f32[2,181,32]{1,2,0:T(8,128)S(1)} %get-tuple-element.6), kind=kLoop, calls=%fused_computation.33 | loop fusion | flops 6394368 | bytes 7877120 | tf_op jit(solution)/shard_map/add | solution.py:62
  56.9 2.5 %collective-permute-done.3 = f32[2,180,75]{1,0,2:T(2,128)} collective-permute-done((f32[2,180,75]{1,0,2:T(2,128)S(1)}, f32[2,180,75]{1,0,2:T(2,128)}, u32[]{:S(2)}, u32[]{:S(2)}) %collective-permute-start.3) | collective-permute-done | bytes 108032 | tf_op jit(solution)/shard_map/ppermute | solution.py:26
  59.4 2.0 %pad_maximum_fusion.1 = f32[2,180,950]{1,0,2:T(2,128)S(1)} fusion(f32[2,180,75]{1,0,2:T(2,128)} %collective-permute-done.3, f32[2,180,800]{1,0,2:T(2,128)S(1)} %bitcast.44, f32[2,180,75]{1,0,2:T(2,128)} %collective-permute-done.2), kind=kLoop, calls=%fused_computation.1 | loop fusion | flops 684000 | bytes 2736000 | tf_op jit(solution)/shard_map/concatenate | solution.py:27
  61.4 1.0 %slice.155 = f32[2,180,38,24]{1,0,3,2:T(2,128)S(1)} slice(f32[2,180,38,25]{1,0,3,2:T(2,128)S(1)} %bitcast.46), slice={[0:2], [0:180], [0:38], [0:24]} | slice | bytes 2626560 | tf_op jit(solution)/shard_map/slice | solution.py:220
  62.7 1.2 %fusion.6 = f32[2,180,792]{1,2,0:T(8,128)S(1)} fusion(f32[2,180,912]{1,2,0:T(8,128)S(1)} %bitcast.41, f32[2,180,33]{1,2,0:T(8,128)S(1)} %get-tuple-element.17, f32[2,180,33]{1,2,0:T(8,128)S(1)} %get-tuple-element.16), kind=kLoop, calls=%fused_computation.13 | loop fusion | flops 6557760 | bytes 8078400 | tf_op jit(solution)/shard_map/add | solution.py:62
  63.9 0.7 %fusion.15 = f32[2,180,768]{1,2,0:T(8,128)S(1)} fusion(f32[2,180,768]{1,2,0:T(8,128)S(1)} %copy.22, f32[2,180,792]{1,2,0:T(8,128)S(1)} %fusion.6, f32[2,181,768]{1,2,0:T(8,128)S(1)} %fusion.22, f32[768]{0:T(1024)S(1)} %reshape.163), kind=kLoop, calls=%fused_computation.24 | loop fusion | flops 1382400 | bytes 6638592 | tf_op jit(solution)/shard_map/sub | solution.py:238
  64.6 1.5 %copy.23 = f32[2,180,768]{2,0,1:T(2,128)} copy(f32[2,180,768]{1,2,0:T(8,128)S(1)} %fusion.15) | data formatting | bytes 2211840
  66.1 0.7 copy.27
  (30 shorter events, 1.3 us)
Async XLA Ops:
  39.5 12.3 %collective-permute-start.1 = (f32[2,3,800]{2,0,1:T(2,128)S(1)}, f32[2,3,800]{2,0,1:T(2,128)S(1)}, u32[]{:S(2)}, u32[]{:S(2)}) collective-permute-start(f32[2,3,800]{2,0,1:T(2,128)S(1)} %copy.16), channel_id=1, source_target_pairs={{1,0},{2,1},{3,2},{4,3},{5,4},{6,5},{7,6},{8,7},{9,8},{10,9},{11,1... | collective-permute-start | bytes 57608 | tf_op jit(solution)/shard_map/ppermute | solution.py:26
  40.2 10.4 %collective-permute-start = (f32[2,3,800]{2,0,1:T(2,128)S(1)}, f32[2,3,800]{2,0,1:T(2,128)S(1)}, u32[]{:S(2)}, u32[]{:S(2)}) collective-permute-start(f32[2,3,800]{2,0,1:T(2,128)S(1)} %copy.14), channel_id=1, source_target_pairs={{0,1},{1,2},{2,3},{3,4},{4,5},{5,6},{6,7},{7,8},{8,9},{9,10},{10,1... | collective-permute-start | bytes 57608 | tf_op jit(solution)/shard_map/ppermute | solution.py:25
  43.9 12.9 %collective-permute-start.2 = (f32[2,180,75]{1,0,2:T(2,128)}, f32[2,180,75]{1,0,2:T(2,128)}, u32[]{:S(2)}, u32[]{:S(2)}) collective-permute-start(f32[2,180,75]{1,0,2:T(2,128)} %get-tuple-element.12), channel_id=1, source_target_pairs={{0,16},{16,32},{32,48},{48,64},{64,80},{80,96},{96,112},{112,128},... | collective-permute-start | bytes 324008 | tf_op jit(solution)/shard_map/ppermute | solution.py:25
  48.2 11.1 %collective-permute-start.3 = (f32[2,180,75]{1,0,2:T(2,128)S(1)}, f32[2,180,75]{1,0,2:T(2,128)}, u32[]{:S(2)}, u32[]{:S(2)}) collective-permute-start(f32[2,180,75]{1,0,2:T(2,128)S(1)} %get-tuple-element.13), channel_id=1, source_target_pairs={{16,0},{32,16},{48,32},{64,48},{80,64},{96,80},{112,96},{128,112},... | collective-permute-start | bytes 324008 | tf_op jit(solution)/shard_map/ppermute | solution.py:26
  53.0 1.2 %copy-start = (f32[2,3,800]{1,2,0:T(8,128)S(1)}, f32[2,3,800]{1,2,0:T(8,128)}, u32[]{:S(2)}) copy-start(f32[2,3,800]{1,2,0:T(8,128)} %copy.15) | copy-start | bytes 57604
  53.0 1.4 %copy-start.1 = (f32[2,3,800]{1,2,0:T(8,128)S(1)}, f32[2,3,800]{1,2,0:T(8,128)}, u32[]{:S(2)}) copy-start(f32[2,3,800]{1,2,0:T(8,128)} %copy.17) | copy-start | bytes 57604
  64.6 1.5 %copy-start.2 = (f32[128,180]{1,0:T(8,128)S(1)}, f32[128,180]{1,0:T(8,128)}, u32[]{:S(2)}) copy-start(f32[128,180]{1,0:T(8,128)} %shard_map.41) | copy-start | bytes 276484

commit v4 on v3

--- a/solution.py
+++ b/solution.py
@@ -2,6 +2,7 @@
 import math
 
 import jax
+import numpy as np
 import jax.numpy as jnp
 from jax import lax
 from jax.experimental import pallas as pl
@@ -62,8 +63,8 @@
     return jnp.maximum(speed, 0.0) * left + jnp.minimum(speed, 0.0) * right
 
 
-def filter_kernel(n, rows, winds_ref, kc_ref, ks_ref, tc_ref, ts_ref, c_ref, s_ref, factor_ref,
-                  out_ref, gathered, restored, send_a, recv_a, send_b, recv_b):
+def filter_kernel(n, rows, winds_ref, scaled_ref, kc_ref, ks_ref, tc_ref, ts_ref, c_ref, s_ref,
+                  divisor_ref, zero_ref, out_ref, gathered, restored, send_a, recv_a, send_b, recv_b):
     me = lax.axis_index("lon")
     band = lax.axis_index("lat")
     barrier = pltpu.get_barrier_semaphore()
@@ -118,7 +119,9 @@
     shifted_im = im * tc - re * ts
     modes_re = mm(shifted_re, c) + mm(shifted_im, s)
     modes_im = mm(shifted_im, c) - mm(shifted_re, s)
-    factor = factor_ref[...]
+    factor = jnp.where(
+        zero_ref[...] > 0.0, 1.0, jnp.minimum(1.0, scaled_ref[...] / divisor_ref[...])
+    )
     modes_re = modes_re * factor
     modes_im = modes_im * factor
     back_re = mm(modes_re, c) - mm(modes_im, s)
@@ -129,40 +132,44 @@
     swap(restored, out_ref, send_b, recv_b)
 
 
+def spectral_tables(n, rows, columns):
+    lon_total = n * columns
+    blocks = np.arange(n)
+    phase = 2.0 * np.pi * (np.outer(blocks, blocks) % n) / n
+    eye = np.eye(rows)
+    column_ids = np.arange(columns)
+    twist = 2.0 * np.pi * (np.outer(blocks, column_ids) % lon_total) / lon_total
+    turn = 2.0 * np.pi * (np.outer(column_ids, column_ids) % columns) / columns
+    wavenumber = blocks[:, None] + n * column_ids[None, :]
+    sine = np.sin(wavenumber.astype(np.float32) * np.float32(math.pi / lon_total))
+    divisor = np.where(wavenumber == 0, np.float32(1.0), sine * sine).astype(np.float32)
+    zero_mode = (wavenumber == 0).astype(np.float32)
+    tables = (
+        np.kron(np.cos(phase), eye),
+        np.kron(np.sin(phase), eye),
+        np.repeat(np.cos(twist), rows, axis=0),
+        np.repeat(np.sin(twist), rows, axis=0),
+        np.cos(turn),
+        np.sin(turn),
+        np.repeat(divisor, rows, axis=0),
+        np.repeat(zero_mode, rows, axis=0),
+    )
+    return [jnp.asarray(t.astype(np.float32)) for t in tables]
+
+
 def spectral(flat_winds, row_cosine, lon_total):
     flat_rows, columns = flat_winds.shape
     n = lax.axis_size("lon")
     lon_index = lax.axis_index("lon")
     rows = flat_rows // n
     own_cosine = lax.dynamic_slice_in_dim(row_cosine, lon_index * rows, rows, 0)
-    block_ids = jnp.arange(n, dtype=jnp.int32)
-    phase = 2.0 * math.pi * (block_ids[:, None] * block_ids[None, :] % n).astype(jnp.float32) / n
-    eye = jnp.eye(rows, dtype=jnp.float32)
-    kron_cos = jnp.kron(jnp.cos(phase), eye)
-    kron_sin = jnp.kron(jnp.sin(phase), eye)
-    column_ids = jnp.arange(columns, dtype=jnp.int32)
-    twist = (
-        2.0
-        * math.pi
-        * (column_ids[None, :] * block_ids[:, None] % lon_total).astype(jnp.float32)
-        / lon_total
-    )
-    twist_cos = jnp.repeat(jnp.cos(twist), rows, axis=0)
-    twist_sin = jnp.repeat(jnp.sin(twist), rows, axis=0)
-    table_turn = (
-        2.0
-        * math.pi
-        * (column_ids[:, None] * column_ids[None, :] % columns).astype(jnp.float32)
-        / columns
-    )
-    wavenumber = block_ids[:, None] + n * column_ids[None, :]
-    factor = damping(own_cosine, wavenumber, lon_total)
-    factor = jnp.transpose(factor, (1, 0, 2)).reshape(n * rows, columns)
+    scaled = (own_cosine / COS_FLOOR) ** 2
+    scaled = jnp.tile(scaled, n).reshape(n * rows, 1)
     vmem = pl.BlockSpec(memory_space=pltpu.VMEM)
     return pl.pallas_call(
         functools.partial(filter_kernel, n, rows),
         out_shape=jax.ShapeDtypeStruct(flat_winds.shape, flat_winds.dtype),
-        in_specs=[vmem] * 8,
+        in_specs=[vmem] * 10,
         out_specs=vmem,
         scratch_shapes=[
             pltpu.VMEM(flat_winds.shape, jnp.float32),
@@ -173,16 +180,7 @@
             pltpu.SemaphoreType.DMA((n,)),
         ],
         compiler_params=pltpu.CompilerParams(collective_id=0, has_side_effects=True),
-    )(
-        flat_winds,
-        kron_cos,
-        kron_sin,
-        twist_cos,
-        twist_sin,
-        jnp.cos(table_turn),
-        jnp.sin(table_turn),
-        factor,
-    )
+    )(flat_winds, scaled, *spectral_tables(n, rows, columns))
 
 
 def local(tracers, wind_field):

time: 67.1 us -> 59 us (0.88)
  local copies, waits for them, and re-layouts: 15.7 us -> 11.5 us
  other arithmetic: 11.8 us -> 8.06 us
    mul x2 -> x0, local copies, waits for them, and re-layouts: 3.31 us -> none  [the longest x1 2.24 us: spectral(): kron_sin = jnp.kron(jnp.sin(phase), eye)]
    sin x3 -> x0, other arithmetic: 1.69 us -> none  [the longest x1 1.54 us: spectral(): jnp.sin(table_turn)]
    mul x2 -> x0, other arithmetic: 1.15 us -> none  [the longest x1 1.14 us: spectral(): kron_sin = jnp.kron(jnp.sin(phase), eye)]
    unnamed x9 -> x11, local copies, waits for them, and re-layouts: 4.18 us -> 3.28 us
    select_n x2 -> x0, other arithmetic: 0.81 us -> none  [the longest x1 0.73 us: damping(): return jnp.where(wavenumber == 0, 1.0, jnp.minimum(1.0, scaled / divisor))]
    another operation x0 -> x2, local copies, waits for them, and re-layouts: none -> 0.72 us  [spectral(): scaled = jnp.tile(scaled, n).reshape(n * rows, 1)]
    reshape x1 -> x0, local copies, waits for them, and re-layouts: 0.72 us -> none  [spectral(): twist_sin = jnp.repeat(jnp.sin(twist), rows, axis=0)]
  transfers between devices with their start and end apart: 4 -> 4, of which waited for: 1 -> 1; matrix products, arithmetic and copies ran while one was open for 13% -> 15% of each run, Pallas kernels for 0% -> 0%
where the time goes in v4:
time: 59 us; the launch traced here: 58.7 us
  Pallas kernels  27.7 us (47%)
  local copies, waits for them, and re-layouts  11.5 us (19%)
  other arithmetic  8.06 us (14%)
  starting transfers between devices  8.01 us (14%)
  waiting for transfers between devices  2.68 us (5%)
  between operations  0.84 us (1%)
    pallas_call x1, Pallas kernels, spectral(): pl.pallas_call(functools.partial(filter_kernel, n, rows), out_shape=jax.S...  27.7 us
    ppermute x2, starting transfers between devices, extended(): before = lax.ppermute(last, axis, up)  5.68 us
    unnamed x11, local copies, waits for them, and re-layouts  3.28 us
    add x2, other arithmetic, upwind(): return jnp.maximum(speed, 0.0) * left + jnp.minimum(speed, 0.0) * right  2.9 us
    concatenate x2, other arithmetic, extended(): array = jnp.concatenate([before, array, after], axis=dim)  2.69 us
    ppermute x2, waiting for transfers between devices, extended(): after = lax.ppermute(first, axis, down)  2.68 us
    ppermute x2, starting transfers between devices, extended(): after = lax.ppermute(first, axis, down)  2.34 us
    concatenate x1, local copies, waits for them, and re-layouts, local(): jnp.concatenate([tracers.reshape(levels, lon_cols, lat_rows, tracer_count...  1.3 us
  transfers between devices with their start and end apart: 4, of which 1 were waited for; matrix products, arithmetic and copies ran while one was open for 15% of the time, Pallas kernels for 0%

profile of v4, /device:TPU:31, one launch (start us, length us, event | category | flops | bytes accessed | tf_op | source)
XLA Modules:
  0.0 58.7 jit_solution(16282258049227918509)
XLA Ops:
  0.7 0.1 tile.7
  0.9 0.7 %reshape_tile.4.scaled_ref = f32[128,1]{1,0:T(8,128)} reshape(f32[16,8]{1,0:T(8,128)S(1)} %tile.8) | data formatting | bytes 1024 | tf_op jit(solution)/shard_map/reshape;tile | solution.py:167
  1.6 27.7 %shard_map.113 = f32[128,180]{1,0:T(8,128)} custom-call(f32[128,180]{1,0:T(8,128)} %bitcast.37, f32[128,1]{1,0:T(8,128)} %reshape_tile.4.scaled_ref, f32[128,128]{1,0:T(8,128)} %constant.24.clone.kc_ref, f32[128,128]{1,0:T(8,128)} %constant.25.clone.ks_ref, f32[128,180]{1,0:T(8,128)} %constant.26.clone.tc_ref, f32[128,180]{1,0:T(8,128)} %constant.27.clone.ts_ref, ...), custom_call_target="tpu_custom_call" | custom-call | tf_op jit(solution)/shard_map/pallas_call | solution.py:169
  29.3 0.9 %fusion.35 = (f32[64,180]{1,0:T(8,128)S(1)}, f32[64,180]{1,0:T(8,128)S(1)}) fusion(f32[128,180]{1,0:T(8,128)} %shard_map.113), kind=kLoop, calls=%fused_computation.58 | loop fusion | bytes 184320 | tf_op jit(solution)/shard_map/slice | solution.py:201
  30.2 0.7 %copy.33 = f32[2,180,768]{1,2,0:T(8,128)S(1)} copy(f32[2,180,768]{2,0,1:T(2,128)S(1)} %copy-done.3) | data formatting | bytes 2211840 | tf_op args[0]
  30.9 0.3 fusion.29
  31.2 0.3 copy.27
  31.5 0.4 collective-permute-start.1
  31.9 0.3 copy.25
  32.2 1.4 %collective-permute-start = (f32[2,3,800]{2,0,1:T(2,128)S(1)}, f32[2,3,800]{2,0,1:T(2,128)S(1)}, u32[]{:S(2)}, u32[]{:S(2)}) collective-permute-start(f32[2,3,800]{2,0,1:T(2,128)S(1)} %copy.25), channel_id=1, source_target_pairs={{0,1},{1,2},{2,3},{3,4},{4,5},{5,6},{6,7},{7,8},{8,9},{9,10},{10,1... | collective-permute-start | bytes 57608 | tf_op jit(solution)/shard_map/ppermute | solution.py:26
  33.6 0.2 pad_maximum_fusion
  33.9 1.3 %copy.30 = f32[2,180,32,25]{1,0,3,2:T(2,128)S(1)} copy(f32[2,180,32,25]{1,3,2,0:T(8,128)S(1)} %pad_maximum_fusion) | data formatting | bytes 2304000 | tf_op jit(solution)/shard_map/concatenate | solution.py:211
  35.2 0.8 %fusion.34 = (f32[2,180,75]{1,0,2:T(2,128)}, f32[2,180,75]{1,0,2:T(2,128)S(1)}) fusion(f32[2,180,800]{1,0,2:T(2,128)S(1)} %bitcast.27), kind=kLoop, calls=%fused_computation.57 | loop fusion | bytes 432000 | tf_op jit(solution)/shard_map/slice | solution.py:24
  35.9 4.3 %collective-permute-start.2 = (f32[2,180,75]{1,0,2:T(2,128)}, f32[2,180,75]{1,0,2:T(2,128)}, u32[]{:S(2)}, u32[]{:S(2)}) collective-permute-start(f32[2,180,75]{1,0,2:T(2,128)} %get-tuple-element.12), channel_id=1, source_target_pairs={{0,16},{16,32},{32,48},{48,64},{64,80},{80,96},{96,112},{112,128},... | collective-permute-start | bytes 324008 | tf_op jit(solution)/shard_map/ppermute | solution.py:26
  40.2 1.9 %collective-permute-start.3 = (f32[2,180,75]{1,0,2:T(2,128)S(1)}, f32[2,180,75]{1,0,2:T(2,128)}, u32[]{:S(2)}, u32[]{:S(2)}) collective-permute-start(f32[2,180,75]{1,0,2:T(2,128)S(1)} %get-tuple-element.13), channel_id=1, source_target_pairs={{16,0},{32,16},{48,32},{64,48},{80,64},{96,80},{112,96},{128,112},... | collective-permute-start | bytes 324008 | tf_op jit(solution)/shard_map/ppermute | solution.py:27
  42.3 0.1 reshape.66
  42.4 1.2 %copy.26 = f32[2,3,800]{1,2,0:T(8,128)} copy(f32[2,3,800]{2,0,1:T(2,128)S(1)} %collective-permute-done) | data formatting | bytes 38400 | tf_op jit(solution)/shard_map/ppermute | solution.py:26
  43.6 1.2 %copy.28 = f32[2,3,800]{1,2,0:T(8,128)} copy(f32[2,3,800]{2,0,1:T(2,128)S(1)} %collective-permute-done.1) | data formatting | bytes 38400 | tf_op jit(solution)/shard_map/ppermute | solution.py:27
  44.8 1.0 %broadcast_maximum_fusion.1 = (f32[2,181,32]{1,2,0:T(8,128)S(1)}, f32[2,181,32]{1,2,0:T(8,128)S(1)}) fusion(f32[2,3,800]{1,2,0:T(8,128)} %copy.28, f32[2,180,32]{1,2,0:T(8,128)S(1)} %bitcast.33, f32[2,180,768]{1,2,0:T(8,128)S(1)} %copy.33, f32[2,3,800]{1,2,0:T(8,128)} %copy.26), kind=kLoop, calls=%fused_computation.51 | loop fusion | flops 81088 | bytes 1283072 | tf_op jit(solution)/shard_map/max | solution.py:63
  45.9 0.2 copy-done
  46.0 0.2 copy-done.1
  46.3 0.7 %maximum_maximum_fusion = (f32[2,183,800]{1,2,0:T(8,128)S(1)}, f32[2,183,800]{1,2,0:T(8,128)S(1)}) fusion(f32[2,180,32]{1,2,0:T(8,128)S(1)} %bitcast.34, f32[2,180,768]{1,2,0:T(8,128)S(1)} %copy.33, f32[2,3,800]{1,2,0:T(8,128)S(1)} %copy-done, f32[2,3,800]{1,2,0:T(8,128)S(1)} %copy-done.1), kind=kLoop, calls=%fused_computation.4 | loop fusion | flops 1171200 | bytes 3532800 | tf_op jit(solution)/shard_map/concatenate | solution.py:28
  47.0 1.7 %fusion.22 = f32[2,181,768]{1,2,0:T(8,128)S(1)} fusion(f32[2,183,800]{1,2,0:T(8,128)S(1)} %get-tuple-element.9, f32[2,183,800]{1,2,0:T(8,128)S(1)} %get-tuple-element.8, f32[2,181,32]{1,2,0:T(8,128)S(1)} %broadcast_minimum_fusion.1, f32[2,181,32]{1,2,0:T(8,128)S(1)} %get-tuple-element.6), kind=kLoop, calls=%fused_computation.33 | loop fusion | flops 6394368 | bytes 7877120 | tf_op jit(solution)/shard_map/add | solution.py:63
  48.7 2.7 %collective-permute-done.3 = f32[2,180,75]{1,0,2:T(2,128)} collective-permute-done((f32[2,180,75]{1,0,2:T(2,128)S(1)}, f32[2,180,75]{1,0,2:T(2,128)}, u32[]{:S(2)}, u32[]{:S(2)}) %collective-permute-start.3) | collective-permute-done | bytes 108032 | tf_op jit(solution)/shard_map/ppermute | solution.py:27
  51.4 2.0 %pad_maximum_fusion.1 = f32[2,180,950]{1,0,2:T(2,128)S(1)} fusion(f32[2,180,75]{1,0,2:T(2,128)} %collective-permute-done.3, f32[2,180,800]{1,0,2:T(2,128)S(1)} %bitcast.28, f32[2,180,75]{1,0,2:T(2,128)} %collective-permute-done.2), kind=kLoop, calls=%fused_computation.1 | loop fusion | flops 684000 | bytes 2736000 | tf_op jit(solution)/shard_map/concatenate | solution.py:28
  53.4 1.0 %slice.155 = f32[2,180,38,24]{1,0,3,2:T(2,128)S(1)} slice(f32[2,180,38,25]{1,0,3,2:T(2,128)S(1)} %bitcast.30), slice={[0:2], [0:180], [0:38], [0:24]} | slice | bytes 2626560 | tf_op jit(solution)/shard_map/slice | solution.py:218
  54.4 0.1 copy.32
  54.6 0.1 broadcast_maximum_fusion
  54.7 1.2 %fusion.6 = f32[2,180,792]{1,2,0:T(8,128)S(1)} fusion(f32[2,180,912]{1,2,0:T(8,128)S(1)} %bitcast.25, f32[2,180,33]{1,2,0:T(8,128)S(1)} %get-tuple-element.17, f32[2,180,33]{1,2,0:T(8,128)S(1)} %get-tuple-element.16), kind=kLoop, calls=%fused_computation.13 | loop fusion | flops 6557760 | bytes 8078400 | tf_op jit(solution)/shard_map/add | solution.py:63
  55.9 0.7 %fusion.15 = f32[2,180,768]{1,2,0:T(8,128)S(1)} fusion(f32[2,180,768]{1,2,0:T(8,128)S(1)} %copy.33, f32[2,180,792]{1,2,0:T(8,128)S(1)} %fusion.6, f32[2,181,768]{1,2,0:T(8,128)S(1)} %fusion.22, f32[768]{0:T(1024)S(1)} %reshape.66), kind=kLoop, calls=%fused_computation.24 | loop fusion | flops 1382400 | bytes 6638592 | tf_op jit(solution)/shard_map/sub | solution.py:236
  56.6 1.5 %copy.34 = f32[2,180,768]{2,0,1:T(2,128)} copy(f32[2,180,768]{1,2,0:T(8,128)S(1)} %fusion.15) | data formatting | bytes 2211840
  58.1 0.7 %copy.38 = f32[2,2,32,180]{3,2,1,0:T(8,128)} copy(f32[2,2,32,180]{3,2,1,0:T(8,128)S(1)} %bitcast.31) | data formatting | bytes 184320
  (19 shorter events, 0.3 us)
Async XLA Ops:
  0.6 29.5 %copy-start.3 = (f32[2,180,768]{2,0,1:T(2,128)S(1)}, f32[2,180,768]{2,0,1:T(2,128)}, u32[]{:S(2)}) copy-start(f32[2,180,768]{2,0,1:T(2,128)} %param.10) | copy-start | bytes 3317764
  31.5 12.1 %collective-permute-start.1 = (f32[2,3,800]{2,0,1:T(2,128)S(1)}, f32[2,3,800]{2,0,1:T(2,128)S(1)}, u32[]{:S(2)}, u32[]{:S(2)}) collective-permute-start(f32[2,3,800]{2,0,1:T(2,128)S(1)} %copy.27), channel_id=1, source_target_pairs={{1,0},{2,1},{3,2},{4,3},{5,4},{6,5},{7,6},{8,7},{9,8},{10,9},{11,1... | collective-permute-start | bytes 57608 | tf_op jit(solution)/shard_map/ppermute | solution.py:27
  32.2 10.2 %collective-permute-start = (f32[2,3,800]{2,0,1:T(2,128)S(1)}, f32[2,3,800]{2,0,1:T(2,128)S(1)}, u32[]{:S(2)}, u32[]{:S(2)}) collective-permute-start(f32[2,3,800]{2,0,1:T(2,128)S(1)} %copy.25), channel_id=1, source_target_pairs={{0,1},{1,2},{2,3},{3,4},{4,5},{5,6},{6,7},{7,8},{8,9},{9,10},{10,1... | collective-permute-start | bytes 57608 | tf_op jit(solution)/shard_map/ppermute | solution.py:26
  35.9 12.8 %collective-permute-start.2 = (f32[2,180,75]{1,0,2:T(2,128)}, f32[2,180,75]{1,0,2:T(2,128)}, u32[]{:S(2)}, u32[]{:S(2)}) collective-permute-start(f32[2,180,75]{1,0,2:T(2,128)} %get-tuple-element.12), channel_id=1, source_target_pairs={{0,16},{16,32},{32,48},{48,64},{64,80},{80,96},{96,112},{112,128},... | collective-permute-start | bytes 324008 | tf_op jit(solution)/shard_map/ppermute | solution.py:26
  40.2 11.1 %collective-permute-start.3 = (f32[2,180,75]{1,0,2:T(2,128)S(1)}, f32[2,180,75]{1,0,2:T(2,128)}, u32[]{:S(2)}, u32[]{:S(2)}) collective-permute-start(f32[2,180,75]{1,0,2:T(2,128)S(1)} %get-tuple-element.13), channel_id=1, source_target_pairs={{16,0},{32,16},{48,32},{64,48},{80,64},{96,80},{112,96},{128,112},... | collective-permute-start | bytes 324008 | tf_op jit(solution)/shard_map/ppermute | solution.py:27
  44.8 1.2 %copy-start = (f32[2,3,800]{1,2,0:T(8,128)S(1)}, f32[2,3,800]{1,2,0:T(8,128)}, u32[]{:S(2)}) copy-start(f32[2,3,800]{1,2,0:T(8,128)} %copy.26) | copy-start | bytes 57604
  44.8 1.4 %copy-start.1 = (f32[2,3,800]{1,2,0:T(8,128)S(1)}, f32[2,3,800]{1,2,0:T(8,128)}, u32[]{:S(2)}) copy-start(f32[2,3,800]{1,2,0:T(8,128)} %copy.28) | copy-start | bytes 57604
  56.6 1.5 %copy-start.2 = (f32[128,180]{1,0:T(8,128)S(1)}, f32[128,180]{1,0:T(8,128)}, u32[]{:S(2)}) copy-start(f32[128,180]{1,0:T(8,128)} %shard_map.113) | copy-start | bytes 276484

commit v5 on v4

--- a/solution.py
+++ b/solution.py
@@ -64,19 +64,56 @@
 
 
 def filter_kernel(n, rows, winds_ref, scaled_ref, kc_ref, ks_ref, tc_ref, ts_ref, c_ref, s_ref,
-                  divisor_ref, zero_ref, out_ref, gathered, restored, send_a, recv_a, send_b, recv_b):
+                  divisor_ref, zero_ref, widen_ref, prev_ref, next_ref, tracers_ref,
+                  out_ref, west_ref, east_ref, south_ref, north_ref, vsouth_ref, vnorth_ref,
+                  gathered, restored, send_a, recv_a, send_b, recv_b, halo_send, halo_recv, local_sem):
     me = lax.axis_index("lon")
     band = lax.axis_index("lat")
+    bands = lax.axis_size("lat")
+    up, down = lax.rem(band + 1, bands), lax.rem(band + bands - 1, bands)
+    east_peer, west_peer = lax.rem(me + 1, n), lax.rem(me + n - 1, n)
     barrier = pltpu.get_barrier_semaphore()
     for k in range(1, n):
         peer = lax.rem(me + k, n)
         pl.semaphore_signal(barrier, inc=1, device_id=(band, peer), device_id_type=MESH)
-    pl.semaphore_wait(barrier, n - 1)
+    for other in (up, down):
+        pl.semaphore_signal(barrier, inc=1, device_id=(other, me), device_id_type=MESH)
+    pl.semaphore_wait(barrier, n + 1)
+
+    cols, merged = tracers_ref.shape[1], tracers_ref.shape[2]
+    lane_depth = south_ref.shape[2]
+    flat_rows = out_ref.shape[0]
+    level_rows = flat_rows // 4
+    halo_plan = [
+        (tracers_ref.at[:, pl.ds(cols - west_ref.shape[1], west_ref.shape[1]), :], west_ref, (band, east_peer)),
+        (tracers_ref.at[:, pl.ds(0, east_ref.shape[1]), :], east_ref, (band, west_peer)),
+        (tracers_ref.at[:, :, pl.ds(merged - lane_depth, lane_depth)], south_ref, (up, me)),
+        (tracers_ref.at[:, :, pl.ds(0, lane_depth)], north_ref, (down, me)),
+    ]
+    for level in range(2):
+        first = 2 * level_rows + level * level_rows
+        halo_plan.append(
+            (out_ref.at[pl.ds(first + level_rows - 1, 1)], vsouth_ref.at[pl.ds(level, 1)], (up, me))
+        )
+    for level in range(2):
+        first = 2 * level_rows + level * level_rows
+        halo_plan.append((out_ref.at[pl.ds(first, 1)], vnorth_ref.at[pl.ds(level, 1)], (down, me)))
+
+    def halo_copy(index):
+        source, target, device = halo_plan[index]
+        return pltpu.make_async_remote_copy(
+            src_ref=source,
+            dst_ref=target,
+            send_sem=halo_send.at[index],
+            recv_sem=halo_recv.at[index],
+            device_id=device,
+            device_id_type=MESH,
+        )
 
     def block(ref, index):
         return ref.at[pl.ds(pl.multiple_of(index * rows, rows), rows)]
 
-    def swap(source, target, send_sem, recv_sem):
+    def swap(source, target, send_sem, recv_sem, slot):
         sends = []
         for k in range(1, n):
             peer = lax.rem(me + k, n)
@@ -90,7 +127,12 @@
             )
             copy.start()
             sends.append(copy)
-        block(target, me)[...] = block(source, me)[...]
+        own = pltpu.make_async_copy(block(source, me), block(target, me), local_sem.at[slot])
+        own.start()
+        return sends, own
+
+    def settle(source, target, send_sem, recv_sem, sends, own):
+        own.wait()
         for k in range(1, n):
             origin = lax.rem(me + n - k, n)
             pltpu.make_async_remote_copy(
@@ -104,7 +146,11 @@
         for copy in sends:
             copy.wait_send()
 
-    swap(winds_ref, gathered, send_a, recv_a)
+    sends, own = swap(winds_ref, gathered, send_a, recv_a, 0)
+    tracer_halos = [halo_copy(i) for i in range(4)]
+    for copy in tracer_halos:
+        copy.start()
+    settle(winds_ref, gathered, send_a, recv_a, sends, own)
 
     def mm(a, b):
         return jnp.dot(a, b, precision=EXACT_MODE, preferred_element_type=jnp.float32)
@@ -128,8 +174,21 @@
     back_im = mm(modes_im, c) + mm(modes_re, s)
     out_re = back_re * tc - back_im * ts
     out_im = back_im * tc + back_re * ts
-    restored[...] = (mm(kc, out_re) - mm(ks, out_im)) / (n * x.shape[1])
-    swap(restored, out_ref, send_b, recv_b)
+    result = (mm(kc, out_re) - mm(ks, out_im)) / (n * x.shape[1])
+    restored[...] = (
+        mm(result, widen_ref[...])
+        + mm(jnp.roll(result, rows, axis=0), prev_ref[...])
+        + mm(jnp.roll(result, -rows, axis=0), next_ref[...])
+    )
+    sends, own = swap(restored, out_ref, send_b, recv_b, 1)
+    settle(restored, out_ref, send_b, recv_b, sends, own)
+    wind_halos = [halo_copy(i) for i in range(4, 8)]
+    for copy in wind_halos:
+        copy.start()
+    for copy in tracer_halos + wind_halos:
+        copy.wait_recv()
+    for copy in tracer_halos + wind_halos:
+        copy.wait_send()
 
 
 def spectral_tables(n, rows, columns):
@@ -144,6 +203,11 @@
     sine = np.sin(wavenumber.astype(np.float32) * np.float32(math.pi / lon_total))
     divisor = np.where(wavenumber == 0, np.float32(1.0), sine * sine).astype(np.float32)
     zero_mode = (wavenumber == 0).astype(np.float32)
+    widen = np.eye(columns, columns + 2)
+    take_last = np.zeros((columns, columns + 2))
+    take_last[columns - 1, columns] = 1.0
+    take_first = np.zeros((columns, columns + 2))
+    take_first[0, columns + 1] = 1.0
     tables = (
         np.kron(np.cos(phase), eye),
         np.kron(np.sin(phase), eye),
@@ -153,82 +217,126 @@
         np.sin(turn),
         np.repeat(divisor, rows, axis=0),
         np.repeat(zero_mode, rows, axis=0),
+        widen,
+        take_last,
+        take_first,
     )
     return [jnp.asarray(t.astype(np.float32)) for t in tables]
 
 
-def spectral(flat_winds, row_cosine, lon_total):
+def exchange_all(flat_winds, row_cosine, tracers):
     flat_rows, columns = flat_winds.shape
+    levels, lon_cols, merged = tracers.shape
     n = lax.axis_size("lon")
     lon_index = lax.axis_index("lon")
     rows = flat_rows // n
-    own_cosine = lax.dynamic_slice_in_dim(row_cosine, lon_index * rows, rows, 0)
+    tracer_count = merged // row_cosine.shape[0]
+    own_cosine = lax.dynamic_slice_in_dim(jnp.tile(row_cosine, flat_rows // row_cosine.shape[0]), lon_index * rows, rows, 0)
     scaled = (own_cosine / COS_FLOOR) ** 2
     scaled = jnp.tile(scaled, n).reshape(n * rows, 1)
     vmem = pl.BlockSpec(memory_space=pltpu.VMEM)
+    west_cols = lon_cols - (lon_cols - 3) // 8 * 8
+    lanes = -(-3 * tracer_count // 128) * 128
+    shapes = [
+        (flat_rows, columns + 2),
+        (levels, west_cols, merged),
+        (levels, 8, merged),
+        (levels, lon_cols, lanes),
+        (levels, lon_cols, lanes),
+        (levels, columns + 2),
+        (levels, columns + 2),
+    ]
     return pl.pallas_call(
         functools.partial(filter_kernel, n, rows),
-        out_shape=jax.ShapeDtypeStruct(flat_winds.shape, flat_winds.dtype),
-        in_specs=[vmem] * 10,
-        out_specs=vmem,
+        out_shape=[jax.ShapeDtypeStruct(shape, jnp.float32) for shape in shapes],
+        in_specs=[vmem] * 13 + [pl.BlockSpec(memory_space=pl.ANY)],
+        out_specs=[vmem] * len(shapes),
         scratch_shapes=[
-            pltpu.VMEM(flat_winds.shape, jnp.float32),
-            pltpu.VMEM(flat_winds.shape, jnp.float32),
+            pltpu.VMEM((flat_rows, columns), jnp.float32),
+            pltpu.VMEM((flat_rows, columns + 2), jnp.float32),
             pltpu.SemaphoreType.DMA((n,)),
             pltpu.SemaphoreType.DMA((n,)),
             pltpu.SemaphoreType.DMA((n,)),
             pltpu.SemaphoreType.DMA((n,)),
+            pltpu.SemaphoreType.DMA((8,)),
+            pltpu.SemaphoreType.DMA((8,)),
+            pltpu.SemaphoreType.DMA((2,)),
         ],
         compiler_params=pltpu.CompilerParams(collective_id=0, has_side_effects=True),
-    )(flat_winds, scaled, *spectral_tables(n, rows, columns))
+    )(flat_winds, scaled, *spectral_tables(n, rows, columns), tracers)
+
+
+def stencil(padded, dim, faces, stride):
+
+    def offset_cells(offset):
+        return lax.slice_in_dim(padded, offset * stride, (offset + faces) * stride, axis=dim)
+
+    left = (
+        2.0 * offset_cells(0)
+        - 13.0 * offset_cells(1)
+        + 47.0 * offset_cells(2)
+        + 27.0 * offset_cells(3)
+        - 3.0 * offset_cells(4)
+    ) / 60.0
+    right = (
+        2.0 * offset_cells(5)
+        - 13.0 * offset_cells(4)
+        + 47.0 * offset_cells(3)
+        + 27.0 * offset_cells(2)
+        - 3.0 * offset_cells(1)
+    ) / 60.0
+    return left, right
+
+
+def spread(values, rows, tracer_count):
+    lanes = jnp.arange(rows * tracer_count, dtype=jnp.int32) // tracer_count
+    pick = (jnp.arange(rows, dtype=jnp.int32)[:, None] == lanes[None, :]).astype(jnp.float32)
+    return jnp.einsum("ljc,jm->lcm", values, pick, precision=EXACT_MODE)
 
 
 def local(tracers, wind_field):
     levels, lon_cols, merged = tracers.shape
     lat_rows = wind_field.shape[2]
     tracer_count = merged // lat_rows
-    lon_total = lon_cols * lax.axis_size("lon")
     lat_total = lat_rows * lax.axis_size("lat")
-    first_row = lax.axis_index("lat") * lat_rows
+    band = lax.axis_index("lat")
+    first_row = band * lat_rows
     row_ids = first_row + jnp.arange(lat_rows, dtype=jnp.int32)
     row_cosine = jnp.cos(
         (row_ids.astype(jnp.float32) + 0.5) * (math.pi / lat_total) - 0.5 * math.pi
     )
     flat_winds = wind_field.reshape(2 * levels * lat_rows, lon_cols)
-    flat_cosine = jnp.tile(row_cosine, 2 * levels)
-    smoothed = spectral(flat_winds, flat_cosine, lon_total)
-    smoothed = smoothed.reshape(2, levels, lat_rows, lon_cols)
-    east_turned = jnp.transpose(smoothed[0], (0, 2, 1))
-    north_turned = jnp.transpose(smoothed[1], (0, 2, 1))
-    zonal_stack = jnp.concatenate([tracers, east_turned], axis=2)
-    zonal_pad = extended(zonal_stack, (("lon", 1),), 3, True)
-    east_wind = zonal_pad[:, :, merged:]
-    zonal_speed = 0.5 * (east_wind[:, 2 : lon_cols + 3] + east_wind[:, 3 : lon_cols + 4])
-    zonal_speed = jnp.repeat(zonal_speed, tracer_count, axis=2)
-    left_x, right_x = face_values(zonal_pad[:, :, :merged], 1, lon_cols, 1)
-    zonal_flux = upwind(zonal_speed, left_x, right_x)
-    slot_count = tracer_count + 1
-    merid_stack = jnp.concatenate(
-        [tracers.reshape(levels, lon_cols, lat_rows, tracer_count), north_turned[..., None]], axis=3
-    )
-    merid_stack = merid_stack.reshape(levels, lon_cols, lat_rows * slot_count)
-    merid_pad = extended(merid_stack, (("lat", 2),), 3 * slot_count, False)
-    merid_pad = merid_pad.reshape(levels, lon_cols, lat_rows + 6, slot_count)
-    north_wind = merid_pad[..., tracer_count]
-    tracer_pad = merid_pad[..., :tracer_count].reshape(
-        levels, lon_cols, (lat_rows + 6) * tracer_count
-    )
+    wide, west, east, south, north, v_south, v_north = exchange_all(flat_winds, row_cosine, tracers)
+    has_south = band > 0
+    has_north = band < lax.axis_size("lat") - 1
+    west = west[:, west.shape[1] - 3 :]
+    east = east[:, :3]
+    south = jnp.where(has_south, south[..., south.shape[2] - 3 * tracer_count :], 0.0)
+    north = jnp.where(has_north, north[..., : 3 * tracer_count], 0.0)
+    v_south = jnp.where(has_south, v_south[:, :lon_cols], 0.0)
+    v_north = jnp.where(has_north, v_north[:, :lon_cols], 0.0)
+    wide = wide.reshape(2, levels, lat_rows, lon_cols + 2)
+    smoothed = wide[..., :lon_cols]
+    east_wide = wide[0]
+    north_wind = smoothed[1]
+    u_pad = jnp.concatenate(
+        [east_wide[..., lon_cols : lon_cols + 1], east_wide[..., :lon_cols], east_wide[..., lon_cols + 1 :]],
+        axis=2,
+    )
+    zonal_speed = 0.5 * (u_pad[:, :, : lon_cols + 1] + u_pad[:, :, 1:])
+    v_pad = jnp.concatenate([v_south[:, None], north_wind, v_north[:, None]], axis=1)
     face_ids = first_row + jnp.arange(lat_rows + 1, dtype=jnp.int32)
     face_cosine = jnp.cos(face_ids.astype(jnp.float32) * (math.pi / lat_total) - 0.5 * math.pi)
     face_cosine = jnp.where((face_ids == 0) | (face_ids == lat_total), 0.0, face_cosine)
-    merid_speed = (
-        0.5
-        * (north_wind[:, :, 2 : lat_rows + 3] + north_wind[:, :, 3 : lat_rows + 4])
-        * face_cosine[None, None, :]
-    )
-    merid_speed = jnp.repeat(merid_speed, tracer_count, axis=2)
-    left_y, right_y = face_values(tracer_pad, 2, lat_rows, tracer_count)
-    merid_flux = upwind(merid_speed, left_y, right_y)
+    merid_speed = 0.5 * (v_pad[:, : lat_rows + 1] + v_pad[:, 1:]) * face_cosine[None, :, None]
+    zonal_rep = spread(zonal_speed, lat_rows, tracer_count)
+    merid_rep = spread(merid_speed, lat_rows + 1, tracer_count)
+    zonal_pad = jnp.concatenate([west, tracers, east], axis=1)
+    left_x, right_x = stencil(zonal_pad, 1, lon_cols + 1, 1)
+    zonal_flux = upwind(zonal_rep, left_x, right_x)
+    merid_pad = jnp.concatenate([south, tracers, north], axis=2)
+    left_y, right_y = stencil(merid_pad, 2, lat_rows + 1, tracer_count)
+    merid_flux = upwind(merid_rep, left_y, right_y)
     metric = jnp.repeat(1.0 / jnp.maximum(row_cosine, COS_FLOOR), tracer_count)
     change = COURANT * (zonal_flux[:, 1:] - zonal_flux[:, :-1]) + COURANT * (
         merid_flux[:, :, tracer_count:] - merid_flux[:, :, :-tracer_count]

time: 59 us -> 55.4 us (0.939)
  the two profiles are of different devices: /device:TPU:31 before, /device:TPU:1 now
where the time goes in v5:
time: 55.4 us; the launch traced here: 55.1 us
  Pallas kernels  36.7 us (66%)
  local copies, waits for them, and re-layouts  6.48 us (12%)
  other arithmetic  5.56 us (10%)
  matrix products  5.54 us (10%)
  between operations  0.79 us (1%)
    pallas_call x1, Pallas kernels, exchange_all(): pl.pallas_call(functools.partial(filter_kernel, n, rows), out_shape=[jax....  36.7 us
    dot_general x2, matrix products, spread(): return jnp.einsum('ljc,jm->lcm', values, pick, precision=EXACT_MODE)  5.54 us
    unnamed x13, local copies, waits for them, and re-layouts  4.56 us
    sub x1, other arithmetic, local(): advected = tracers - metric[None, None, :] * change  2.05 us

profile of v5, /device:TPU:1, one launch (start us, length us, event | category | flops | bytes accessed | tf_op | source)
XLA Modules:
  0.0 55.1 jit_solution(1358879684777014862)
XLA Ops:
  0.6 2.3 %copy.33.tracers_ref = f32[2,180,768]{2,1,0:T(8,128)} copy(f32[2,180,768]{2,0,1:T(2,128)} %param.13) | data formatting | bytes 2211840 | tf_op args[0]
  3.0 0.1 tile.7
  3.1 0.1 multiply_multiply_fusion
  3.2 0.7 %reshape_tile.4.scaled_ref = f32[128,1]{1,0:T(8,128)} reshape(f32[16,8]{1,0:T(8,128)S(1)} %tile.8) | data formatting | bytes 1024 | tf_op jit(solution)/shard_map/reshape;tile | solution.py:236
  3.9 0.0 copy-start
  3.9 36.7 %shard_map.140 = (f32[128,182]{1,0:T(8,128)}, f32[2,4,768]{2,1,0:T(4,128)}, f32[2,8,768]{2,1,0:T(8,128)}, f32[2,180,128]{2,1,0:T(8,128)}, f32[2,180,128]{2,1,0:T...) custom-call(f32[128,180]{1,0:T(8,128)} %bitcast.21, f32[128,1]{1,0:T(8,128)} %reshape_tile.4.scaled_ref, ...), custom_call_target="tpu_custom_call" | custom-call | tf_op jit(solution)/shard_map/pallas_call | solution.py:249
  40.6 1.0 %slice_select_fusion.1 = f32[2,180,72]{2,1,0:T(8,128)S(1)} fusion(f32[2,180,128]{2,1,0:T(8,128)} %get-tuple-element.14, pred[]{:T(512)S(6)} %gt.3), kind=kLoop, calls=%fused_computation.60 | loop fusion | flops 25920 | bytes 207361 | tf_op jit(solution)/shard_map/jit(_where)/select_n | solution.py:314
  41.7 0.9 %slice_select_fusion = f32[2,180,72]{2,1,0:T(8,128)S(1)} fusion(f32[2,180,128]{2,1,0:T(8,128)} %get-tuple-element.15, pred[]{:T(512)S(6)} %lt.7), kind=kLoop, calls=%fused_computation.59 | loop fusion | flops 25920 | bytes 207361 | tf_op jit(solution)/shard_map/jit(_where)/select_n | solution.py:315
  42.6 0.8 %slice_bitcast_fusion = f32[2,32,180]{2,1,0:T(8,128)S(1)} fusion(f32[2,2,32,182]{3,2,1,0:T(8,128)} %bitcast.17), kind=kLoop, calls=%fused_computation.73 | loop fusion | bytes 92160 | tf_op jit(solution)/shard_map/squeeze | solution.py:321
  43.5 0.7 %select_bitcast_fusion.1 = f32[2,1,180]{2,0,1:T(2,128)S(1)} fusion(f32[2,182]{1,0:T(2,128)} %get-tuple-element.12, pred[]{:T(512)S(6)} %gt.3), kind=kLoop, calls=%fused_computation.99 | loop fusion | flops 360 | bytes 2881 | tf_op jit(solution)/shard_map/broadcast_in_dim | solution.py:327
  44.2 0.7 %select_bitcast_fusion = f32[2,1,180]{2,0,1:T(2,128)S(1)} fusion(f32[2,182]{1,0:T(2,128)} %get-tuple-element.13, pred[]{:T(512)S(6)} %lt.7), kind=kLoop, calls=%fused_computation.98 | loop fusion | flops 360 | bytes 2881 | tf_op jit(solution)/shard_map/broadcast_in_dim | solution.py:327
  44.9 0.0 copy-done
  44.9 0.0 copy-start.3
  44.9 0.0 copy-start.4
  44.9 0.0 copy-start.2
  44.9 3.6 %fusion.11 = f32[2,180,792]{2,1,0:T(8,128)} fusion(f32[2,180,768]{2,1,0:T(8,128)S(1)} %copy-done, f32[2,180,72]{2,1,0:T(8,128)S(1)} %slice_select_fusion.1, f32[2,180,72]{2,1,0:T(8,128)S(1)} %slice_select_fusion, f32[2,32,180]{2,1,0:T(8,128)S(1)} %slice_bitcast_fusion, f32[2,1,180]{2,1,0:T(1,128)S(1)} %copy.29, f32[2,1,180]{2,1,0:T(1,128)S(1)} %copy.30, ...), kind=kOutput, calls=%fused_computation.23 | convolution fusion | flops 121819896 | bytes 2506020 | tf_op jit(solution)/shard_map/ljc,jm->lcm/dot_general | solution.py:294
  48.6 0.0 copy-done.3
  48.6 0.0 copy-done.4
  48.6 0.0 copy-done.2
  48.6 0.1 fusion.73
  48.7 0.0 copy-start.1
  48.7 1.9 %fusion.30 = f32[2,181,768]{2,1,0:T(8,128)S(1)} fusion(f32[2,3,768]{2,1,0:T(4,128)S(1)} %slice.118, f32[2,3,768]{2,1,0:T(4,128)S(1)} %slice.122, f32[2,180,768]{2,1,0:T(8,128)S(1)} %copy-done, f32[2,32,180]{2,1,0:T(8,128)S(1)} %bitcast.20, f32[2,32,1]{2,1,0:T(8,128)S(1)} %get-tuple-element.21, f32[2,32,1]{2,1,0:T(8,128)S(1)} %get-tuple-element.20, ...), kind=kOutput, calls=%fused_computation.44 | convolution fusion | flops 115447552 | bytes 2304512 | tf_op jit(solution)/shard_map/ljc,jm->lcm/dot_general | solution.py:294
  50.6 0.1 broadcast.171
  50.7 0.1 reshape.64
  50.8 0.0 copy-done.1
  50.8 2.0 %fusion.33 = f32[2,180,768]{2,1,0:T(8,128)S(1)} fusion(f32[2,180,792]{2,1,0:T(8,128)} %fusion.11, f32[2,181,768]{2,1,0:T(8,128)S(1)} %fusion.30, f32[768]{0:T(1024)S(1)} %reshape.64, f32[2,180,768]{2,0,1:T(2,128)S(1)} %copy-done.1), kind=kLoop, calls=%fused_computation.48 | loop fusion | flops 1382400 | bytes 6638592 | tf_op jit(solution)/shard_map/sub | solution.py:344
  52.9 1.6 %copy.34 = f32[2,180,768]{2,0,1:T(2,128)} copy(f32[2,180,768]{2,1,0:T(8,128)S(1)} %fusion.33) | data formatting | bytes 2211840
  54.4 0.7 %copy.37 = f32[2,2,32,180]{3,2,1,0:T(8,128)} copy(f32[2,2,32,180]{3,2,1,0:T(8,128)S(1)} %bitcast.18) | data formatting | bytes 184320
  (11 shorter events, 0.2 us)
Async XLA Ops:
  3.9 41.0 %copy-start = (f32[2,180,768]{2,1,0:T(8,128)S(1)}, f32[2,180,768]{2,1,0:T(8,128)}, u32[]{:S(2)}) copy-start(f32[2,180,768]{2,1,0:T(8,128)} %copy.33.tracers_ref) | copy-start | bytes 3317764
  44.9 3.7 %copy-start.3 = (f32[2,4,768]{2,1,0:T(4,128)S(1)}, f32[2,4,768]{2,1,0:T(4,128)}, u32[]{:S(2)}) copy-start(f32[2,4,768]{2,1,0:T(4,128)} %get-tuple-element.10) | copy-start | bytes 73732
  44.9 3.7 %copy-start.4 = (f32[2,8,768]{2,1,0:T(8,128)S(1)}, f32[2,8,768]{2,1,0:T(8,128)}, u32[]{:S(2)}) copy-start(f32[2,8,768]{2,1,0:T(8,128)} %get-tuple-element.11) | copy-start | bytes 147460
  44.9 3.7 %copy-start.2 = (f32[128,182]{1,0:T(8,128)S(1)}, f32[128,182]{1,0:T(8,128)}, u32[]{:S(2)}) copy-start(f32[128,182]{1,0:T(8,128)} %get-tuple-element.9) | copy-start | bytes 279556
  48.7 2.1 %copy-start.1 = (f32[2,180,768]{2,0,1:T(2,128)S(1)}, f32[2,180,768]{2,0,1:T(2,128)}, u32[]{:S(2)}) copy-start(f32[2,180,768]{2,0,1:T(2,128)} %param.13) | copy-start | bytes 3317764

commit v6 on v5

--- a/solution.py
+++ b/solution.py
@@ -65,7 +65,7 @@
 
 def filter_kernel(n, rows, winds_ref, scaled_ref, kc_ref, ks_ref, tc_ref, ts_ref, c_ref, s_ref,
                   divisor_ref, zero_ref, widen_ref, prev_ref, next_ref, tracers_ref,
-                  out_ref, west_ref, east_ref, south_ref, north_ref, vsouth_ref, vnorth_ref,
+                  out_ref, smooth_ref, west_ref, east_ref, south_ref, north_ref, vsouth_ref, vnorth_ref,
                   gathered, restored, send_a, recv_a, send_b, recv_b, halo_send, halo_recv, local_sem):
     me = lax.axis_index("lon")
     band = lax.axis_index("lat")
@@ -80,13 +80,13 @@
         pl.semaphore_signal(barrier, inc=1, device_id=(other, me), device_id_type=MESH)
     pl.semaphore_wait(barrier, n + 1)
 
-    cols, merged = tracers_ref.shape[1], tracers_ref.shape[2]
-    lane_depth = south_ref.shape[2]
+    cols, merged = tracers_ref.shape[0], tracers_ref.shape[2]
+    depth, lane_depth = west_ref.shape[0], south_ref.shape[2]
     flat_rows = out_ref.shape[0]
     level_rows = flat_rows // 4
     halo_plan = [
-        (tracers_ref.at[:, pl.ds(cols - west_ref.shape[1], west_ref.shape[1]), :], west_ref, (band, east_peer)),
-        (tracers_ref.at[:, pl.ds(0, east_ref.shape[1]), :], east_ref, (band, west_peer)),
+        (tracers_ref.at[pl.ds(cols - depth, depth)], west_ref, (band, east_peer)),
+        (tracers_ref.at[pl.ds(0, depth)], east_ref, (band, west_peer)),
         (tracers_ref.at[:, :, pl.ds(merged - lane_depth, lane_depth)], south_ref, (up, me)),
         (tracers_ref.at[:, :, pl.ds(0, lane_depth)], north_ref, (down, me)),
     ]
@@ -185,10 +185,21 @@
     wind_halos = [halo_copy(i) for i in range(4, 8)]
     for copy in wind_halos:
         copy.start()
+    smooth_ref[...] = out_ref[:, : smooth_ref.shape[1]]
     for copy in tracer_halos + wind_halos:
         copy.wait_recv()
     for copy in tracer_halos + wind_halos:
         copy.wait_send()
+
+    @pl.when(band == 0)
+    def _():
+        south_ref[...] = jnp.zeros(south_ref.shape, jnp.float32)
+        vsouth_ref[...] = jnp.zeros(vsouth_ref.shape, jnp.float32)
+
+    @pl.when(band == bands - 1)
+    def _():
+        north_ref[...] = jnp.zeros(north_ref.shape, jnp.float32)
+        vnorth_ref[...] = jnp.zeros(vnorth_ref.shape, jnp.float32)
 
 
 def spectral_tables(n, rows, columns):
@@ -226,7 +237,7 @@
 
 def exchange_all(flat_winds, row_cosine, tracers):
     flat_rows, columns = flat_winds.shape
-    levels, lon_cols, merged = tracers.shape
+    lon_cols, levels, merged = tracers.shape
     n = lax.axis_size("lon")
     lon_index = lax.axis_index("lon")
     rows = flat_rows // n
@@ -235,14 +246,14 @@
     scaled = (own_cosine / COS_FLOOR) ** 2
     scaled = jnp.tile(scaled, n).reshape(n * rows, 1)
     vmem = pl.BlockSpec(memory_space=pltpu.VMEM)
-    west_cols = lon_cols - (lon_cols - 3) // 8 * 8
     lanes = -(-3 * tracer_count // 128) * 128
     shapes = [
         (flat_rows, columns + 2),
-        (levels, west_cols, merged),
-        (levels, 8, merged),
-        (levels, lon_cols, lanes),
-        (levels, lon_cols, lanes),
+        (flat_rows, columns),
+        (3, levels, merged),
+        (3, levels, merged),
+        (lon_cols, levels, lanes),
+        (lon_cols, levels, lanes),
         (levels, columns + 2),
         (levels, columns + 2),
     ]
@@ -291,7 +302,7 @@
 def spread(values, rows, tracer_count):
     lanes = jnp.arange(rows * tracer_count, dtype=jnp.int32) // tracer_count
     pick = (jnp.arange(rows, dtype=jnp.int32)[:, None] == lanes[None, :]).astype(jnp.float32)
-    return jnp.einsum("ljc,jm->lcm", values, pick, precision=EXACT_MODE)
+    return jnp.einsum("ljc,jm->clm", values, pick, precision=EXACT_MODE)
 
 
 def local(tracers, wind_field):
@@ -305,44 +316,42 @@
     row_cosine = jnp.cos(
         (row_ids.astype(jnp.float32) + 0.5) * (math.pi / lat_total) - 0.5 * math.pi
     )
+    columns_first = jnp.transpose(tracers, (1, 0, 2))
     flat_winds = wind_field.reshape(2 * levels * lat_rows, lon_cols)
-    wide, west, east, south, north, v_south, v_north = exchange_all(flat_winds, row_cosine, tracers)
-    has_south = band > 0
-    has_north = band < lax.axis_size("lat") - 1
-    west = west[:, west.shape[1] - 3 :]
-    east = east[:, :3]
-    south = jnp.where(has_south, south[..., south.shape[2] - 3 * tracer_count :], 0.0)
-    north = jnp.where(has_north, north[..., : 3 * tracer_count], 0.0)
-    v_south = jnp.where(has_south, v_south[:, :lon_cols], 0.0)
-    v_north = jnp.where(has_north, v_north[:, :lon_cols], 0.0)
-    wide = wide.reshape(2, levels, lat_rows, lon_cols + 2)
-    smoothed = wide[..., :lon_cols]
-    east_wide = wide[0]
+    wide, smoothed, west, east, south, north, v_south, v_north = exchange_all(
+        flat_winds, row_cosine, columns_first
+    )
+    south = south[..., south.shape[2] - 3 * tracer_count :]
+    north = north[..., : 3 * tracer_count]
+    smoothed = smoothed.reshape(2, levels, lat_rows, lon_cols)
+    east_wide = wide.reshape(2, levels, lat_rows, lon_cols + 2)[0]
     north_wind = smoothed[1]
     u_pad = jnp.concatenate(
-        [east_wide[..., lon_cols : lon_cols + 1], east_wide[..., :lon_cols], east_wide[..., lon_cols + 1 :]],
+        [east_wide[..., lon_cols : lon_cols + 1], smoothed[0], east_wide[..., lon_cols + 1 :]],
         axis=2,
     )
     zonal_speed = 0.5 * (u_pad[:, :, : lon_cols + 1] + u_pad[:, :, 1:])
-    v_pad = jnp.concatenate([v_south[:, None], north_wind, v_north[:, None]], axis=1)
+    v_pad = jnp.concatenate(
+        [v_south[:, None, :lon_cols], north_wind, v_north[:, None, :lon_cols]], axis=1
+    )
     face_ids = first_row + jnp.arange(lat_rows + 1, dtype=jnp.int32)
     face_cosine = jnp.cos(face_ids.astype(jnp.float32) * (math.pi / lat_total) - 0.5 * math.pi)
     face_cosine = jnp.where((face_ids == 0) | (face_ids == lat_total), 0.0, face_cosine)
     merid_speed = 0.5 * (v_pad[:, : lat_rows + 1] + v_pad[:, 1:]) * face_cosine[None, :, None]
     zonal_rep = spread(zonal_speed, lat_rows, tracer_count)
     merid_rep = spread(merid_speed, lat_rows + 1, tracer_count)
-    zonal_pad = jnp.concatenate([west, tracers, east], axis=1)
-    left_x, right_x = stencil(zonal_pad, 1, lon_cols + 1, 1)
+    zonal_pad = jnp.concatenate([west, columns_first, east], axis=0)
+    left_x, right_x = stencil(zonal_pad, 0, lon_cols + 1, 1)
     zonal_flux = upwind(zonal_rep, left_x, right_x)
-    merid_pad = jnp.concatenate([south, tracers, north], axis=2)
+    merid_pad = jnp.concatenate([south, columns_first, north], axis=2)
     left_y, right_y = stencil(merid_pad, 2, lat_rows + 1, tracer_count)
     merid_flux = upwind(merid_rep, left_y, right_y)
     metric = jnp.repeat(1.0 / jnp.maximum(row_cosine, COS_FLOOR), tracer_count)
-    change = COURANT * (zonal_flux[:, 1:] - zonal_flux[:, :-1]) + COURANT * (
+    change = COURANT * (zonal_flux[1:] - zonal_flux[:-1]) + COURANT * (
         merid_flux[:, :, tracer_count:] - merid_flux[:, :, :-tracer_count]
     )
-    advected = tracers - metric[None, None, :] * change
-    return (advected, smoothed)
+    advected = columns_first - metric[None, None, :] * change
+    return (jnp.transpose(advected, (1, 0, 2)), smoothed)
 
 
 def solution(mesh):

time: 55.4 us -> 60.5 us (1.092)
  other arithmetic: 5.56 us -> 16.2 us
  matrix products: 5.54 us -> 1.56 us
  local copies, waits for them, and re-layouts: 6.48 us -> 5.26 us
    add x0 -> x2, other arithmetic: none -> 13.5 us  [upwind(): return jnp.maximum(speed, 0.0) * left + jnp.minimum(speed, 0.0) * right]
    dot_general x2, matrix products: 5.54 us -> 1.56 us  [spread(): return jnp.einsum('ljc,jm->clm', values, pick, precision=EXACT_MODE)]
    unnamed x13, local copies, waits for them, and re-layouts: 4.56 us -> 0.68 us
    transpose x0 -> x1, other arithmetic: none -> 2.46 us  [local(): return (jnp.transpose(advected, (1, 0, 2)), smoothed)]
    slice x3, local copies, waits for them, and re-layouts: 0.02 us -> 2.17 us  [the longest x1 1.28 us: local(): south = south[..., south.shape[2] - 3 * tracer_count:]]
    sub x1 -> x0, other arithmetic: 2.05 us -> none  [local(): advected = tracers - metric[None, None, :] * change]
    select_n x2 -> x0, other arithmetic: 1.98 us -> none  [the longest x1 1.04 us: local(): jnp.where(has_south, south[..., south.shape[2] - 3 * tracer_count:], 0.0)]
    broadcast_in_dim x2 -> x4, local copies, waits for them, and re-layouts: 0.01 us -> 1.37 us  [the longest x2 0.69 us: local(): v_south[:, None, :lon_cols]]
where the time goes in v6:
time: 60.5 us; the launch traced here: 60.3 us
  Pallas kernels  36.5 us (60%)
  other arithmetic  16.2 us (27%)
  local copies, waits for them, and re-layouts  5.26 us (9%)
  matrix products  1.56 us (3%)
  between operations  0.8 us (1%)
    pallas_call x1, Pallas kernels, exchange_all(): pl.pallas_call(functools.partial(filter_kernel, n, rows), out_shape=[jax....  36.5 us
    add x2, other arithmetic, upwind(): return jnp.maximum(speed, 0.0) * left + jnp.minimum(speed, 0.0) * right  13.5 us
    transpose x1, other arithmetic, local(): return (jnp.transpose(advected, (1, 0, 2)), smoothed)  2.46 us
    dot_general x2, matrix products, spread(): return jnp.einsum('ljc,jm->clm', values, pick, precision=EXACT_MODE)  1.56 us
    slice x1, local copies, waits for them, and re-layouts, local(): south = south[..., south.shape[2] - 3 * tracer_count:]  1.28 us

profile of v6, /device:TPU:1, one launch (start us, length us, event | category | flops | bytes accessed | tf_op | source)
XLA Modules:
  0.0 60.3 jit_solution(13966047842405875178)
XLA Ops:
  0.7 0.1 tile.7
  0.8 0.1 multiply_multiply_fusion
  0.9 0.7 %reshape_tile.4.scaled_ref = f32[128,1]{1,0:T(8,128)} reshape(f32[16,8]{1,0:T(8,128)S(1)} %tile.8) | data formatting | bytes 1024 | tf_op jit(solution)/shard_map/reshape;tile | solution.py:247
  1.6 36.5 %shard_map.140 = (f32[128,182]{1,0:T(8,128)}, f32[128,180]{1,0:T(8,128)}, f32[3,2,768]{2,1,0:T(2,128)}, f32[3,2,768]{2,1,0:T(2,128)}, f32[180,2,128]{2,1,0:T(2,1...) custom-call(f32[128,180]{1,0:T(8,128)} %bitcast.44, f32[128,1]{1,0:T(8,128)} %reshape_tile.4.scaled_ref, ...), custom_call_target="tpu_custom_call" | custom-call | tf_op jit(solution)/shard_map/pallas_call | solution.py:260
  38.0 0.0 copy-start
  38.1 0.0 copy-start.2
  38.1 1.3 %slice.121 = f32[180,2,72]{2,1,0:T(2,128)S(1)} slice(f32[180,2,128]{2,1,0:T(2,128)} %get-tuple-element.16), slice={[0:180], [0:2], [56:128]} | slice | bytes 207360 | tf_op jit(solution)/shard_map/slice | solution.py:324
  39.3 0.9 %fusion.66 = (f32[64,180]{1,0:T(8,128)S(1)}, f32[64,180]{1,0:T(8,128)S(1)}) fusion(f32[128,180]{1,0:T(8,128)} %get-tuple-element.11), kind=kLoop, calls=%fused_computation.98 | loop fusion | bytes 184320 | tf_op jit(solution)/shard_map/slice | solution.py:330
  40.2 0.7 %slice_bitcast_fusion.1 = f32[2,1,180]{2,0,1:T(2,128)S(1)} fusion(f32[2,182]{1,0:T(2,128)} %get-tuple-element.14), kind=kLoop, calls=%fused_computation.89 | loop fusion | bytes 2880 | tf_op jit(solution)/shard_map/broadcast_in_dim | solution.py:335
  40.9 0.7 %slice_bitcast_fusion = f32[2,1,180]{2,0,1:T(2,128)S(1)} fusion(f32[2,182]{1,0:T(2,128)} %get-tuple-element.15), kind=kLoop, calls=%fused_computation.88 | loop fusion | bytes 2880 | tf_op jit(solution)/shard_map/broadcast_in_dim | solution.py:335
  41.7 0.8 %fusion.33 = f32[792,2,180]{0,2,1:T(8,128)S(1)} fusion(f32[2,32,180]{2,1,0:T(8,128)S(1)} %bitcast.41, f32[2,1,180]{2,1,0:T(1,128)S(1)} %copy.25, f32[2,1,180]{2,1,0:T(1,128)S(1)} %copy.26, s32[792]{0:T(1024)S(1)} %add_select_fusion, f32[33]{0:T(128)S(1)} %fusion.62), kind=kOutput, calls=%fused_computation.52 | convolution fusion | flops 112981176 | bytes 1192740 | tf_op jit(solution)/shard_map/ljc,jm->clm/dot_general | solution.py:305
  42.5 0.0 copy-done
  42.5 0.0 copy-done.2
  42.5 0.0 copy-start.3
  42.5 8.9 %fusion.13 = f32[180,2,792]{2,1,0:T(2,128)S(1)} fusion(f32[180,2,72]{2,1,0:T(2,128)S(1)} %bitcast.43, f32[180,2,768]{2,1,0:T(2,128)S(1)} %bitcast.37, f32[180,2,72]{2,1,0:T(2,128)S(1)} %slice.121, f32[792,2,180]{0,2,1:T(8,128)S(1)} %fusion.33), kind=kLoop, calls=%fused_computation.24 | loop fusion | flops 8838720 | bytes 3594240 | tf_op jit(solution)/shard_map/add | solution.py:63
  51.5 0.0 copy-start.4
  51.5 0.0 copy-start.5
  51.5 0.0 copy-done.3
  51.5 0.1 fusion.67
  51.6 0.7 %fusion.36 = f32[768,2,181]{0,2,1:T(8,128)S(1)} fusion(f32[2,32,180]{2,1,0:T(8,128)S(1)} %bitcast.40, f32[2,32,1]{2,1,0:T(8,128)S(1)} %get-tuple-element.21, f32[2,32,1]{2,1,0:T(8,128)S(1)} %get-tuple-element.20, s32[768]{0:T(1024)S(1)} %add_select_fusion.1), kind=kOutput, calls=%fused_computation.55 | convolution fusion | flops 106829056 | bytes 1161728 | tf_op jit(solution)/shard_map/ljc,jm->clm/dot_general | solution.py:305
  52.4 0.0 copy-done.4
  52.4 0.0 copy-done.5
  52.4 4.6 %fusion.27 = f32[181,2,768]{2,1,0:T(2,128)S(1)} fusion(f32[3,2,768]{2,1,0:T(2,128)S(1)} %copy-done.5, f32[180,2,768]{2,1,0:T(2,128)S(1)} %bitcast.38, f32[3,2,768]{2,1,0:T(2,128)S(1)} %copy-done.4, f32[768,2,181]{0,2,1:T(8,128)S(1)} %fusion.36), kind=kLoop, calls=%fused_computation.42 | loop fusion | flops 8618496 | bytes 3366912 | tf_op jit(solution)/shard_map/add | solution.py:63
  57.0 0.1 broadcast.177
  57.1 0.1 reshape.69
  57.1 0.0 copy-start.1
  57.2 2.5 %fusion.31 = f32[2,180,768]{2,0,1:T(2,128)} fusion(f32[180,2,792]{2,1,0:T(2,128)S(1)} %fusion.13, f32[181,2,768]{2,1,0:T(2,128)S(1)} %fusion.27, f32[768]{0:T(1024)S(1)} %reshape.69, f32[2,180,768]{2,0,1:T(2,128)S(1)} %copy-done), kind=kLoop, calls=%fused_computation.49 | loop fusion | flops 1382400 | bytes 6638592 | tf_op jit(solution)/shard_map/transpose | solution.py:354
  59.6 0.0 copy-done.1
  59.6 0.7 %copy.32 = f32[2,2,32,180]{3,2,1,0:T(8,128)} copy(f32[2,2,32,180]{3,2,1,0:T(8,128)S(1)} %bitcast.39) | data formatting | bytes 184320
  (9 shorter events, 0.1 us)
Async XLA Ops:
  38.0 4.4 %copy-start = (f32[2,180,768]{2,0,1:T(2,128)S(1)}, f32[2,180,768]{2,0,1:T(2,128)}, u32[]{:S(2)}) copy-start(f32[2,180,768]{2,0,1:T(2,128)} %param.13) | copy-start | bytes 3317764
  38.1 4.4 %copy-start.2 = (f32[180,2,128]{2,1,0:T(2,128)S(1)}, f32[180,2,128]{2,1,0:T(2,128)}, u32[]{:S(2)}) copy-start(f32[180,2,128]{2,1,0:T(2,128)} %get-tuple-element.17) | copy-start | bytes 552964
  42.5 9.0 %copy-start.3 = (f32[128,182]{1,0:T(8,128)S(1)}, f32[128,182]{1,0:T(8,128)}, u32[]{:S(2)}) copy-start(f32[128,182]{1,0:T(8,128)} %get-tuple-element.10) | copy-start | bytes 279556
  51.5 0.9 %copy-start.4 = (f32[3,2,768]{2,1,0:T(2,128)S(1)}, f32[3,2,768]{2,1,0:T(2,128)}, u32[]{:S(2)}) copy-start(f32[3,2,768]{2,1,0:T(2,128)} %get-tuple-element.12) | copy-start | bytes 55300
  51.5 0.9 %copy-start.5 = (f32[3,2,768]{2,1,0:T(2,128)S(1)}, f32[3,2,768]{2,1,0:T(2,128)}, u32[]{:S(2)}) copy-start(f32[3,2,768]{2,1,0:T(2,128)} %get-tuple-element.13) | copy-start | bytes 55300
  57.1 2.5 %copy-start.1 = (f32[128,180]{1,0:T(8,128)S(1)}, f32[128,180]{1,0:T(8,128)}, u32[]{:S(2)}) copy-start(f32[128,180]{1,0:T(8,128)} %get-tuple-element.11) | copy-start | bytes 276484

commit v7 on v5

--- a/solution.py
+++ b/solution.py
@@ -65,7 +65,7 @@
 
 def filter_kernel(n, rows, winds_ref, scaled_ref, kc_ref, ks_ref, tc_ref, ts_ref, c_ref, s_ref,
                   divisor_ref, zero_ref, widen_ref, prev_ref, next_ref, tracers_ref,
-                  out_ref, west_ref, east_ref, south_ref, north_ref, vsouth_ref, vnorth_ref,
+                  out_ref, smooth_ref, west_ref, east_ref, south_ref, north_ref, vsouth_ref, vnorth_ref,
                   gathered, restored, send_a, recv_a, send_b, recv_b, halo_send, halo_recv, local_sem):
     me = lax.axis_index("lon")
     band = lax.axis_index("lat")
@@ -185,10 +185,21 @@
     wind_halos = [halo_copy(i) for i in range(4, 8)]
     for copy in wind_halos:
         copy.start()
+    smooth_ref[...] = out_ref[:, : smooth_ref.shape[1]]
     for copy in tracer_halos + wind_halos:
         copy.wait_recv()
     for copy in tracer_halos + wind_halos:
         copy.wait_send()
+
+    @pl.when(band == 0)
+    def _():
+        south_ref[...] = jnp.zeros(south_ref.shape, jnp.float32)
+        vsouth_ref[...] = jnp.zeros(vsouth_ref.shape, jnp.float32)
+
+    @pl.when(band == bands - 1)
+    def _():
+        north_ref[...] = jnp.zeros(north_ref.shape, jnp.float32)
+        vnorth_ref[...] = jnp.zeros(vnorth_ref.shape, jnp.float32)
 
 
 def spectral_tables(n, rows, columns):
@@ -239,6 +250,7 @@
     lanes = -(-3 * tracer_count // 128) * 128
     shapes = [
         (flat_rows, columns + 2),
+        (flat_rows, columns),
         (levels, west_cols, merged),
         (levels, 8, merged),
         (levels, lon_cols, lanes),
@@ -306,21 +318,20 @@
         (row_ids.astype(jnp.float32) + 0.5) * (math.pi / lat_total) - 0.5 * math.pi
     )
     flat_winds = wind_field.reshape(2 * levels * lat_rows, lon_cols)
-    wide, west, east, south, north, v_south, v_north = exchange_all(flat_winds, row_cosine, tracers)
-    has_south = band > 0
-    has_north = band < lax.axis_size("lat") - 1
+    wide, smoothed, west, east, south, north, v_south, v_north = exchange_all(
+        flat_winds, row_cosine, tracers
+    )
     west = west[:, west.shape[1] - 3 :]
     east = east[:, :3]
-    south = jnp.where(has_south, south[..., south.shape[2] - 3 * tracer_count :], 0.0)
-    north = jnp.where(has_north, north[..., : 3 * tracer_count], 0.0)
-    v_south = jnp.where(has_south, v_south[:, :lon_cols], 0.0)
-    v_north = jnp.where(has_north, v_north[:, :lon_cols], 0.0)
-    wide = wide.reshape(2, levels, lat_rows, lon_cols + 2)
-    smoothed = wide[..., :lon_cols]
-    east_wide = wide[0]
+    south = south[..., south.shape[2] - 3 * tracer_count :]
+    north = north[..., : 3 * tracer_count]
+    v_south = v_south[:, :lon_cols]
+    v_north = v_north[:, :lon_cols]
+    smoothed = smoothed.reshape(2, levels, lat_rows, lon_cols)
+    east_wide = wide.reshape(2, levels, lat_rows, lon_cols + 2)[0]
     north_wind = smoothed[1]
     u_pad = jnp.concatenate(
-        [east_wide[..., lon_cols : lon_cols + 1], east_wide[..., :lon_cols], east_wide[..., lon_cols + 1 :]],
+        [east_wide[..., lon_cols : lon_cols + 1], smoothed[0], east_wide[..., lon_cols + 1 :]],
         axis=2,
     )
     zonal_speed = 0.5 * (u_pad[:, :, : lon_cols + 1] + u_pad[:, :, 1:])

time: 55.4 us -> 55.7 us (level)
  other arithmetic: 5.56 us -> 2.22 us
  local copies, waits for them, and re-layouts: 6.48 us -> 8.91 us
  matrix products: 5.54 us -> 6.62 us
    select_n x2 -> x0, other arithmetic: 1.98 us -> none  [the longest x1 1.04 us: local(): jnp.where(has_south, south[..., south.shape[2] - 3 * tracer_count:], 0.0)]
    slice x1 -> x3, local copies, waits for them, and re-layouts: 0.01 us -> 1.92 us  [the longest x1 1.03 us: local(): south = south[..., south.shape[2] - 3 * tracer_count:]]
    broadcast_in_dim x2 -> x0, other arithmetic: 1.34 us -> none  [the longest x1 0.68 us: local(): v_south[:, None]]
    dot_general x2, matrix products: 5.54 us -> 6.62 us  [spread(): return jnp.einsum('ljc,jm->lcm', values, pick, precision=EXACT_MODE)]
    squeeze x1 -> x0, local copies, waits for them, and re-layouts: 0.85 us -> none  [local(): north_wind = smoothed[1]]
    broadcast_in_dim x1 -> x2, local copies, waits for them, and re-layouts: 0.01 us -> 0.68 us  [local(): v_north[:, None]]
    broadcast_in_dim x1 -> x2, local copies, waits for them, and re-layouts: 0.01 us -> 0.68 us  [local(): v_south[:, None]]
    unnamed x13 -> x15, local copies, waits for them, and re-layouts: 4.56 us -> 4.57 us
where the time goes in v7:
time: 55.7 us; the launch traced here: 55.3 us
  Pallas kernels  36.8 us (66%)
  local copies, waits for them, and re-layouts  8.91 us (16%)
  matrix products  6.62 us (12%)
  other arithmetic  2.22 us (4%)
  between operations  0.78 us (1%)
    pallas_call x1, Pallas kernels, exchange_all(): pl.pallas_call(functools.partial(filter_kernel, n, rows), out_shape=[jax....  36.8 us
    dot_general x2, matrix products, spread(): return jnp.einsum('ljc,jm->lcm', values, pick, precision=EXACT_MODE)  6.62 us
    unnamed x15, local copies, waits for them, and re-layouts  4.57 us
    sub x1, other arithmetic, local(): advected = tracers - metric[None, None, :] * change  2.02 us

profile of v7, /device:TPU:1, one launch (start us, length us, event | category | flops | bytes accessed | tf_op | source)
XLA Modules:
  0.0 55.3 jit_solution(9497171129469186799)
XLA Ops:
  0.6 2.3 %copy.33.tracers_ref = f32[2,180,768]{2,1,0:T(8,128)} copy(f32[2,180,768]{2,0,1:T(2,128)} %param.13) | data formatting | bytes 2211840 | tf_op args[0]
  3.0 0.1 tile.7
  3.1 0.1 multiply_multiply_fusion
  3.2 0.7 %reshape_tile.4.scaled_ref = f32[128,1]{1,0:T(8,128)} reshape(f32[16,8]{1,0:T(8,128)S(1)} %tile.8) | data formatting | bytes 1024 | tf_op jit(solution)/shard_map/reshape;tile | solution.py:247
  3.9 0.0 copy-start
  3.9 36.8 %shard_map.140 = (f32[128,182]{1,0:T(8,128)}, f32[128,180]{1,0:T(8,128)}, f32[2,4,768]{2,1,0:T(4,128)}, f32[2,8,768]{2,1,0:T(8,128)}, f32[2,180,128]{2,1,0:T(8,1...) custom-call(f32[128,180]{1,0:T(8,128)} %bitcast.18, f32[128,1]{1,0:T(8,128)} %reshape_tile.4.scaled_ref, ...), custom_call_target="tpu_custom_call" | custom-call | tf_op jit(solution)/shard_map/pallas_call | solution.py:261
  40.7 1.0 %slice.129 = f32[2,180,72]{2,1,0:T(8,128)S(1)} slice(f32[2,180,128]{2,1,0:T(8,128)} %get-tuple-element.16), slice={[0:2], [0:180], [56:128]} | slice | bytes 207360 | tf_op jit(solution)/shard_map/slice | solution.py:326
  41.7 0.9 %fusion.73 = (f32[64,180]{1,0:T(8,128)S(1)}, f32[64,180]{1,0:T(8,128)S(1)}) fusion(f32[128,180]{1,0:T(8,128)} %get-tuple-element.11), kind=kLoop, calls=%fused_computation.105 | loop fusion | bytes 184320 | tf_op jit(solution)/shard_map/slice | solution.py:334
  42.6 0.7 %slice_bitcast_fusion.1 = f32[2,1,180]{2,0,1:T(2,128)S(1)} fusion(f32[2,182]{1,0:T(2,128)} %get-tuple-element.14), kind=kLoop, calls=%fused_computation.96 | loop fusion | bytes 2880 | tf_op jit(solution)/shard_map/broadcast_in_dim | solution.py:338
  43.3 0.7 %slice_bitcast_fusion = f32[2,1,180]{2,0,1:T(2,128)S(1)} fusion(f32[2,182]{1,0:T(2,128)} %get-tuple-element.15), kind=kLoop, calls=%fused_computation.95 | loop fusion | bytes 2880 | tf_op jit(solution)/shard_map/broadcast_in_dim | solution.py:338
  44.1 0.0 copy-done
  44.1 0.0 copy-start.4
  44.1 0.0 copy-start.5
  44.1 0.0 copy-start.3
  44.1 4.7 %fusion.11 = f32[2,180,792]{2,1,0:T(8,128)} fusion(f32[2,180,768]{2,1,0:T(8,128)S(1)} %copy-done, f32[2,180,72]{2,1,0:T(8,128)S(1)} %slice.129, f32[2,180,72]{2,1,0:T(8,128)} %bitcast.21, f32[2,32,180]{2,1,0:T(8,128)S(1)} %bitcast.20, f32[2,1,180]{2,1,0:T(1,128)S(1)} %copy.29, f32[2,1,180]{2,1,0:T(1,128)S(1)} %copy.30, s32[792]{0:T(1024)S(1)} %add_select_fusion, ...), kind=kOutput, calls=%fused_computation.23 | convolution fusion | flops 121819896 | bytes 2506020 | tf_op jit(solution)/shard_map/ljc,jm->lcm/dot_general | solution.py:306
  48.8 0.0 copy-done.4
  48.8 0.0 copy-done.5
  48.9 0.0 copy-done.3
  48.9 0.1 fusion.74
  49.0 0.0 copy-start.1
  49.0 1.9 %fusion.30 = f32[2,181,768]{2,1,0:T(8,128)S(1)} fusion(f32[2,3,768]{2,1,0:T(4,128)S(1)} %slice.116, f32[2,3,768]{2,1,0:T(4,128)S(1)} %slice.120, f32[2,180,768]{2,1,0:T(8,128)S(1)} %copy-done, f32[2,32,180]{2,1,0:T(8,128)S(1)} %bitcast.19, f32[2,32,1]{2,1,0:T(8,128)S(1)} %get-tuple-element.25, f32[2,32,1]{2,1,0:T(8,128)S(1)} %get-tuple-element.24, ...), kind=kOutput, calls=%fused_computation.44 | convolution fusion | flops 115447552 | bytes 2304512 | tf_op jit(solution)/shard_map/ljc,jm->lcm/dot_general | solution.py:306
  50.9 0.1 broadcast.171
  51.0 0.1 reshape.69
  51.1 0.0 copy-done.1
  51.1 2.0 %fusion.33 = f32[2,180,768]{2,1,0:T(8,128)S(1)} fusion(f32[2,180,792]{2,1,0:T(8,128)} %fusion.11, f32[2,181,768]{2,1,0:T(8,128)S(1)} %fusion.30, f32[768]{0:T(1024)S(1)} %reshape.69, f32[2,180,768]{2,0,1:T(2,128)S(1)} %copy-done.1), kind=kLoop, calls=%fused_computation.48 | loop fusion | flops 1382400 | bytes 6638592 | tf_op jit(solution)/shard_map/sub | solution.py:355
  53.1 0.0 copy-start.2
  53.1 1.6 %copy.34 = f32[2,180,768]{2,0,1:T(2,128)} copy(f32[2,180,768]{2,1,0:T(8,128)S(1)} %fusion.33) | data formatting | bytes 2211840
  54.7 0.0 copy-done.2
  54.7 0.7 %copy.37 = f32[2,2,32,180]{3,2,1,0:T(8,128)} copy(f32[2,2,32,180]{3,2,1,0:T(8,128)S(1)} %bitcast.16) | data formatting | bytes 184320
  (11 shorter events, 0.2 us)
Async XLA Ops:
  3.9 40.2 %copy-start = (f32[2,180,768]{2,1,0:T(8,128)S(1)}, f32[2,180,768]{2,1,0:T(8,128)}, u32[]{:S(2)}) copy-start(f32[2,180,768]{2,1,0:T(8,128)} %copy.33.tracers_ref) | copy-start | bytes 3317764
  44.1 4.8 %copy-start.4 = (f32[2,4,768]{2,1,0:T(4,128)S(1)}, f32[2,4,768]{2,1,0:T(4,128)}, u32[]{:S(2)}) copy-start(f32[2,4,768]{2,1,0:T(4,128)} %get-tuple-element.12) | copy-start | bytes 73732
  44.1 4.8 %copy-start.5 = (f32[2,8,768]{2,1,0:T(8,128)S(1)}, f32[2,8,768]{2,1,0:T(8,128)}, u32[]{:S(2)}) copy-start(f32[2,8,768]{2,1,0:T(8,128)} %get-tuple-element.13) | copy-start | bytes 147460
  44.1 4.8 %copy-start.3 = (f32[128,182]{1,0:T(8,128)S(1)}, f32[128,182]{1,0:T(8,128)}, u32[]{:S(2)}) copy-start(f32[128,182]{1,0:T(8,128)} %get-tuple-element.10) | copy-start | bytes 279556
  49.0 2.1 %copy-start.1 = (f32[2,180,768]{2,0,1:T(2,128)S(1)}, f32[2,180,768]{2,0,1:T(2,128)}, u32[]{:S(2)}) copy-start(f32[2,180,768]{2,0,1:T(2,128)} %param.13) | copy-start | bytes 3317764
  53.1 1.6 %copy-start.2 = (f32[128,180]{1,0:T(8,128)S(1)}, f32[128,180]{1,0:T(8,128)}, u32[]{:S(2)}) copy-start(f32[128,180]{1,0:T(8,128)} %get-tuple-element.11) | copy-start | bytes 276484

commit v8 on v7

--- a/solution.py
+++ b/solution.py
@@ -66,24 +66,33 @@
 def filter_kernel(n, rows, winds_ref, scaled_ref, kc_ref, ks_ref, tc_ref, ts_ref, c_ref, s_ref,
                   divisor_ref, zero_ref, widen_ref, prev_ref, next_ref, tracers_ref,
                   out_ref, smooth_ref, west_ref, east_ref, south_ref, north_ref, vsouth_ref, vnorth_ref,
-                  gathered, restored, send_a, recv_a, send_b, recv_b, halo_send, halo_recv, local_sem):
+                  stage_a, gathered, restored, stage_b, chip_send, chip_recv, pair_send, pair_recv,
+                  halo_send, halo_recv, local_sem):
     me = lax.axis_index("lon")
     band = lax.axis_index("lat")
     bands = lax.axis_size("lat")
+    pair = 2
+    chips = n // pair
+    chip, core = me // pair, me % pair
+    partner = chip * pair + (1 - core)
+    cross = lax.rem(me + 2 * core - 1 + n, n)
     up, down = lax.rem(band + 1, bands), lax.rem(band + bands - 1, bands)
     east_peer, west_peer = lax.rem(me + 1, n), lax.rem(me + n - 1, n)
     barrier = pltpu.get_barrier_semaphore()
-    for k in range(1, n):
-        peer = lax.rem(me + k, n)
-        pl.semaphore_signal(barrier, inc=1, device_id=(band, peer), device_id_type=MESH)
-    for other in (up, down):
-        pl.semaphore_signal(barrier, inc=1, device_id=(other, me), device_id_type=MESH)
-    pl.semaphore_wait(barrier, n + 1)
+    for k in range(1, chips):
+        other = lax.rem(chip + k, chips) * pair + core
+        pl.semaphore_signal(barrier, inc=1, device_id=(band, other), device_id_type=MESH)
+    for device in ((band, partner), (band, cross), (up, me), (down, me)):
+        pl.semaphore_signal(barrier, inc=1, device_id=device, device_id_type=MESH)
+    pl.semaphore_wait(barrier, chips + 3)
 
     cols, merged = tracers_ref.shape[1], tracers_ref.shape[2]
     lane_depth = south_ref.shape[2]
-    flat_rows = out_ref.shape[0]
+    flat_rows = n * rows
     level_rows = flat_rows // 4
+
+    def flat_row(ref, index):
+        return ref.at[index // (pair * rows), (index // rows) % pair, pl.ds(index % rows, 1)]
     halo_plan = [
         (tracers_ref.at[:, pl.ds(cols - west_ref.shape[1], west_ref.shape[1]), :], west_ref, (band, east_peer)),
         (tracers_ref.at[:, pl.ds(0, east_ref.shape[1]), :], east_ref, (band, west_peer)),
@@ -93,11 +102,11 @@
     for level in range(2):
         first = 2 * level_rows + level * level_rows
         halo_plan.append(
-            (out_ref.at[pl.ds(first + level_rows - 1, 1)], vsouth_ref.at[pl.ds(level, 1)], (up, me))
+            (flat_row(out_ref, first + level_rows - 1), vsouth_ref.at[pl.ds(level, 1)], (up, me))
         )
     for level in range(2):
         first = 2 * level_rows + level * level_rows
-        halo_plan.append((out_ref.at[pl.ds(first, 1)], vnorth_ref.at[pl.ds(level, 1)], (down, me)))
+        halo_plan.append((flat_row(out_ref, first), vnorth_ref.at[pl.ds(level, 1)], (down, me)))
 
     def halo_copy(index):
         source, target, device = halo_plan[index]
@@ -110,52 +119,69 @@
             device_id_type=MESH,
         )
 
-    def block(ref, index):
-        return ref.at[pl.ds(pl.multiple_of(index * rows, rows), rows)]
-
-    def swap(source, target, send_sem, recv_sem, slot):
+    def chip_rows(ref, index):
+        return ref.at[index]
+
+    def swap(source, stage, target, phase):
         sends = []
-        for k in range(1, n):
-            peer = lax.rem(me + k, n)
+        for k in range(1, chips):
+            other = lax.rem(chip + k, chips)
             copy = pltpu.make_async_remote_copy(
-                src_ref=block(source, peer),
-                dst_ref=block(target, me),
-                send_sem=send_sem.at[peer],
-                recv_sem=recv_sem.at[me],
-                device_id=(band, peer),
+                src_ref=chip_rows(source, other),
+                dst_ref=stage.at[chip],
+                send_sem=chip_send.at[phase, other],
+                recv_sem=chip_recv.at[phase, chip],
+                device_id=(band, other * pair + core),
                 device_id_type=MESH,
             )
             copy.start()
             sends.append(copy)
-        own = pltpu.make_async_copy(block(source, me), block(target, me), local_sem.at[slot])
+        own = pltpu.make_async_copy(chip_rows(source, chip), stage.at[chip], local_sem.at[phase, 0])
         own.start()
-        return sends, own
-
-    def settle(source, target, send_sem, recv_sem, sends, own):
         own.wait()
-        for k in range(1, n):
-            origin = lax.rem(me + n - k, n)
+        for k in range(1, chips):
+            origin = lax.rem(chip + chips - k, chips)
             pltpu.make_async_remote_copy(
-                src_ref=block(source, origin),
-                dst_ref=block(target, origin),
-                send_sem=send_sem.at[origin],
-                recv_sem=recv_sem.at[origin],
-                device_id=(band, origin),
+                src_ref=chip_rows(source, origin),
+                dst_ref=stage.at[origin],
+                send_sem=chip_send.at[phase, origin],
+                recv_sem=chip_recv.at[phase, origin],
+                device_id=(band, origin * pair + core),
                 device_id_type=MESH,
             ).wait_recv()
+        across = pltpu.make_async_remote_copy(
+            src_ref=stage.at[:, 1 - core],
+            dst_ref=target.at[:, core],
+            send_sem=pair_send.at[phase],
+            recv_sem=pair_recv.at[phase],
+            device_id=(band, partner),
+            device_id_type=MESH,
+        )
+        across.start()
+        keep = pltpu.make_async_copy(stage.at[:, core], target.at[:, core], local_sem.at[phase, 1])
+        keep.start()
+        keep.wait()
+        pltpu.make_async_remote_copy(
+            src_ref=stage.at[:, core],
+            dst_ref=target.at[:, 1 - core],
+            send_sem=pair_send.at[phase],
+            recv_sem=pair_recv.at[phase],
+            device_id=(band, partner),
+            device_id_type=MESH,
+        ).wait_recv()
         for copy in sends:
             copy.wait_send()
-
-    sends, own = swap(winds_ref, gathered, send_a, recv_a, 0)
+        across.wait_send()
+
     tracer_halos = [halo_copy(i) for i in range(4)]
     for copy in tracer_halos:
         copy.start()
-    settle(winds_ref, gathered, send_a, recv_a, sends, own)
+    swap(winds_ref, stage_a, gathered, 0)
 
     def mm(a, b):
         return jnp.dot(a, b, precision=EXACT_MODE, preferred_element_type=jnp.float32)
 
-    x = gathered[...]
+    x = gathered[...].reshape(flat_rows, -1)
     kc, ks = kc_ref[...], ks_ref[...]
     tc, ts = tc_ref[...], ts_ref[...]
     c, s = c_ref[...], s_ref[...]
@@ -179,13 +205,12 @@
         mm(result, widen_ref[...])
         + mm(jnp.roll(result, rows, axis=0), prev_ref[...])
         + mm(jnp.roll(result, -rows, axis=0), next_ref[...])
-    )
-    sends, own = swap(restored, out_ref, send_b, recv_b, 1)
-    settle(restored, out_ref, send_b, recv_b, sends, own)
+    ).reshape(restored.shape)
+    swap(restored, stage_b, out_ref, 1)
+    smooth_ref[...] = out_ref[..., : smooth_ref.shape[3]]
     wind_halos = [halo_copy(i) for i in range(4, 8)]
     for copy in wind_halos:
         copy.start()
-    smooth_ref[...] = out_ref[:, : smooth_ref.shape[1]]
     for copy in tracer_halos + wind_halos:
         copy.wait_recv()
     for copy in tracer_halos + wind_halos:
@@ -249,8 +274,8 @@
     west_cols = lon_cols - (lon_cols - 3) // 8 * 8
     lanes = -(-3 * tracer_count // 128) * 128
     shapes = [
-        (flat_rows, columns + 2),
-        (flat_rows, columns),
+        (n // 2, 2, rows, columns + 2),
+        (n // 2, 2, rows, columns),
         (levels, west_cols, merged),
         (levels, 8, merged),
         (levels, lon_cols, lanes),
@@ -264,18 +289,20 @@
         in_specs=[vmem] * 13 + [pl.BlockSpec(memory_space=pl.ANY)],
         out_specs=[vmem] * len(shapes),
         scratch_shapes=[
-            pltpu.VMEM((flat_rows, columns), jnp.float32),
-            pltpu.VMEM((flat_rows, columns + 2), jnp.float32),
-            pltpu.SemaphoreType.DMA((n,)),
-            pltpu.SemaphoreType.DMA((n,)),
-            pltpu.SemaphoreType.DMA((n,)),
-            pltpu.SemaphoreType.DMA((n,)),
+            pltpu.VMEM((n // 2, 2, rows, columns), jnp.float32),
+            pltpu.VMEM((n // 2, 2, rows, columns), jnp.float32),
+            pltpu.VMEM((n // 2, 2, rows, columns + 2), jnp.float32),
+            pltpu.VMEM((n // 2, 2, rows, columns + 2), jnp.float32),
+            pltpu.SemaphoreType.DMA((2, n // 2)),
+            pltpu.SemaphoreType.DMA((2, n // 2)),
+            pltpu.SemaphoreType.DMA((2,)),
+            pltpu.SemaphoreType.DMA((2,)),
             pltpu.SemaphoreType.DMA((8,)),
             pltpu.SemaphoreType.DMA((8,)),
-            pltpu.SemaphoreType.DMA((2,)),
+            pltpu.SemaphoreType.DMA((2, 2)),
         ],
         compiler_params=pltpu.CompilerParams(collective_id=0, has_side_effects=True),
-    )(flat_winds, scaled, *spectral_tables(n, rows, columns), tracers)
+    )(flat_winds.reshape(n // 2, 2, rows, columns), scaled, *spectral_tables(n, rows, columns), tracers)
 
 
 def stencil(padded, dim, faces, stride):

time: 55.7 us -> 57.3 us (1.029)
  Pallas kernels: 36.8 us -> 38.4 us
    pallas_call x1, Pallas kernels: 36.8 us -> 38.4 us  [exchange_all(): pl.pallas_call(functools.partial(filter_kernel, n, rows), out_shape=[jax....]
where the time goes in v8:
time: 57.3 us; the launch traced here: 57 us
  Pallas kernels  38.4 us (67%)
  local copies, waits for them, and re-layouts  8.91 us (16%)
  matrix products  6.62 us (12%)
  other arithmetic  2.22 us (4%)
  between operations  0.78 us (1%)
    pallas_call x1, Pallas kernels, exchange_all(): pl.pallas_call(functools.partial(filter_kernel, n, rows), out_shape=[jax....  38.4 us
    dot_general x2, matrix products, spread(): return jnp.einsum('ljc,jm->lcm', values, pick, precision=EXACT_MODE)  6.62 us
    unnamed x15, local copies, waits for them, and re-layouts  4.57 us
    sub x1, other arithmetic, local(): advected = tracers - metric[None, None, :] * change  2.02 us

profile of v8, /device:TPU:1, one launch (start us, length us, event | category | flops | bytes accessed | tf_op | source)
XLA Modules:
  0.0 57.0 jit_solution(14165395119986988904)
XLA Ops:
  0.6 2.3 %copy.33.tracers_ref = f32[2,180,768]{2,1,0:T(8,128)} copy(f32[2,180,768]{2,0,1:T(2,128)} %param.13) | data formatting | bytes 2211840 | tf_op args[0]
  3.0 0.1 tile.7
  3.1 0.1 multiply_multiply_fusion
  3.2 0.7 %reshape_tile.4.scaled_ref = f32[128,1]{1,0:T(8,128)} reshape(f32[16,8]{1,0:T(8,128)S(1)} %tile.8) | data formatting | bytes 1024 | tf_op jit(solution)/shard_map/reshape;tile | solution.py:272
  3.9 0.0 copy-start
  3.9 38.4 %shard_map.140 = (f32[8,2,8,182]{3,2,1,0:T(8,128)}, f32[8,2,8,180]{3,2,1,0:T(8,128)}, f32[2,4,768]{2,1,0:T(4,128)}, f32[2,8,768]{2,1,0:T(8,128)}, f32[2,180,128]...) custom-call(f32[8,2,8,180]{3,2,1,0:T(8,128)} %bitcast.18, ...), custom_call_target="tpu_custom_call" | custom-call | tf_op jit(solution)/shard_map/pallas_call | solution.py:286
  42.3 1.0 %slice.129 = f32[2,180,72]{2,1,0:T(8,128)S(1)} slice(f32[2,180,128]{2,1,0:T(8,128)} %get-tuple-element.16), slice={[0:2], [0:180], [56:128]} | slice | bytes 207360 | tf_op jit(solution)/shard_map/slice | solution.py:353
  43.4 0.9 %fusion.73 = (f32[4,2,8,180]{3,2,1,0:T(8,128)S(1)}, f32[4,2,8,180]{3,2,1,0:T(8,128)S(1)}) fusion(f32[8,2,8,180]{3,2,1,0:T(8,128)} %get-tuple-element.11), kind=kLoop, calls=%fused_computation.105 | loop fusion | bytes 184320 | tf_op jit(solution)/shard_map/slice | solution.py:361
  44.3 0.7 %slice_bitcast_fusion.1 = f32[2,1,180]{2,0,1:T(2,128)S(1)} fusion(f32[2,182]{1,0:T(2,128)} %get-tuple-element.14), kind=kLoop, calls=%fused_computation.96 | loop fusion | bytes 2880 | tf_op jit(solution)/shard_map/broadcast_in_dim | solution.py:365
  44.9 0.7 %slice_bitcast_fusion = f32[2,1,180]{2,0,1:T(2,128)S(1)} fusion(f32[2,182]{1,0:T(2,128)} %get-tuple-element.15), kind=kLoop, calls=%fused_computation.95 | loop fusion | bytes 2880 | tf_op jit(solution)/shard_map/broadcast_in_dim | solution.py:365
  45.7 0.0 copy-done
  45.7 0.0 copy-start.4
  45.7 0.0 copy-start.5
  45.7 0.0 copy-start.3
  45.7 4.7 %fusion.11 = f32[2,180,792]{2,1,0:T(8,128)} fusion(f32[2,180,768]{2,1,0:T(8,128)S(1)} %copy-done, f32[2,180,72]{2,1,0:T(8,128)S(1)} %slice.129, f32[2,180,72]{2,1,0:T(8,128)} %bitcast.21, f32[2,32,180]{2,1,0:T(8,128)S(1)} %bitcast.20, f32[2,1,180]{2,1,0:T(1,128)S(1)} %copy.29, f32[2,1,180]{2,1,0:T(1,128)S(1)} %copy.30, s32[792]{0:T(1024)S(1)} %add_select_fusion, ...), kind=kOutput, calls=%fused_computation.23 | convolution fusion | flops 121819896 | bytes 2506020 | tf_op jit(solution)/shard_map/ljc,jm->lcm/dot_general | solution.py:333
  50.5 0.0 copy-done.4
  50.5 0.0 copy-done.5
  50.5 0.0 copy-done.3
  50.5 0.1 fusion.74
  50.6 0.0 copy-start.1
  50.6 1.9 %fusion.30 = f32[2,181,768]{2,1,0:T(8,128)S(1)} fusion(f32[2,3,768]{2,1,0:T(4,128)S(1)} %slice.116, f32[2,3,768]{2,1,0:T(4,128)S(1)} %slice.120, f32[2,180,768]{2,1,0:T(8,128)S(1)} %copy-done, f32[2,32,180]{2,1,0:T(8,128)S(1)} %bitcast.19, f32[2,32,1]{2,1,0:T(8,128)S(1)} %get-tuple-element.25, f32[2,32,1]{2,1,0:T(8,128)S(1)} %get-tuple-element.24, ...), kind=kOutput, calls=%fused_computation.44 | convolution fusion | flops 115447552 | bytes 2304512 | tf_op jit(solution)/shard_map/ljc,jm->lcm/dot_general | solution.py:333
  52.5 0.1 broadcast.171
  52.6 0.1 reshape.65
  52.7 0.0 copy-done.1
  52.7 2.0 %fusion.33 = f32[2,180,768]{2,1,0:T(8,128)S(1)} fusion(f32[2,180,792]{2,1,0:T(8,128)} %fusion.11, f32[2,181,768]{2,1,0:T(8,128)S(1)} %fusion.30, f32[768]{0:T(1024)S(1)} %reshape.65, f32[2,180,768]{2,0,1:T(2,128)S(1)} %copy-done.1), kind=kLoop, calls=%fused_computation.48 | loop fusion | flops 1382400 | bytes 6638592 | tf_op jit(solution)/shard_map/sub | solution.py:382
  54.7 0.0 copy-start.2
  54.7 1.6 %copy.34 = f32[2,180,768]{2,0,1:T(2,128)} copy(f32[2,180,768]{2,1,0:T(8,128)S(1)} %fusion.33) | data formatting | bytes 2211840
  56.3 0.0 copy-done.2
  56.3 0.7 %copy.37 = f32[2,2,32,180]{3,2,1,0:T(8,128)} copy(f32[2,2,32,180]{3,2,1,0:T(8,128)S(1)} %bitcast.16) | data formatting | bytes 184320
  (11 shorter events, 0.2 us)
Async XLA Ops:
  3.9 41.8 %copy-start = (f32[2,180,768]{2,1,0:T(8,128)S(1)}, f32[2,180,768]{2,1,0:T(8,128)}, u32[]{:S(2)}) copy-start(f32[2,180,768]{2,1,0:T(8,128)} %copy.33.tracers_ref) | copy-start | bytes 3317764
  45.7 4.8 %copy-start.4 = (f32[2,4,768]{2,1,0:T(4,128)S(1)}, f32[2,4,768]{2,1,0:T(4,128)}, u32[]{:S(2)}) copy-start(f32[2,4,768]{2,1,0:T(4,128)} %get-tuple-element.12) | copy-start | bytes 73732
  45.7 4.8 %copy-start.5 = (f32[2,8,768]{2,1,0:T(8,128)S(1)}, f32[2,8,768]{2,1,0:T(8,128)}, u32[]{:S(2)}) copy-start(f32[2,8,768]{2,1,0:T(8,128)} %get-tuple-element.13) | copy-start | bytes 147460
  45.7 4.8 %copy-start.3 = (f32[8,2,8,182]{3,2,1,0:T(8,128)S(1)}, f32[8,2,8,182]{3,2,1,0:T(8,128)}, u32[]{:S(2)}) copy-start(f32[8,2,8,182]{3,2,1,0:T(8,128)} %get-tuple-element.10) | copy-start | bytes 279556
  50.6 2.1 %copy-start.1 = (f32[2,180,768]{2,0,1:T(2,128)S(1)}, f32[2,180,768]{2,0,1:T(2,128)}, u32[]{:S(2)}) copy-start(f32[2,180,768]{2,0,1:T(2,128)} %param.13) | copy-start | bytes 3317764
  54.7 1.6 %copy-start.2 = (f32[8,2,8,180]{3,2,1,0:T(8,128)S(1)}, f32[8,2,8,180]{3,2,1,0:T(8,128)}, u32[]{:S(2)}) copy-start(f32[8,2,8,180]{3,2,1,0:T(8,128)} %get-tuple-element.11) | copy-start | bytes 276484

commit v9 on v7

--- a/solution.py
+++ b/solution.py
@@ -156,30 +156,36 @@
         return jnp.dot(a, b, precision=EXACT_MODE, preferred_element_type=jnp.float32)
 
     x = gathered[...]
-    kc, ks = kc_ref[...], ks_ref[...]
+    half = x.shape[0]
     tc, ts = tc_ref[...], ts_ref[...]
-    c, s = c_ref[...], s_ref[...]
-    re = mm(kc, x)
-    im = -mm(ks, x)
+    stacked = mm(kc_ref[...], x)
+    re, im = stacked[:half], -stacked[half:]
     shifted_re = re * tc + im * ts
     shifted_im = im * tc - re * ts
-    modes_re = mm(shifted_re, c) + mm(shifted_im, s)
-    modes_im = mm(shifted_im, c) - mm(shifted_re, s)
+    stacked = jnp.concatenate([shifted_re, shifted_im], axis=0)
+    with_cos = mm(stacked, c_ref[...])
+    with_sin = mm(stacked, s_ref[...])
+    modes_re = with_cos[:half] + with_sin[half:]
+    modes_im = with_cos[half:] - with_sin[:half]
     factor = jnp.where(
         zero_ref[...] > 0.0, 1.0, jnp.minimum(1.0, scaled_ref[...] / divisor_ref[...])
     )
-    modes_re = modes_re * factor
-    modes_im = modes_im * factor
-    back_re = mm(modes_re, c) - mm(modes_im, s)
-    back_im = mm(modes_im, c) + mm(modes_re, s)
-    out_re = back_re * tc - back_im * ts
-    out_im = back_im * tc + back_re * ts
-    result = (mm(kc, out_re) - mm(ks, out_im)) / (n * x.shape[1])
-    restored[...] = (
-        mm(result, widen_ref[...])
-        + mm(jnp.roll(result, rows, axis=0), prev_ref[...])
-        + mm(jnp.roll(result, -rows, axis=0), next_ref[...])
-    )
+    stacked = jnp.concatenate([modes_re * factor, modes_im * factor], axis=0)
+    with_cos = mm(stacked, widen_ref[...])
+    with_sin = mm(stacked, prev_ref[...])
+    back_re = with_cos[:half] - with_sin[half:]
+    back_im = with_cos[half:] + with_sin[:half]
+    tcw, tsw = next_ref[0], next_ref[1]
+    out_re = back_re * tcw - back_im * tsw
+    out_im = back_im * tcw + back_re * tsw
+    result = mm(ks_ref[...], jnp.concatenate([out_re, out_im], axis=0)) / (n * x.shape[1])
+    columns = x.shape[1]
+    lane = lax.broadcasted_iota(jnp.int32, result.shape, 1)
+    before = jnp.sum(
+        jnp.where(lane == columns - 1, jnp.roll(result, rows, axis=0), 0.0), axis=1, keepdims=True
+    )
+    after = jnp.sum(jnp.where(lane == 0, jnp.roll(result, -rows, axis=0), 0.0), axis=1, keepdims=True)
+    restored[...] = jnp.where(lane == columns, before, jnp.where(lane == columns + 1, after, result))
     sends, own = swap(restored, out_ref, send_b, recv_b, 1)
     settle(restored, out_ref, send_b, recv_b, sends, own)
     wind_halos = [halo_copy(i) for i in range(4, 8)]
@@ -215,22 +221,22 @@
     divisor = np.where(wavenumber == 0, np.float32(1.0), sine * sine).astype(np.float32)
     zero_mode = (wavenumber == 0).astype(np.float32)
     widen = np.eye(columns, columns + 2)
-    take_last = np.zeros((columns, columns + 2))
-    take_last[columns - 1, columns] = 1.0
-    take_first = np.zeros((columns, columns + 2))
-    take_first[0, columns + 1] = 1.0
+    kron_cos, kron_sin = np.kron(np.cos(phase), eye), np.kron(np.sin(phase), eye)
+    twist_wide = np.stack(
+        [np.repeat(np.cos(twist), rows, axis=0) @ widen, np.repeat(np.sin(twist), rows, axis=0) @ widen]
+    )
     tables = (
-        np.kron(np.cos(phase), eye),
-        np.kron(np.sin(phase), eye),
+        np.concatenate([kron_cos, kron_sin], axis=0),
+        np.concatenate([kron_cos, -kron_sin], axis=1),
         np.repeat(np.cos(twist), rows, axis=0),
         np.repeat(np.sin(twist), rows, axis=0),
         np.cos(turn),
         np.sin(turn),
         np.repeat(divisor, rows, axis=0),
         np.repeat(zero_mode, rows, axis=0),
-        widen,
-        take_last,
-        take_first,
+        np.cos(turn) @ widen,
+        np.sin(turn) @ widen,
+        twist_wide,
     )
     return [jnp.asarray(t.astype(np.float32)) for t in tables]
 

time: 55.7 us -> 55.6 us (level)
  no operation moved by 1% of the time
where the time goes in v9:
time: 55.6 us; the launch traced here: 55.2 us
  Pallas kernels  36.7 us (66%)
  local copies, waits for them, and re-layouts  8.91 us (16%)
  matrix products  6.62 us (12%)
  other arithmetic  2.22 us (4%)
  between operations  0.78 us (1%)
    pallas_call x1, Pallas kernels, exchange_all(): pl.pallas_call(functools.partial(filter_kernel, n, rows), out_shape=[jax....  36.7 us
    dot_general x2, matrix products, spread(): return jnp.einsum('ljc,jm->lcm', values, pick, precision=EXACT_MODE)  6.62 us
    unnamed x15, local copies, waits for them, and re-layouts  4.57 us
    sub x1, other arithmetic, local(): advected = tracers - metric[None, None, :] * change  2.02 us

profile of v9, /device:TPU:1, one launch (start us, length us, event | category | flops | bytes accessed | tf_op | source)
XLA Modules:
  0.0 55.2 jit_solution(10985379998400705933)
XLA Ops:
  0.6 2.3 %copy.33.tracers_ref = f32[2,180,768]{2,1,0:T(8,128)} copy(f32[2,180,768]{2,0,1:T(2,128)} %param.13) | data formatting | bytes 2211840 | tf_op args[0]
  3.0 0.1 tile.7
  3.1 0.1 multiply_multiply_fusion
  3.2 0.7 %reshape_tile.4.scaled_ref = f32[128,1]{1,0:T(8,128)} reshape(f32[16,8]{1,0:T(8,128)S(1)} %tile.8) | data formatting | bytes 1024 | tf_op jit(solution)/shard_map/reshape;tile | solution.py:253
  3.9 0.0 copy-start
  3.9 36.7 %shard_map.140 = (f32[128,182]{1,0:T(8,128)}, f32[128,180]{1,0:T(8,128)}, f32[2,4,768]{2,1,0:T(4,128)}, f32[2,8,768]{2,1,0:T(8,128)}, f32[2,180,128]{2,1,0:T(8,1...) custom-call(f32[128,180]{1,0:T(8,128)} %bitcast.18, f32[128,1]{1,0:T(8,128)} %reshape_tile.4.scaled_ref, ...), custom_call_target="tpu_custom_call" | custom-call | tf_op jit(solution)/shard_map/pallas_call | solution.py:267
  40.6 1.0 %slice.129 = f32[2,180,72]{2,1,0:T(8,128)S(1)} slice(f32[2,180,128]{2,1,0:T(8,128)} %get-tuple-element.16), slice={[0:2], [0:180], [56:128]} | slice | bytes 207360 | tf_op jit(solution)/shard_map/slice | solution.py:332
  41.6 0.9 %fusion.73 = (f32[64,180]{1,0:T(8,128)S(1)}, f32[64,180]{1,0:T(8,128)S(1)}) fusion(f32[128,180]{1,0:T(8,128)} %get-tuple-element.11), kind=kLoop, calls=%fused_computation.105 | loop fusion | bytes 184320 | tf_op jit(solution)/shard_map/slice | solution.py:340
  42.5 0.7 %slice_bitcast_fusion.1 = f32[2,1,180]{2,0,1:T(2,128)S(1)} fusion(f32[2,182]{1,0:T(2,128)} %get-tuple-element.14), kind=kLoop, calls=%fused_computation.96 | loop fusion | bytes 2880 | tf_op jit(solution)/shard_map/broadcast_in_dim | solution.py:344
  43.2 0.7 %slice_bitcast_fusion = f32[2,1,180]{2,0,1:T(2,128)S(1)} fusion(f32[2,182]{1,0:T(2,128)} %get-tuple-element.15), kind=kLoop, calls=%fused_computation.95 | loop fusion | bytes 2880 | tf_op jit(solution)/shard_map/broadcast_in_dim | solution.py:344
  44.0 0.0 copy-done
  44.0 0.0 copy-start.4
  44.0 0.0 copy-start.5
  44.0 0.0 copy-start.3
  44.0 4.7 %fusion.11 = f32[2,180,792]{2,1,0:T(8,128)} fusion(f32[2,180,768]{2,1,0:T(8,128)S(1)} %copy-done, f32[2,180,72]{2,1,0:T(8,128)S(1)} %slice.129, f32[2,180,72]{2,1,0:T(8,128)} %bitcast.21, f32[2,32,180]{2,1,0:T(8,128)S(1)} %bitcast.20, f32[2,1,180]{2,1,0:T(1,128)S(1)} %copy.29, f32[2,1,180]{2,1,0:T(1,128)S(1)} %copy.30, s32[792]{0:T(1024)S(1)} %add_select_fusion, ...), kind=kOutput, calls=%fused_computation.23 | convolution fusion | flops 121819896 | bytes 2506020 | tf_op jit(solution)/shard_map/ljc,jm->lcm/dot_general | solution.py:312
  48.7 0.0 copy-done.4
  48.7 0.0 copy-done.5
  48.8 0.0 copy-done.3
  48.8 0.1 fusion.74
  48.9 0.0 copy-start.1
  48.9 1.9 %fusion.30 = f32[2,181,768]{2,1,0:T(8,128)S(1)} fusion(f32[2,3,768]{2,1,0:T(4,128)S(1)} %slice.116, f32[2,3,768]{2,1,0:T(4,128)S(1)} %slice.120, f32[2,180,768]{2,1,0:T(8,128)S(1)} %copy-done, f32[2,32,180]{2,1,0:T(8,128)S(1)} %bitcast.19, f32[2,32,1]{2,1,0:T(8,128)S(1)} %get-tuple-element.25, f32[2,32,1]{2,1,0:T(8,128)S(1)} %get-tuple-element.24, ...), kind=kOutput, calls=%fused_computation.44 | convolution fusion | flops 115447552 | bytes 2304512 | tf_op jit(solution)/shard_map/ljc,jm->lcm/dot_general | solution.py:312
  50.8 0.1 broadcast.171
  50.9 0.1 reshape.69
  51.0 0.0 copy-done.1
  51.0 2.0 %fusion.33 = f32[2,180,768]{2,1,0:T(8,128)S(1)} fusion(f32[2,180,792]{2,1,0:T(8,128)} %fusion.11, f32[2,181,768]{2,1,0:T(8,128)S(1)} %fusion.30, f32[768]{0:T(1024)S(1)} %reshape.69, f32[2,180,768]{2,0,1:T(2,128)S(1)} %copy-done.1), kind=kLoop, calls=%fused_computation.48 | loop fusion | flops 1382400 | bytes 6638592 | tf_op jit(solution)/shard_map/sub | solution.py:361
  53.0 0.0 copy-start.2
  53.0 1.6 %copy.34 = f32[2,180,768]{2,0,1:T(2,128)} copy(f32[2,180,768]{2,1,0:T(8,128)S(1)} %fusion.33) | data formatting | bytes 2211840
  54.6 0.0 copy-done.2
  54.6 0.7 %copy.37 = f32[2,2,32,180]{3,2,1,0:T(8,128)} copy(f32[2,2,32,180]{3,2,1,0:T(8,128)S(1)} %bitcast.16) | data formatting | bytes 184320
  (11 shorter events, 0.2 us)
Async XLA Ops:
  3.9 40.1 %copy-start = (f32[2,180,768]{2,1,0:T(8,128)S(1)}, f32[2,180,768]{2,1,0:T(8,128)}, u32[]{:S(2)}) copy-start(f32[2,180,768]{2,1,0:T(8,128)} %copy.33.tracers_ref) | copy-start | bytes 3317764
  44.0 4.8 %copy-start.4 = (f32[2,4,768]{2,1,0:T(4,128)S(1)}, f32[2,4,768]{2,1,0:T(4,128)}, u32[]{:S(2)}) copy-start(f32[2,4,768]{2,1,0:T(4,128)} %get-tuple-element.12) | copy-start | bytes 73732
  44.0 4.8 %copy-start.5 = (f32[2,8,768]{2,1,0:T(8,128)S(1)}, f32[2,8,768]{2,1,0:T(8,128)}, u32[]{:S(2)}) copy-start(f32[2,8,768]{2,1,0:T(8,128)} %get-tuple-element.13) | copy-start | bytes 147460
  44.0 4.8 %copy-start.3 = (f32[128,182]{1,0:T(8,128)S(1)}, f32[128,182]{1,0:T(8,128)}, u32[]{:S(2)}) copy-start(f32[128,182]{1,0:T(8,128)} %get-tuple-element.10) | copy-start | bytes 279556
  48.9 2.1 %copy-start.1 = (f32[2,180,768]{2,0,1:T(2,128)S(1)}, f32[2,180,768]{2,0,1:T(2,128)}, u32[]{:S(2)}) copy-start(f32[2,180,768]{2,0,1:T(2,128)} %param.13) | copy-start | bytes 3317764
  53.0 1.6 %copy-start.2 = (f32[128,180]{1,0:T(8,128)S(1)}, f32[128,180]{1,0:T(8,128)}, u32[]{:S(2)}) copy-start(f32[128,180]{1,0:T(8,128)} %get-tuple-element.11) | copy-start | bytes 276484

commit v10 on v9

--- a/solution.py
+++ b/solution.py
@@ -98,6 +98,7 @@
     for level in range(2):
         first = 2 * level_rows + level * level_rows
         halo_plan.append((out_ref.at[pl.ds(first, 1)], vnorth_ref.at[pl.ds(level, 1)], (down, me)))
+    edge_rows = [2 * level_rows + k for k in (0, level_rows - 1, level_rows, 2 * level_rows - 1)]
 
     def halo_copy(index):
         source, target, device = halo_plan[index]
@@ -187,10 +188,40 @@
     after = jnp.sum(jnp.where(lane == 0, jnp.roll(result, -rows, axis=0), 0.0), axis=1, keepdims=True)
     restored[...] = jnp.where(lane == columns, before, jnp.where(lane == columns + 1, after, result))
     sends, own = swap(restored, out_ref, send_b, recv_b, 1)
-    settle(restored, out_ref, send_b, recv_b, sends, own)
+    own.wait()
+    holders = sorted({row // rows for row in edge_rows})
+
+    def arrival(origin):
+        return pltpu.make_async_remote_copy(
+            src_ref=block(restored, origin),
+            dst_ref=block(out_ref, origin),
+            send_sem=send_b.at[origin],
+            recv_sem=recv_b.at[origin],
+            device_id=(band, origin),
+            device_id_type=MESH,
+        )
+
+    for holder in holders:
+
+        @pl.when(me != holder)
+        def _():
+            arrival(holder).wait_recv()
+
     wind_halos = [halo_copy(i) for i in range(4, 8)]
     for copy in wind_halos:
         copy.start()
+    for k in range(1, n):
+        origin = lax.rem(me + n - k, n)
+        pending = origin >= 0
+        for holder in holders:
+            pending = jnp.logical_and(pending, origin != holder)
+
+        @pl.when(pending)
+        def _():
+            arrival(origin).wait_recv()
+
+    for copy in sends:
+        copy.wait_send()
     smooth_ref[...] = out_ref[:, : smooth_ref.shape[1]]
     for copy in tracer_halos + wind_halos:
         copy.wait_recv()

time: 55.6 us -> 55.5 us (level)
  no operation moved by 1% of the time
where the time goes in v10:
time: 55.5 us; the launch traced here: 55.2 us
  Pallas kernels  36.7 us (66%)
  local copies, waits for them, and re-layouts  8.91 us (16%)
  matrix products  6.62 us (12%)
  other arithmetic  2.22 us (4%)
  between operations  0.78 us (1%)
    pallas_call x1, Pallas kernels, exchange_all(): pl.pallas_call(functools.partial(filter_kernel, n, rows), out_shape=[jax....  36.7 us
    dot_general x2, matrix products, spread(): return jnp.einsum('ljc,jm->lcm', values, pick, precision=EXACT_MODE)  6.62 us
    unnamed x15, local copies, waits for them, and re-layouts  4.57 us
    sub x1, other arithmetic, local(): advected = tracers - metric[None, None, :] * change  2.02 us

profile of v10, /device:TPU:1, one launch (start us, length us, event | category | flops | bytes accessed | tf_op | source)
XLA Modules:
  0.0 55.2 jit_solution(10260519543798176185)
XLA Ops:
  0.6 2.3 %copy.33.tracers_ref = f32[2,180,768]{2,1,0:T(8,128)} copy(f32[2,180,768]{2,0,1:T(2,128)} %param.13) | data formatting | bytes 2211840 | tf_op args[0]
  3.0 0.1 tile.7
  3.1 0.1 multiply_multiply_fusion
  3.2 0.7 %reshape_tile.4.scaled_ref = f32[128,1]{1,0:T(8,128)} reshape(f32[16,8]{1,0:T(8,128)S(1)} %tile.8) | data formatting | bytes 1024 | tf_op jit(solution)/shard_map/reshape;tile | solution.py:284
  3.9 0.0 copy-start
  3.9 36.7 %shard_map.140 = (f32[128,182]{1,0:T(8,128)}, f32[128,180]{1,0:T(8,128)}, f32[2,4,768]{2,1,0:T(4,128)}, f32[2,8,768]{2,1,0:T(8,128)}, f32[2,180,128]{2,1,0:T(8,1...) custom-call(f32[128,180]{1,0:T(8,128)} %bitcast.18, f32[128,1]{1,0:T(8,128)} %reshape_tile.4.scaled_ref, ...), custom_call_target="tpu_custom_call" | custom-call | tf_op jit(solution)/shard_map/pallas_call | solution.py:298
  40.6 1.0 %slice.129 = f32[2,180,72]{2,1,0:T(8,128)S(1)} slice(f32[2,180,128]{2,1,0:T(8,128)} %get-tuple-element.16), slice={[0:2], [0:180], [56:128]} | slice | bytes 207360 | tf_op jit(solution)/shard_map/slice | solution.py:363
  41.6 0.9 %fusion.73 = (f32[64,180]{1,0:T(8,128)S(1)}, f32[64,180]{1,0:T(8,128)S(1)}) fusion(f32[128,180]{1,0:T(8,128)} %get-tuple-element.11), kind=kLoop, calls=%fused_computation.105 | loop fusion | bytes 184320 | tf_op jit(solution)/shard_map/slice | solution.py:371
  42.5 0.7 %slice_bitcast_fusion.1 = f32[2,1,180]{2,0,1:T(2,128)S(1)} fusion(f32[2,182]{1,0:T(2,128)} %get-tuple-element.14), kind=kLoop, calls=%fused_computation.96 | loop fusion | bytes 2880 | tf_op jit(solution)/shard_map/broadcast_in_dim | solution.py:375
  43.2 0.7 %slice_bitcast_fusion = f32[2,1,180]{2,0,1:T(2,128)S(1)} fusion(f32[2,182]{1,0:T(2,128)} %get-tuple-element.15), kind=kLoop, calls=%fused_computation.95 | loop fusion | bytes 2880 | tf_op jit(solution)/shard_map/broadcast_in_dim | solution.py:375
  43.9 0.0 copy-done
  43.9 0.0 copy-start.4
  44.0 0.0 copy-start.5
  44.0 0.0 copy-start.3
  44.0 4.7 %fusion.11 = f32[2,180,792]{2,1,0:T(8,128)} fusion(f32[2,180,768]{2,1,0:T(8,128)S(1)} %copy-done, f32[2,180,72]{2,1,0:T(8,128)S(1)} %slice.129, f32[2,180,72]{2,1,0:T(8,128)} %bitcast.21, f32[2,32,180]{2,1,0:T(8,128)S(1)} %bitcast.20, f32[2,1,180]{2,1,0:T(1,128)S(1)} %copy.29, f32[2,1,180]{2,1,0:T(1,128)S(1)} %copy.30, s32[792]{0:T(1024)S(1)} %add_select_fusion, ...), kind=kOutput, calls=%fused_computation.23 | convolution fusion | flops 121819896 | bytes 2506020 | tf_op jit(solution)/shard_map/ljc,jm->lcm/dot_general | solution.py:343
  48.7 0.0 copy-done.4
  48.7 0.0 copy-done.5
  48.7 0.0 copy-done.3
  48.8 0.1 fusion.74
  48.9 0.0 copy-start.1
  48.9 1.9 %fusion.30 = f32[2,181,768]{2,1,0:T(8,128)S(1)} fusion(f32[2,3,768]{2,1,0:T(4,128)S(1)} %slice.116, f32[2,3,768]{2,1,0:T(4,128)S(1)} %slice.120, f32[2,180,768]{2,1,0:T(8,128)S(1)} %copy-done, f32[2,32,180]{2,1,0:T(8,128)S(1)} %bitcast.19, f32[2,32,1]{2,1,0:T(8,128)S(1)} %get-tuple-element.25, f32[2,32,1]{2,1,0:T(8,128)S(1)} %get-tuple-element.24, ...), kind=kOutput, calls=%fused_computation.44 | convolution fusion | flops 115447552 | bytes 2304512 | tf_op jit(solution)/shard_map/ljc,jm->lcm/dot_general | solution.py:343
  50.8 0.1 broadcast.171
  50.8 0.1 reshape.69
  50.9 0.0 copy-done.1
  50.9 2.0 %fusion.33 = f32[2,180,768]{2,1,0:T(8,128)S(1)} fusion(f32[2,180,792]{2,1,0:T(8,128)} %fusion.11, f32[2,181,768]{2,1,0:T(8,128)S(1)} %fusion.30, f32[768]{0:T(1024)S(1)} %reshape.69, f32[2,180,768]{2,0,1:T(2,128)S(1)} %copy-done.1), kind=kLoop, calls=%fused_computation.48 | loop fusion | flops 1382400 | bytes 6638592 | tf_op jit(solution)/shard_map/sub | solution.py:392
  53.0 0.0 copy-start.2
  53.0 1.6 %copy.34 = f32[2,180,768]{2,0,1:T(2,128)} copy(f32[2,180,768]{2,1,0:T(8,128)S(1)} %fusion.33) | data formatting | bytes 2211840
  54.5 0.0 copy-done.2
  54.5 0.7 %copy.37 = f32[2,2,32,180]{3,2,1,0:T(8,128)} copy(f32[2,2,32,180]{3,2,1,0:T(8,128)S(1)} %bitcast.16) | data formatting | bytes 184320
  (11 shorter events, 0.2 us)
Async XLA Ops:
  3.9 40.0 %copy-start = (f32[2,180,768]{2,1,0:T(8,128)S(1)}, f32[2,180,768]{2,1,0:T(8,128)}, u32[]{:S(2)}) copy-start(f32[2,180,768]{2,1,0:T(8,128)} %copy.33.tracers_ref) | copy-start | bytes 3317764
  43.9 4.8 %copy-start.4 = (f32[2,4,768]{2,1,0:T(4,128)S(1)}, f32[2,4,768]{2,1,0:T(4,128)}, u32[]{:S(2)}) copy-start(f32[2,4,768]{2,1,0:T(4,128)} %get-tuple-element.12) | copy-start | bytes 73732
  44.0 4.8 %copy-start.5 = (f32[2,8,768]{2,1,0:T(8,128)S(1)}, f32[2,8,768]{2,1,0:T(8,128)}, u32[]{:S(2)}) copy-start(f32[2,8,768]{2,1,0:T(8,128)} %get-tuple-element.13) | copy-start | bytes 147460
  44.0 4.8 %copy-start.3 = (f32[128,182]{1,0:T(8,128)S(1)}, f32[128,182]{1,0:T(8,128)}, u32[]{:S(2)}) copy-start(f32[128,182]{1,0:T(8,128)} %get-tuple-element.10) | copy-start | bytes 279556
  48.9 2.1 %copy-start.1 = (f32[2,180,768]{2,0,1:T(2,128)S(1)}, f32[2,180,768]{2,0,1:T(2,128)}, u32[]{:S(2)}) copy-start(f32[2,180,768]{2,0,1:T(2,128)} %param.13) | copy-start | bytes 3317764
  53.0 1.6 %copy-start.2 = (f32[128,180]{1,0:T(8,128)S(1)}, f32[128,180]{1,0:T(8,128)}, u32[]{:S(2)}) copy-start(f32[128,180]{1,0:T(8,128)} %get-tuple-element.11) | copy-start | bytes 276484

commit v11 on v10

--- a/solution.py
+++ b/solution.py
@@ -64,8 +64,10 @@
 
 
 def filter_kernel(n, rows, winds_ref, scaled_ref, kc_ref, ks_ref, tc_ref, ts_ref, c_ref, s_ref,
-                  divisor_ref, zero_ref, widen_ref, prev_ref, next_ref, tracers_ref,
-                  out_ref, smooth_ref, west_ref, east_ref, south_ref, north_ref, vsouth_ref, vnorth_ref,
+                  divisor_ref, zero_ref, widen_ref, prev_ref, next_ref, pairs_ref, fm_ref, fs_ref, fn_ref,
+                  tracers_ref,
+                  smooth_ref, zonal_ref, merid_ref, west_ref, east_ref, south_out, north_out,
+                  out_ref, south_ref, north_ref, vsouth_ref, vnorth_ref,
                   gathered, restored, send_a, recv_a, send_b, recv_b, halo_send, halo_recv, local_sem):
     me = lax.axis_index("lon")
     band = lax.axis_index("lat")
@@ -228,15 +230,24 @@
     for copy in tracer_halos + wind_halos:
         copy.wait_send()
 
-    @pl.when(band == 0)
-    def _():
-        south_ref[...] = jnp.zeros(south_ref.shape, jnp.float32)
-        vsouth_ref[...] = jnp.zeros(vsouth_ref.shape, jnp.float32)
-
-    @pl.when(band == bands - 1)
-    def _():
-        north_ref[...] = jnp.zeros(north_ref.shape, jnp.float32)
-        vnorth_ref[...] = jnp.zeros(vnorth_ref.shape, jnp.float32)
+    keep_south = jnp.where(band > 0, 1.0, 0.0)
+    keep_north = jnp.where(band < bands - 1, 1.0, 0.0)
+    width = south_out.shape[2]
+    south = pltpu.roll(south_ref[...], width, 2)
+    south_out[...] = south[..., :width] * keep_south
+    north_out[...] = north_ref[..., :width] * keep_north
+    band_rows = level_rows
+    for level in range(2):
+        east_rows = out_ref[pl.ds(level * band_rows, band_rows), :]
+        zonal_ref[level] = mm(east_rows, pairs_ref[...])
+        first = 2 * level_rows + level * level_rows
+        north_rows = out_ref[pl.ds(first, band_rows), :]
+        merid = (
+            mm(fm_ref[...], north_rows)
+            + fs_ref[...] * (vsouth_ref[pl.ds(level, 1), :] * keep_south)
+            + fn_ref[...] * (vnorth_ref[pl.ds(level, 1), :] * keep_north)
+        )
+        merid_ref[level] = merid[:, : merid_ref.shape[2]]
 
 
 def spectral_tables(n, rows, columns):
@@ -272,35 +283,52 @@
     return [jnp.asarray(t.astype(np.float32)) for t in tables]
 
 
-def exchange_all(flat_winds, row_cosine, tracers):
+def exchange_all(flat_winds, row_cosine, face_cosine, tracers):
     flat_rows, columns = flat_winds.shape
     levels, lon_cols, merged = tracers.shape
     n = lax.axis_size("lon")
     lon_index = lax.axis_index("lon")
     rows = flat_rows // n
-    tracer_count = merged // row_cosine.shape[0]
-    own_cosine = lax.dynamic_slice_in_dim(jnp.tile(row_cosine, flat_rows // row_cosine.shape[0]), lon_index * rows, rows, 0)
+    lat_rows = row_cosine.shape[0]
+    tracer_count = merged // lat_rows
+    own_cosine = lax.dynamic_slice_in_dim(
+        jnp.tile(row_cosine, flat_rows // lat_rows), lon_index * rows, rows, 0
+    )
     scaled = (own_cosine / COS_FLOOR) ** 2
     scaled = jnp.tile(scaled, n).reshape(n * rows, 1)
+    half_cosine = 0.5 * face_cosine
+    pair_rows = np.zeros((columns + 2, columns + 1), np.float32)
+    for face in range(columns + 1):
+        pair_rows[columns if face == 0 else face - 1, face] = 0.5
+        pair_rows[columns + 1 if face == columns else face, face] = 0.5
+    faces = jnp.arange(lat_rows + 1)[:, None]
+    cells = jnp.arange(lat_rows)[None, :]
+    face_weights = jnp.where((cells == faces - 1) | (cells == faces), half_cosine[:, None], 0.0)
+    south_weight = jnp.where(faces == 0, half_cosine[:, None], 0.0)
+    north_weight = jnp.where(faces == lat_rows, half_cosine[:, None], 0.0)
     vmem = pl.BlockSpec(memory_space=pltpu.VMEM)
+    wide_lanes = -(-3 * tracer_count // 128) * 128
     west_cols = lon_cols - (lon_cols - 3) // 8 * 8
-    lanes = -(-3 * tracer_count // 128) * 128
     shapes = [
-        (flat_rows, columns + 2),
         (flat_rows, columns),
+        (levels, lat_rows, columns + 1),
+        (levels, lat_rows + 1, columns),
         (levels, west_cols, merged),
         (levels, 8, merged),
-        (levels, lon_cols, lanes),
-        (levels, lon_cols, lanes),
-        (levels, columns + 2),
-        (levels, columns + 2),
+        (levels, lon_cols, 3 * tracer_count),
+        (levels, lon_cols, 3 * tracer_count),
     ]
     return pl.pallas_call(
         functools.partial(filter_kernel, n, rows),
         out_shape=[jax.ShapeDtypeStruct(shape, jnp.float32) for shape in shapes],
-        in_specs=[vmem] * 13 + [pl.BlockSpec(memory_space=pl.ANY)],
+        in_specs=[vmem] * 17 + [pl.BlockSpec(memory_space=pl.ANY)],
         out_specs=[vmem] * len(shapes),
         scratch_shapes=[
+            pltpu.VMEM((flat_rows, columns + 2), jnp.float32),
+            pltpu.VMEM((levels, lon_cols, wide_lanes), jnp.float32),
+            pltpu.VMEM((levels, lon_cols, wide_lanes), jnp.float32),
+            pltpu.VMEM((levels, columns + 2), jnp.float32),
+            pltpu.VMEM((levels, columns + 2), jnp.float32),
             pltpu.VMEM((flat_rows, columns), jnp.float32),
             pltpu.VMEM((flat_rows, columns + 2), jnp.float32),
             pltpu.SemaphoreType.DMA((n,)),
@@ -312,7 +340,16 @@
             pltpu.SemaphoreType.DMA((2,)),
         ],
         compiler_params=pltpu.CompilerParams(collective_id=0, has_side_effects=True),
-    )(flat_winds, scaled, *spectral_tables(n, rows, columns), tracers)
+    )(
+        flat_winds,
+        scaled,
+        *spectral_tables(n, rows, columns),
+        jnp.asarray(pair_rows),
+        face_weights,
+        south_weight,
+        north_weight,
+        tracers,
+    )
 
 
 def stencil(padded, dim, faces, stride):
@@ -355,28 +392,15 @@
         (row_ids.astype(jnp.float32) + 0.5) * (math.pi / lat_total) - 0.5 * math.pi
     )
     flat_winds = wind_field.reshape(2 * levels * lat_rows, lon_cols)
-    wide, smoothed, west, east, south, north, v_south, v_north = exchange_all(
-        flat_winds, row_cosine, tracers
-    )
-    west = west[:, west.shape[1] - 3 :]
-    east = east[:, :3]
-    south = south[..., south.shape[2] - 3 * tracer_count :]
-    north = north[..., : 3 * tracer_count]
-    v_south = v_south[:, :lon_cols]
-    v_north = v_north[:, :lon_cols]
-    smoothed = smoothed.reshape(2, levels, lat_rows, lon_cols)
-    east_wide = wide.reshape(2, levels, lat_rows, lon_cols + 2)[0]
-    north_wind = smoothed[1]
-    u_pad = jnp.concatenate(
-        [east_wide[..., lon_cols : lon_cols + 1], smoothed[0], east_wide[..., lon_cols + 1 :]],
-        axis=2,
-    )
-    zonal_speed = 0.5 * (u_pad[:, :, : lon_cols + 1] + u_pad[:, :, 1:])
-    v_pad = jnp.concatenate([v_south[:, None], north_wind, v_north[:, None]], axis=1)
     face_ids = first_row + jnp.arange(lat_rows + 1, dtype=jnp.int32)
     face_cosine = jnp.cos(face_ids.astype(jnp.float32) * (math.pi / lat_total) - 0.5 * math.pi)
     face_cosine = jnp.where((face_ids == 0) | (face_ids == lat_total), 0.0, face_cosine)
-    merid_speed = 0.5 * (v_pad[:, : lat_rows + 1] + v_pad[:, 1:]) * face_cosine[None, :, None]
+    smoothed, zonal_speed, merid_speed, west, east, south, north = exchange_all(
+        flat_winds, row_cosine, face_cosine, tracers
+    )
+    west = west[:, west.shape[1] - 3 :]
+    east = east[:, :3]
+    smoothed = smoothed.reshape(2, levels, lat_rows, lon_cols)
     zonal_rep = spread(zonal_speed, lat_rows, tracer_count)
     merid_rep = spread(merid_speed, lat_rows + 1, tracer_count)
     zonal_pad = jnp.concatenate([west, tracers, east], axis=1)

time: 55.5 us -> 54.4 us (0.980)
  local copies, waits for them, and re-layouts: 8.91 us -> 6.56 us
  other arithmetic: 2.22 us -> 3.58 us
    slice x4 -> x0, local copies, waits for them, and re-layouts: 2 us -> none  [the longest x1 1.03 us: local(): south = south[..., south.shape[2] - 3 * tracer_count:]]
    select_n x0 -> x2, other arithmetic: none -> 1.36 us  [the longest x1 0.68 us: exchange_all(): jnp.where((cells == faces - 1) | (cells == faces), half_cosine[:, None],...]
    broadcast_in_dim x4 -> x0, local copies, waits for them, and re-layouts: 1.36 us -> none  [the longest x2 0.68 us: local(): v_north[:, None]]
    concatenate x0 -> x1, local copies, waits for them, and re-layouts: none -> 0.94 us  [local(): merid_pad = jnp.concatenate([south, tracers, north], axis=2)]
where the time goes in v11:
time: 54.4 us; the launch traced here: 54.1 us
  Pallas kernels  37 us (68%)
  local copies, waits for them, and re-layouts  6.56 us (12%)
  matrix products  6.24 us (11%)
  other arithmetic  3.58 us (7%)
  between operations  0.78 us (1%)
    pallas_call x1, Pallas kernels, exchange_all(): pl.pallas_call(functools.partial(filter_kernel, n, rows), out_shape=[jax....  37 us
    dot_general x2, matrix products, spread(): return jnp.einsum('ljc,jm->lcm', values, pick, precision=EXACT_MODE)  6.24 us
    unnamed x15, local copies, waits for them, and re-layouts  4.65 us
    sub x1, other arithmetic, local(): advected = tracers - metric[None, None, :] * change  2.02 us

profile of v11, /device:TPU:1, one launch (start us, length us, event | category | flops | bytes accessed | tf_op | source)
XLA Modules:
  0.0 54.1 jit_solution(6818568025928660680)
XLA Ops:
  0.6 2.4 %constant_dynamic-update-slice_fusion.1 = (f32[2,180,840]{2,1,0:T(8,128)S(1)}, f32[2,180,768]{2,1,0:T(8,128)}) fusion(f32[2,180,768]{2,0,1:T(2,128)} %param.14), kind=kLoop, calls=%fused_computation.78 | loop fusion | bytes 3342336
  3.1 0.1 tile.7
  3.2 0.1 multiply_multiply_fusion
  3.3 0.7 %reshape_tile.4.scaled_ref = f32[128,1]{1,0:T(8,128)} reshape(f32[16,8]{1,0:T(8,128)S(1)} %tile.8) | data formatting | bytes 1024 | tf_op jit(solution)/shard_map/reshape;tile | solution.py:298
  4.0 0.7 %fusion.50.fm_ref = f32[33,32]{1,0:T(8,128)} fusion(f32[33]{0:T(128)S(1)} %fusion.57, s32[33]{0:T(128)S(1)} %iota_add_fusion.1), kind=kLoop, calls=%fused_computation.70 | loop fusion | flops 4224 | bytes 4488 | tf_op jit(solution)/shard_map/jit(_where)/select_n | solution.py:306
  4.7 0.7 %fusion.46 = (f32[33,1]{1,0:T(8,128)}, f32[33,1]{1,0:T(8,128)}) fusion(s32[]{:T(128)S(6)} %mul.152), kind=kLoop, calls=%fused_computation.65 | loop fusion | flops 429 | bytes 268 | tf_op jit(solution)/shard_map/jit(_where)/select_n | solution.py:308
  5.4 0.0 copy-start
  5.4 37.0 %shard_map.149 = (f32[128,180]{1,0:T(8,128)}, f32[2,32,181]{2,1,0:T(8,128)}, f32[2,33,180]{2,1,0:T(8,128)}, f32[2,4,768]{2,1,0:T(4,128)}, f32[2,8,768]{2,1,0:T(8...) custom-call(f32[128,180]{1,0:T(8,128)} %bitcast.10, f32[128,1]{1,0:T(8,128)} %reshape_tile.4.scaled_ref, ...), custom_call_target="tpu_custom_call" | custom-call | tf_op jit(solution)/shard_map/pallas_call | solution.py:321
  42.4 0.9 %constant_dynamic-update-slice_fusion = f32[2,180,840]{2,1,0:T(8,128)S(1)} fusion(f32[2,180,840]{2,1,0:T(8,128)S(1)} %get-tuple-element.20, f32[2,180,72]{2,1,0:T(8,128)} %get-tuple-element.14), kind=kLoop, calls=%fused_computation.77 | loop fusion | bytes 292096 | tf_op jit(solution)/shard_map/concatenate | solution.py:409
  43.3 0.0 copy-done
  43.3 0.0 copy-start.3
  43.3 0.0 copy-start.4
  43.4 0.0 copy-start.5
  43.4 4.4 %fusion.9 = f32[2,180,792]{2,1,0:T(8,128)} fusion(f32[2,180,768]{2,1,0:T(8,128)S(1)} %copy-done, f32[2,180,72]{2,1,0:T(8,128)} %get-tuple-element.13, f32[2,180,840]{2,1,0:T(8,128)S(1)} %constant_dynamic-update-slice_fusion, f32[2,33,180]{2,1,0:T(8,128)} %get-tuple-element.12, s32[792]{0:T(1024)S(1)} %add_select_fusion), kind=kOutput, calls=%fused_computation.17 | convolution fusion | flops 120917016 | bytes 5822208 | tf_op jit(solution)/shard_map/ljc,jm->lcm/dot_general | solution.py:380
  47.8 0.0 copy-done.3
  47.8 0.0 copy-done.4
  47.8 0.0 copy-done.5
  47.8 0.0 copy-start.1
  47.9 1.8 %fusion.27 = f32[2,181,768]{2,1,0:T(8,128)S(1)} fusion(f32[2,3,768]{2,1,0:T(4,128)S(1)} %slice.74, f32[2,3,768]{2,1,0:T(4,128)S(1)} %slice.78, f32[2,180,768]{2,1,0:T(8,128)S(1)} %copy-done, f32[2,32,181]{2,1,0:T(8,128)S(1)} %copy-done.5, s32[768]{0:T(1024)S(1)} %add_select_fusion.1), kind=kOutput, calls=%fused_computation.37 | convolution fusion | flops 115401216 | bytes 2304256 | tf_op jit(solution)/shard_map/ljc,jm->lcm/dot_general | solution.py:380
  49.7 0.1 broadcast.293
  49.8 0.1 reshape.116
  49.8 0.0 copy-done.1
  49.9 2.0 %fusion.30 = f32[2,180,768]{2,1,0:T(8,128)S(1)} fusion(f32[2,180,792]{2,1,0:T(8,128)} %fusion.9, f32[2,181,768]{2,1,0:T(8,128)S(1)} %fusion.27, f32[768]{0:T(1024)S(1)} %reshape.116, f32[2,180,768]{2,0,1:T(2,128)S(1)} %copy-done.1), kind=kLoop, calls=%fused_computation.41 | loop fusion | flops 1382400 | bytes 6638592 | tf_op jit(solution)/shard_map/sub | solution.py:416
  51.9 0.0 copy-start.2
  51.9 1.6 %copy.31 = f32[2,180,768]{2,0,1:T(2,128)} copy(f32[2,180,768]{2,1,0:T(8,128)S(1)} %fusion.30) | data formatting | bytes 2211840
  53.5 0.0 copy-done.2
  53.5 0.7 %copy.37 = f32[2,2,32,180]{3,2,1,0:T(8,128)} copy(f32[2,2,32,180]{3,2,1,0:T(8,128)S(1)} %bitcast.11) | data formatting | bytes 184320
  (9 shorter events, 0.1 us)
Async XLA Ops:
  5.4 37.9 %copy-start = (f32[2,180,768]{2,1,0:T(8,128)S(1)}, f32[2,180,768]{2,1,0:T(8,128)}, u32[]{:S(2)}) copy-start(f32[2,180,768]{2,1,0:T(8,128)} %get-tuple-element.21.tracers_ref) | copy-start | bytes 3317764
  43.3 4.5 %copy-start.3 = (f32[2,4,768]{2,1,0:T(4,128)S(1)}, f32[2,4,768]{2,1,0:T(4,128)}, u32[]{:S(2)}) copy-start(f32[2,4,768]{2,1,0:T(4,128)} %get-tuple-element.10) | copy-start | bytes 73732
  43.3 4.5 %copy-start.4 = (f32[2,8,768]{2,1,0:T(8,128)S(1)}, f32[2,8,768]{2,1,0:T(8,128)}, u32[]{:S(2)}) copy-start(f32[2,8,768]{2,1,0:T(8,128)} %get-tuple-element.11) | copy-start | bytes 147460
  43.4 4.5 %copy-start.5 = (f32[2,32,181]{2,1,0:T(8,128)S(1)}, f32[2,32,181]{2,1,0:T(8,128)}, u32[]{:S(2)}) copy-start(f32[2,32,181]{2,1,0:T(8,128)} %get-tuple-element.9) | copy-start | bytes 139012
  47.8 2.0 %copy-start.1 = (f32[2,180,768]{2,0,1:T(2,128)S(1)}, f32[2,180,768]{2,0,1:T(2,128)}, u32[]{:S(2)}) copy-start(f32[2,180,768]{2,0,1:T(2,128)} %param.14) | copy-start | bytes 3317764
  51.9 1.6 %copy-start.2 = (f32[128,180]{1,0:T(8,128)S(1)}, f32[128,180]{1,0:T(8,128)}, u32[]{:S(2)}) copy-start(f32[128,180]{1,0:T(8,128)} %get-tuple-element.15) | copy-start | bytes 276484

commit v12 on v11

--- a/solution.py
+++ b/solution.py
@@ -63,8 +63,8 @@
     return jnp.maximum(speed, 0.0) * left + jnp.minimum(speed, 0.0) * right
 
 
-def filter_kernel(n, rows, winds_ref, scaled_ref, kc_ref, ks_ref, tc_ref, ts_ref, c_ref, s_ref,
-                  divisor_ref, zero_ref, widen_ref, prev_ref, next_ref, pairs_ref, fm_ref, fs_ref, fn_ref,
+def filter_kernel(n, rows, winds_ref, scales_ref, kc_ref, ks_ref, tc_ref, ts_ref, c_ref, s_ref,
+                  divisor_ref, zero_ref, widen_ref, prev_ref, next_ref, pairs_ref, halves_ref,
                   tracers_ref,
                   smooth_ref, zonal_ref, merid_ref, west_ref, east_ref, south_out, north_out,
                   out_ref, south_ref, north_ref, vsouth_ref, vnorth_ref,
@@ -170,9 +170,12 @@
     with_sin = mm(stacked, s_ref[...])
     modes_re = with_cos[:half] + with_sin[half:]
     modes_im = with_cos[half:] - with_sin[:half]
-    factor = jnp.where(
-        zero_ref[...] > 0.0, 1.0, jnp.minimum(1.0, scaled_ref[...] / divisor_ref[...])
-    )
+    lane_rows = lax.broadcasted_iota(jnp.int32, (n * rows, 1), 0) % rows
+    base = (band * n + me) * rows
+    scaled = jnp.zeros((n * rows, 1), jnp.float32)
+    for r in range(rows):
+        scaled = jnp.where(lane_rows == r, scales_ref[base + r], scaled)
+    factor = jnp.where(zero_ref[...] > 0.0, 1.0, jnp.minimum(1.0, scaled / divisor_ref[...]))
     stacked = jnp.concatenate([modes_re * factor, modes_im * factor], axis=0)
     with_cos = mm(stacked, widen_ref[...])
     with_sin = mm(stacked, prev_ref[...])
@@ -237,15 +240,24 @@
     south_out[...] = south[..., :width] * keep_south
     north_out[...] = north_ref[..., :width] * keep_north
     band_rows = level_rows
+    face_ids = lax.broadcasted_iota(jnp.int32, (band_rows + 1, 1), 0)
+    half = jnp.zeros((band_rows + 1, 1), jnp.float32)
+    for face in range(band_rows + 1):
+        half = jnp.where(face_ids == face, halves_ref[band * (band_rows + 1) + face], half)
+    faces = lax.broadcasted_iota(jnp.int32, (band_rows + 1, band_rows), 0)
+    cells = lax.broadcasted_iota(jnp.int32, (band_rows + 1, band_rows), 1)
+    face_weights = jnp.where((cells == faces - 1) | (cells == faces), half, 0.0)
+    south_weight = jnp.where(face_ids == 0, half, 0.0)
+    north_weight = jnp.where(face_ids == band_rows, half, 0.0)
     for level in range(2):
         east_rows = out_ref[pl.ds(level * band_rows, band_rows), :]
         zonal_ref[level] = mm(east_rows, pairs_ref[...])
         first = 2 * level_rows + level * level_rows
         north_rows = out_ref[pl.ds(first, band_rows), :]
         merid = (
-            mm(fm_ref[...], north_rows)
-            + fs_ref[...] * (vsouth_ref[pl.ds(level, 1), :] * keep_south)
-            + fn_ref[...] * (vnorth_ref[pl.ds(level, 1), :] * keep_north)
+            mm(face_weights, north_rows)
+            + south_weight * (vsouth_ref[pl.ds(level, 1), :] * keep_south)
+            + north_weight * (vnorth_ref[pl.ds(level, 1), :] * keep_north)
         )
         merid_ref[level] = merid[:, : merid_ref.shape[2]]
 
@@ -283,30 +295,37 @@
     return [jnp.asarray(t.astype(np.float32)) for t in tables]
 
 
-def exchange_all(flat_winds, row_cosine, face_cosine, tracers):
+def position_tables(n, rows, bands, lat_rows, flat_rows):
+    lat_total = bands * lat_rows
+    cells = np.arange(lat_total, dtype=np.float32)
+    row_cosine = np.cos(
+        (cells + np.float32(0.5)) * np.float32(math.pi / lat_total) - np.float32(0.5 * math.pi)
+    ).astype(np.float32)
+    scaled = ((row_cosine / np.float32(COS_FLOOR)) ** 2).astype(np.float32)
+    own_rows = (np.arange(n)[:, None] * rows + np.arange(rows)[None, :]) % lat_rows
+    scales = scaled[np.arange(bands)[:, None, None] * lat_rows + own_rows[None]]
+    face_ids = np.arange(bands)[:, None] * lat_rows + np.arange(lat_rows + 1)[None, :]
+    face_cosine = np.cos(
+        face_ids.astype(np.float32) * np.float32(math.pi / lat_total) - np.float32(0.5 * math.pi)
+    ).astype(np.float32)
+    face_cosine = np.where((face_ids == 0) | (face_ids == lat_total), 0.0, face_cosine)
+    halves = (np.float32(0.5) * face_cosine).astype(np.float32)
+    return jnp.asarray(scales.reshape(-1)), jnp.asarray(halves.reshape(-1))
+
+
+def exchange_all(flat_winds, lat_rows, tracers):
     flat_rows, columns = flat_winds.shape
     levels, lon_cols, merged = tracers.shape
     n = lax.axis_size("lon")
-    lon_index = lax.axis_index("lon")
     rows = flat_rows // n
-    lat_rows = row_cosine.shape[0]
     tracer_count = merged // lat_rows
-    own_cosine = lax.dynamic_slice_in_dim(
-        jnp.tile(row_cosine, flat_rows // lat_rows), lon_index * rows, rows, 0
-    )
-    scaled = (own_cosine / COS_FLOOR) ** 2
-    scaled = jnp.tile(scaled, n).reshape(n * rows, 1)
-    half_cosine = 0.5 * face_cosine
+    scales, halves = position_tables(n, rows, lax.axis_size("lat"), lat_rows, flat_rows)
     pair_rows = np.zeros((columns + 2, columns + 1), np.float32)
     for face in range(columns + 1):
         pair_rows[columns if face == 0 else face - 1, face] = 0.5
         pair_rows[columns + 1 if face == columns else face, face] = 0.5
-    faces = jnp.arange(lat_rows + 1)[:, None]
-    cells = jnp.arange(lat_rows)[None, :]
-    face_weights = jnp.where((cells == faces - 1) | (cells == faces), half_cosine[:, None], 0.0)
-    south_weight = jnp.where(faces == 0, half_cosine[:, None], 0.0)
-    north_weight = jnp.where(faces == lat_rows, half_cosine[:, None], 0.0)
     vmem = pl.BlockSpec(memory_space=pltpu.VMEM)
+    smem = pl.BlockSpec(memory_space=pltpu.SMEM)
     wide_lanes = -(-3 * tracer_count // 128) * 128
     west_cols = lon_cols - (lon_cols - 3) // 8 * 8
     shapes = [
@@ -321,7 +340,9 @@
     return pl.pallas_call(
         functools.partial(filter_kernel, n, rows),
         out_shape=[jax.ShapeDtypeStruct(shape, jnp.float32) for shape in shapes],
-        in_specs=[vmem] * 17 + [pl.BlockSpec(memory_space=pl.ANY)],
+        in_specs=[vmem, smem]
+        + [vmem] * 12
+        + [smem, pl.BlockSpec(memory_space=pl.ANY)],
         out_specs=[vmem] * len(shapes),
         scratch_shapes=[
             pltpu.VMEM((flat_rows, columns + 2), jnp.float32),
@@ -342,12 +363,10 @@
         compiler_params=pltpu.CompilerParams(collective_id=0, has_side_effects=True),
     )(
         flat_winds,
-        scaled,
+        scales,
         *spectral_tables(n, rows, columns),
         jnp.asarray(pair_rows),
-        face_weights,
-        south_weight,
-        north_weight,
+        halves,
         tracers,
     )
 
@@ -392,11 +411,8 @@
         (row_ids.astype(jnp.float32) + 0.5) * (math.pi / lat_total) - 0.5 * math.pi
     )
     flat_winds = wind_field.reshape(2 * levels * lat_rows, lon_cols)
-    face_ids = first_row + jnp.arange(lat_rows + 1, dtype=jnp.int32)
-    face_cosine = jnp.cos(face_ids.astype(jnp.float32) * (math.pi / lat_total) - 0.5 * math.pi)
-    face_cosine = jnp.where((face_ids == 0) | (face_ids == lat_total), 0.0, face_cosine)
     smoothed, zonal_speed, merid_speed, west, east, south, north = exchange_all(
-        flat_winds, row_cosine, face_cosine, tracers
+        flat_winds, lat_rows, tracers
     )
     west = west[:, west.shape[1] - 3 :]
     east = east[:, :3]

time: 54.4 us -> 52 us (0.956)
  other arithmetic: 3.58 us -> 2.12 us
  local copies, waits for them, and re-layouts: 6.56 us -> 5.76 us
    select_n x2 -> x0, other arithmetic: 1.36 us -> none  [the longest x1 0.68 us: exchange_all(): jnp.where((cells == faces - 1) | (cells == faces), half_cosine[:, None],...]
    another operation x4 -> x0, local copies, waits for them, and re-layouts: 0.81 us -> none  [the longest x2 0.72 us: exchange_all(): scaled = jnp.tile(scaled, n).reshape(n * rows, 1)]
where the time goes in v12:
time: 52 us; the launch traced here: 51.8 us
  Pallas kernels  36.9 us (71%)
  matrix products  6.21 us (12%)
  local copies, waits for them, and re-layouts  5.76 us (11%)
  other arithmetic  2.12 us (4%)
  between operations  0.76 us (1%)
    pallas_call x1, Pallas kernels, exchange_all(): pl.pallas_call(functools.partial(filter_kernel, n, rows), out_shape=[jax....  36.9 us
    dot_general x2, matrix products, spread(): return jnp.einsum('ljc,jm->lcm', values, pick, precision=EXACT_MODE)  6.21 us
    unnamed x15, local copies, waits for them, and re-layouts  4.64 us
    sub x1, other arithmetic, local(): advected = tracers - metric[None, None, :] * change  2.05 us

profile of v12, /device:TPU:1, one launch (start us, length us, event | category | flops | bytes accessed | tf_op | source)
XLA Modules:
  0.0 51.8 jit_solution(17598216925201022227)
XLA Ops:
  0.6 2.4 %constant_dynamic-update-slice_fusion.1 = (f32[2,180,840]{2,1,0:T(8,128)S(1)}, f32[2,180,768]{2,1,0:T(8,128)}) fusion(f32[2,180,768]{2,0,1:T(2,128)} %param.16), kind=kLoop, calls=%fused_computation.65 | loop fusion | bytes 3342336
  3.0 0.0 copy-start
  3.0 36.9 %shard_map.167 = (f32[128,180]{1,0:T(8,128)}, f32[2,32,181]{2,1,0:T(8,128)}, f32[2,33,180]{2,1,0:T(8,128)}, f32[2,4,768]{2,1,0:T(4,128)}, f32[2,8,768]{2,1,0:T(8...) custom-call(f32[128,180]{1,0:T(8,128)} %bitcast.10, f32[4096]{0:T(1024)} %constant.88.clone.scales_ref, ...), custom_call_target="tpu_custom_call" | custom-call | tf_op jit(solution)/shard_map/pallas_call | solution.py:340
  40.0 0.9 %constant_dynamic-update-slice_fusion = f32[2,180,840]{2,1,0:T(8,128)S(1)} fusion(f32[2,180,840]{2,1,0:T(8,128)S(1)} %get-tuple-element.20, f32[2,180,72]{2,1,0:T(8,128)} %get-tuple-element.14), kind=kLoop, calls=%fused_computation.64 | loop fusion | bytes 292096 | tf_op jit(solution)/shard_map/concatenate | solution.py:425
  40.9 0.0 copy-done
  40.9 0.0 copy-start.3
  40.9 0.0 copy-start.4
  41.0 0.0 copy-start.5
  41.0 4.4 %fusion.9 = f32[2,180,792]{2,1,0:T(8,128)} fusion(f32[2,180,768]{2,1,0:T(8,128)S(1)} %copy-done, f32[2,180,72]{2,1,0:T(8,128)} %get-tuple-element.13, f32[2,180,840]{2,1,0:T(8,128)S(1)} %constant_dynamic-update-slice_fusion, f32[2,33,180]{2,1,0:T(8,128)} %get-tuple-element.12, s32[792]{0:T(1024)S(1)} %add_select_fusion), kind=kOutput, calls=%fused_computation.17 | convolution fusion | flops 120917016 | bytes 5822208 | tf_op jit(solution)/shard_map/ljc,jm->lcm/dot_general | solution.py:399
  45.4 0.0 copy-done.3
  45.4 0.0 copy-done.4
  45.4 0.0 copy-done.5
  45.4 0.0 copy-start.1
  45.4 1.8 %fusion.27 = f32[2,181,768]{2,1,0:T(8,128)S(1)} fusion(f32[2,3,768]{2,1,0:T(4,128)S(1)} %slice.74, f32[2,3,768]{2,1,0:T(4,128)S(1)} %slice.78, f32[2,180,768]{2,1,0:T(8,128)S(1)} %copy-done, f32[2,32,181]{2,1,0:T(8,128)S(1)} %copy-done.5, s32[768]{0:T(1024)S(1)} %add_select_fusion.1), kind=kOutput, calls=%fused_computation.37 | convolution fusion | flops 115401216 | bytes 2304256 | tf_op jit(solution)/shard_map/ljc,jm->lcm/dot_general | solution.py:399
  47.3 0.1 broadcast.119
  47.4 0.1 reshape.40
  47.5 0.0 copy-done.1
  47.5 2.0 %fusion.30 = f32[2,180,768]{2,1,0:T(8,128)S(1)} fusion(f32[2,180,792]{2,1,0:T(8,128)} %fusion.9, f32[2,181,768]{2,1,0:T(8,128)S(1)} %fusion.27, f32[768]{0:T(1024)S(1)} %reshape.40, f32[2,180,768]{2,0,1:T(2,128)S(1)} %copy-done.1), kind=kLoop, calls=%fused_computation.41 | loop fusion | flops 1382400 | bytes 6638592 | tf_op jit(solution)/shard_map/sub | solution.py:432
  49.6 0.0 copy-start.2
  49.6 1.6 %copy.31 = f32[2,180,768]{2,0,1:T(2,128)} copy(f32[2,180,768]{2,1,0:T(8,128)S(1)} %fusion.30) | data formatting | bytes 2211840
  51.1 0.0 copy-done.2
  51.1 0.7 %copy.37 = f32[2,2,32,180]{3,2,1,0:T(8,128)} copy(f32[2,2,32,180]{3,2,1,0:T(8,128)S(1)} %bitcast.11) | data formatting | bytes 184320
  (5 shorter events, 0.1 us)
Async XLA Ops:
  3.0 37.9 %copy-start = (f32[2,180,768]{2,1,0:T(8,128)S(1)}, f32[2,180,768]{2,1,0:T(8,128)}, u32[]{:S(2)}) copy-start(f32[2,180,768]{2,1,0:T(8,128)} %get-tuple-element.21.tracers_ref) | copy-start | bytes 3317764
  40.9 4.4 %copy-start.3 = (f32[2,4,768]{2,1,0:T(4,128)S(1)}, f32[2,4,768]{2,1,0:T(4,128)}, u32[]{:S(2)}) copy-start(f32[2,4,768]{2,1,0:T(4,128)} %get-tuple-element.10) | copy-start | bytes 73732
  40.9 4.4 %copy-start.4 = (f32[2,8,768]{2,1,0:T(8,128)S(1)}, f32[2,8,768]{2,1,0:T(8,128)}, u32[]{:S(2)}) copy-start(f32[2,8,768]{2,1,0:T(8,128)} %get-tuple-element.11) | copy-start | bytes 147460
  41.0 4.5 %copy-start.5 = (f32[2,32,181]{2,1,0:T(8,128)S(1)}, f32[2,32,181]{2,1,0:T(8,128)}, u32[]{:S(2)}) copy-start(f32[2,32,181]{2,1,0:T(8,128)} %get-tuple-element.9) | copy-start | bytes 139012
  45.4 2.1 %copy-start.1 = (f32[2,180,768]{2,0,1:T(2,128)S(1)}, f32[2,180,768]{2,0,1:T(2,128)}, u32[]{:S(2)}) copy-start(f32[2,180,768]{2,0,1:T(2,128)} %param.16) | copy-start | bytes 3317764
  49.6 1.6 %copy-start.2 = (f32[128,180]{1,0:T(8,128)S(1)}, f32[128,180]{1,0:T(8,128)}, u32[]{:S(2)}) copy-start(f32[128,180]{1,0:T(8,128)} %get-tuple-element.15) | copy-start | bytes 276484

commit v13 on v12

--- a/solution.py
+++ b/solution.py
@@ -64,10 +64,9 @@
 
 
 def filter_kernel(n, rows, winds_ref, scales_ref, kc_ref, ks_ref, tc_ref, ts_ref, c_ref, s_ref,
-                  divisor_ref, zero_ref, widen_ref, prev_ref, next_ref, pairs_ref, halves_ref,
-                  tracers_ref,
-                  smooth_ref, zonal_ref, merid_ref, west_ref, east_ref, south_out, north_out,
-                  out_ref, south_ref, north_ref, vsouth_ref, vnorth_ref,
+                  divisor_ref, zero_ref, widen_ref, prev_ref, next_ref, pairs_ref, tracers_ref,
+                  smooth_ref, zonal_ref, west_ref, east_ref, south_out, north_out, out_ref,
+                  south_ref, north_ref,
                   gathered, restored, send_a, recv_a, send_b, recv_b, halo_send, halo_recv, local_sem):
     me = lax.axis_index("lon")
     band = lax.axis_index("lat")
@@ -92,15 +91,6 @@
         (tracers_ref.at[:, :, pl.ds(merged - lane_depth, lane_depth)], south_ref, (up, me)),
         (tracers_ref.at[:, :, pl.ds(0, lane_depth)], north_ref, (down, me)),
     ]
-    for level in range(2):
-        first = 2 * level_rows + level * level_rows
-        halo_plan.append(
-            (out_ref.at[pl.ds(first + level_rows - 1, 1)], vsouth_ref.at[pl.ds(level, 1)], (up, me))
-        )
-    for level in range(2):
-        first = 2 * level_rows + level * level_rows
-        halo_plan.append((out_ref.at[pl.ds(first, 1)], vnorth_ref.at[pl.ds(level, 1)], (down, me)))
-    edge_rows = [2 * level_rows + k for k in (0, level_rows - 1, level_rows, 2 * level_rows - 1)]
 
     def halo_copy(index):
         source, target, device = halo_plan[index]
@@ -193,46 +183,12 @@
     after = jnp.sum(jnp.where(lane == 0, jnp.roll(result, -rows, axis=0), 0.0), axis=1, keepdims=True)
     restored[...] = jnp.where(lane == columns, before, jnp.where(lane == columns + 1, after, result))
     sends, own = swap(restored, out_ref, send_b, recv_b, 1)
-    own.wait()
-    holders = sorted({row // rows for row in edge_rows})
-
-    def arrival(origin):
-        return pltpu.make_async_remote_copy(
-            src_ref=block(restored, origin),
-            dst_ref=block(out_ref, origin),
-            send_sem=send_b.at[origin],
-            recv_sem=recv_b.at[origin],
-            device_id=(band, origin),
-            device_id_type=MESH,
-        )
-
-    for holder in holders:
-
-        @pl.when(me != holder)
-        def _():
-            arrival(holder).wait_recv()
-
-    wind_halos = [halo_copy(i) for i in range(4, 8)]
-    for copy in wind_halos:
-        copy.start()
-    for k in range(1, n):
-        origin = lax.rem(me + n - k, n)
-        pending = origin >= 0
-        for holder in holders:
-            pending = jnp.logical_and(pending, origin != holder)
-
-        @pl.when(pending)
-        def _():
-            arrival(origin).wait_recv()
-
-    for copy in sends:
+    settle(restored, out_ref, send_b, recv_b, sends, own)
+    smooth_ref[...] = out_ref[:, : smooth_ref.shape[1]]
+    for copy in tracer_halos:
+        copy.wait_recv()
+    for copy in tracer_halos:
         copy.wait_send()
-    smooth_ref[...] = out_ref[:, : smooth_ref.shape[1]]
-    for copy in tracer_halos + wind_halos:
-        copy.wait_recv()
-    for copy in tracer_halos + wind_halos:
-        copy.wait_send()
-
     keep_south = jnp.where(band > 0, 1.0, 0.0)
     keep_north = jnp.where(band < bands - 1, 1.0, 0.0)
     width = south_out.shape[2]
@@ -240,6 +196,38 @@
     south_out[...] = south[..., :width] * keep_south
     north_out[...] = north_ref[..., :width] * keep_north
     band_rows = level_rows
+    for level in range(2):
+        east_rows = out_ref[pl.ds(level * band_rows, band_rows), :]
+        zonal_ref[level] = mm(east_rows, pairs_ref[...])
+
+
+def merid_kernel(wide_ref, halves_ref, after_ref, merid_ref, vsouth_ref, vnorth_ref, send_sem, recv_sem):
+    band = lax.axis_index("lat")
+    me = lax.axis_index("lon")
+    bands = lax.axis_size("lat")
+    up, down = lax.rem(band + 1, bands), lax.rem(band + bands - 1, bands)
+    barrier = pltpu.get_barrier_semaphore()
+    for other in (up, down):
+        pl.semaphore_signal(barrier, inc=1, device_id=(other, me), device_id_type=MESH)
+    pl.semaphore_wait(barrier, 2)
+    band_rows = merid_ref.shape[1] - 1
+    plan = []
+    for level in range(2):
+        first = (2 + level) * band_rows
+        plan.append((wide_ref.at[pl.ds(first + band_rows - 1, 1)], vsouth_ref.at[pl.ds(level, 1)], up))
+        plan.append((wide_ref.at[pl.ds(first, 1)], vnorth_ref.at[pl.ds(level, 1)], down))
+    copies = []
+    for index, (source, target, other) in enumerate(plan):
+        copy = pltpu.make_async_remote_copy(
+            src_ref=source,
+            dst_ref=target,
+            send_sem=send_sem.at[index],
+            recv_sem=recv_sem.at[index],
+            device_id=(other, me),
+            device_id_type=MESH,
+        )
+        copy.start()
+        copies.append(copy)
     face_ids = lax.broadcasted_iota(jnp.int32, (band_rows + 1, 1), 0)
     half = jnp.zeros((band_rows + 1, 1), jnp.float32)
     for face in range(band_rows + 1):
@@ -249,17 +237,48 @@
     face_weights = jnp.where((cells == faces - 1) | (cells == faces), half, 0.0)
     south_weight = jnp.where(face_ids == 0, half, 0.0)
     north_weight = jnp.where(face_ids == band_rows, half, 0.0)
+    inner = [
+        jnp.dot(
+            face_weights,
+            wide_ref[pl.ds((2 + level) * band_rows, band_rows), :],
+            precision=EXACT_MODE,
+            preferred_element_type=jnp.float32,
+        )
+        for level in range(2)
+    ]
+    for copy in copies:
+        copy.wait_recv()
+    for copy in copies:
+        copy.wait_send()
+    keep_south = jnp.where(band > 0, 1.0, 0.0)
+    keep_north = jnp.where(band < bands - 1, 1.0, 0.0)
     for level in range(2):
-        east_rows = out_ref[pl.ds(level * band_rows, band_rows), :]
-        zonal_ref[level] = mm(east_rows, pairs_ref[...])
-        first = 2 * level_rows + level * level_rows
-        north_rows = out_ref[pl.ds(first, band_rows), :]
         merid = (
-            mm(face_weights, north_rows)
+            inner[level]
             + south_weight * (vsouth_ref[pl.ds(level, 1), :] * keep_south)
             + north_weight * (vnorth_ref[pl.ds(level, 1), :] * keep_north)
         )
         merid_ref[level] = merid[:, : merid_ref.shape[2]]
+
+
+def merid_speeds(wide, halves, after, levels, lat_rows, columns):
+    return pl.pallas_call(
+        merid_kernel,
+        out_shape=jax.ShapeDtypeStruct((levels, lat_rows + 1, columns), jnp.float32),
+        in_specs=[
+            pl.BlockSpec(memory_space=pltpu.VMEM),
+            pl.BlockSpec(memory_space=pltpu.SMEM),
+            pl.BlockSpec(memory_space=pltpu.VMEM),
+        ],
+        out_specs=pl.BlockSpec(memory_space=pltpu.VMEM),
+        scratch_shapes=[
+            pltpu.VMEM((levels, columns + 2), jnp.float32),
+            pltpu.VMEM((levels, columns + 2), jnp.float32),
+            pltpu.SemaphoreType.DMA((2 * levels,)),
+            pltpu.SemaphoreType.DMA((2 * levels,)),
+        ],
+        compiler_params=pltpu.CompilerParams(collective_id=1, has_side_effects=True),
+    )(wide, halves, after)
 
 
 def spectral_tables(n, rows, columns):
@@ -331,25 +350,20 @@
     shapes = [
         (flat_rows, columns),
         (levels, lat_rows, columns + 1),
-        (levels, lat_rows + 1, columns),
         (levels, west_cols, merged),
         (levels, 8, merged),
         (levels, lon_cols, 3 * tracer_count),
         (levels, lon_cols, 3 * tracer_count),
+        (flat_rows, columns + 2),
     ]
     return pl.pallas_call(
         functools.partial(filter_kernel, n, rows),
         out_shape=[jax.ShapeDtypeStruct(shape, jnp.float32) for shape in shapes],
-        in_specs=[vmem, smem]
-        + [vmem] * 12
-        + [smem, pl.BlockSpec(memory_space=pl.ANY)],
+        in_specs=[vmem, smem] + [vmem] * 12 + [pl.BlockSpec(memory_space=pl.ANY)],
         out_specs=[vmem] * len(shapes),
         scratch_shapes=[
-            pltpu.VMEM((flat_rows, columns + 2), jnp.float32),
             pltpu.VMEM((levels, lon_cols, wide_lanes), jnp.float32),
             pltpu.VMEM((levels, lon_cols, wide_lanes), jnp.float32),
-            pltpu.VMEM((levels, columns + 2), jnp.float32),
-            pltpu.VMEM((levels, columns + 2), jnp.float32),
             pltpu.VMEM((flat_rows, columns), jnp.float32),
             pltpu.VMEM((flat_rows, columns + 2), jnp.float32),
             pltpu.SemaphoreType.DMA((n,)),
@@ -366,9 +380,8 @@
         scales,
         *spectral_tables(n, rows, columns),
         jnp.asarray(pair_rows),
-        halves,
         tracers,
-    )
+    ), halves
 
 
 def stencil(padded, dim, faces, stride):
@@ -411,17 +424,17 @@
         (row_ids.astype(jnp.float32) + 0.5) * (math.pi / lat_total) - 0.5 * math.pi
     )
     flat_winds = wind_field.reshape(2 * levels * lat_rows, lon_cols)
-    smoothed, zonal_speed, merid_speed, west, east, south, north = exchange_all(
-        flat_winds, lat_rows, tracers
-    )
+    outputs, halves = exchange_all(flat_winds, lat_rows, tracers)
+    smoothed, zonal_speed, west, east, south, north, wide = outputs
     west = west[:, west.shape[1] - 3 :]
     east = east[:, :3]
     smoothed = smoothed.reshape(2, levels, lat_rows, lon_cols)
     zonal_rep = spread(zonal_speed, lat_rows, tracer_count)
-    merid_rep = spread(merid_speed, lat_rows + 1, tracer_count)
     zonal_pad = jnp.concatenate([west, tracers, east], axis=1)
     left_x, right_x = stencil(zonal_pad, 1, lon_cols + 1, 1)
     zonal_flux = upwind(zonal_rep, left_x, right_x)
+    merid_speed = merid_speeds(wide, halves, zonal_flux[:, :8, :128], levels, lat_rows, lon_cols)
+    merid_rep = spread(merid_speed, lat_rows + 1, tracer_count)
     merid_pad = jnp.concatenate([south, tracers, north], axis=2)
     left_y, right_y = stencil(merid_pad, 2, lat_rows + 1, tracer_count)
     merid_flux = upwind(merid_rep, left_y, right_y)

time: 52 us -> 59.8 us (1.15)
  Pallas kernels: 36.9 us -> 40.1 us
  matrix products: 6.21 us -> 8.58 us
  local copies, waits for them, and re-layouts: 5.76 us -> 7.91 us
    pallas_call x0 -> x1, Pallas kernels: none -> 8.34 us  [merid_speeds(): pl.pallas_call(merid_kernel, out_shape=jax.ShapeDtypeStruct((levels, lat_...]
    pallas_call x1, Pallas kernels: 36.9 us -> 31.7 us  [exchange_all(): pl.pallas_call(functools.partial(filter_kernel, n, rows), out_shape=[jax....]
    dot_general x2, matrix products: 6.21 us -> 8.58 us  [spread(): return jnp.einsum('ljc,jm->lcm', values, pick, precision=EXACT_MODE)]
    slice x1, local copies, waits for them, and re-layouts: 0.01 us -> 0.8 us  [local(): east = east[:, :3]]
    slice x1, local copies, waits for them, and re-layouts: 0.01 us -> 0.77 us  [local(): west = west[:, west.shape[1] - 3:]]
    slice x0 -> x1, local copies, waits for them, and re-layouts: none -> 0.6 us  [local(): zonal_flux[:, :8, :128]]
    unnamed x15 -> x13, local copies, waits for them, and re-layouts: 4.64 us -> 4.64 us
where the time goes in v13:
time: 59.8 us; the launch traced here: 59.4 us
  Pallas kernels  40.1 us (67%)
  matrix products  8.58 us (14%)
  local copies, waits for them, and re-layouts  7.91 us (13%)
  other arithmetic  2.11 us (4%)
  between operations  0.74 us (1%)
    pallas_call x1, Pallas kernels, exchange_all(): pl.pallas_call(functools.partial(filter_kernel, n, rows), out_shape=[jax....  31.7 us
    dot_general x2, matrix products, spread(): return jnp.einsum('ljc,jm->lcm', values, pick, precision=EXACT_MODE)  8.58 us
    pallas_call x1, Pallas kernels, merid_speeds(): pl.pallas_call(merid_kernel, out_shape=jax.ShapeDtypeStruct((levels, lat_...  8.34 us
    unnamed x13, local copies, waits for them, and re-layouts  4.64 us
    sub x1, other arithmetic, local(): advected = tracers - metric[None, None, :] * change  2.04 us

profile of v13, /device:TPU:1, one launch (start us, length us, event | category | flops | bytes accessed | tf_op | source)
XLA Modules:
  0.0 59.4 jit_solution(9083495574713758918)
XLA Ops:
  0.6 2.4 %constant_dynamic-update-slice_fusion.1 = (f32[2,180,840]{2,1,0:T(8,128)S(1)}, f32[2,180,768]{2,1,0:T(8,128)}) fusion(f32[2,180,768]{2,0,1:T(2,128)} %param.16), kind=kLoop, calls=%fused_computation.65 | loop fusion | bytes 3342336
  3.0 0.0 copy-start
  3.0 31.7 %shard_map.167 = (f32[128,180]{1,0:T(8,128)}, f32[2,32,181]{2,1,0:T(8,128)}, f32[2,4,768]{2,1,0:T(4,128)}, f32[2,8,768]{2,1,0:T(8,128)}, f32[2,180,72]{2,1,0:T(8...) custom-call(f32[128,180]{1,0:T(8,128)} %bitcast.10, f32[4096]{0:T(1024)} %constant.88.clone.scales_ref, ...), custom_call_target="tpu_custom_call" | custom-call | tf_op jit(solution)/shard_map/pallas_call | solution.py:359
  34.8 0.9 %constant_dynamic-update-slice_fusion = f32[2,180,840]{2,1,0:T(8,128)S(1)} fusion(f32[2,180,840]{2,1,0:T(8,128)S(1)} %get-tuple-element.20, f32[2,180,72]{2,1,0:T(8,128)} %get-tuple-element.14), kind=kLoop, calls=%fused_computation.64 | loop fusion | bytes 292096 | tf_op jit(solution)/shard_map/concatenate | solution.py:438
  35.7 0.0 copy-start.2
  35.7 0.8 %slice.77 = f32[2,3,768]{2,1,0:T(4,128)S(1)} slice(f32[2,4,768]{2,1,0:T(4,128)} %get-tuple-element.10), slice={[0:2], [1:4], [0:768]} | slice | bytes 36864 | tf_op jit(solution)/shard_map/slice | solution.py:429
  36.5 0.8 %slice.81 = f32[2,3,768]{2,1,0:T(4,128)S(1)} slice(f32[2,8,768]{2,1,0:T(8,128)} %get-tuple-element.11), slice={[0:2], [0:3], [0:768]} | slice | bytes 36864 | tf_op jit(solution)/shard_map/slice | solution.py:430
  37.3 0.0 copy-done.2
  37.3 0.0 copy-done
  37.3 0.0 copy-start.4
  37.3 2.9 %fusion.27 = f32[2,181,768]{2,1,0:T(8,128)S(1)} fusion(f32[2,3,768]{2,1,0:T(4,128)S(1)} %slice.77, f32[2,3,768]{2,1,0:T(4,128)S(1)} %slice.81, f32[2,180,768]{2,1,0:T(8,128)S(1)} %copy-done, f32[2,32,181]{2,1,0:T(8,128)} %get-tuple-element.9, s32[768]{0:T(1024)S(1)} %add_select_fusion.1), kind=kOutput, calls=%fused_computation.37 | convolution fusion | flops 115401216 | bytes 2304256 | tf_op jit(solution)/shard_map/ljc,jm->lcm/dot_general | solution.py:412
  40.2 0.6 %slice.106.after_ref = f32[2,8,128]{2,1,0:T(8,128)} slice(f32[2,181,768]{2,1,0:T(8,128)S(1)} %fusion.27), slice={[0:2], [0:8], [0:128]} | slice | bytes 16384 | tf_op jit(solution)/shard_map/slice | solution.py:436
  40.9 8.3 %shard_map.168 = f32[2,33,180]{2,1,0:T(8,128)} custom-call(f32[128,182]{1,0:T(8,128)} %get-tuple-element.12.wide_ref, f32[1056]{0:T(1024)} %constant.89.clone.halves_ref, f32[2,8,128]{2,1,0:T(8,128)} %slice.106.after_ref), custom_call_target="tpu_custom_call" | custom-call | tf_op jit(solution)/shard_map/pallas_call | solution.py:265
  49.2 0.0 copy-done.4
  49.2 0.0 copy-start.1
  49.2 5.6 %fusion.9 = f32[2,180,792]{2,1,0:T(8,128)} fusion(f32[2,180,768]{2,1,0:T(8,128)S(1)} %copy-done, f32[2,180,72]{2,1,0:T(8,128)S(1)} %copy-done.4, f32[2,180,840]{2,1,0:T(8,128)} %copy-done.2, f32[2,33,180]{2,1,0:T(8,128)} %shard_map.168, s32[792]{0:T(1024)S(1)} %add_select_fusion), kind=kOutput, calls=%fused_computation.17 | convolution fusion | flops 120917016 | bytes 5822208 | tf_op jit(solution)/shard_map/ljc,jm->lcm/dot_general | solution.py:412
  54.9 0.1 broadcast.119
  55.0 0.1 reshape.40
  55.1 0.0 copy-done.1
  55.1 2.0 %fusion.30 = f32[2,180,768]{2,1,0:T(8,128)S(1)} fusion(f32[2,180,792]{2,1,0:T(8,128)} %fusion.9, f32[2,181,768]{2,1,0:T(8,128)S(1)} %fusion.27, f32[768]{0:T(1024)S(1)} %reshape.40, f32[2,180,768]{2,0,1:T(2,128)S(1)} %copy-done.1), kind=kLoop, calls=%fused_computation.41 | loop fusion | flops 1382400 | bytes 6638592 | tf_op jit(solution)/shard_map/sub | solution.py:445
  57.2 0.0 copy-start.3
  57.2 1.6 %copy.31 = f32[2,180,768]{2,0,1:T(2,128)} copy(f32[2,180,768]{2,1,0:T(8,128)S(1)} %fusion.30) | data formatting | bytes 2211840
  58.7 0.0 copy-done.3
  58.7 0.7 %copy.37 = f32[2,2,32,180]{3,2,1,0:T(8,128)} copy(f32[2,2,32,180]{3,2,1,0:T(8,128)S(1)} %bitcast.11) | data formatting | bytes 184320
  (3 shorter events, 0.1 us)
Async XLA Ops:
  3.0 34.3 %copy-start = (f32[2,180,768]{2,1,0:T(8,128)S(1)}, f32[2,180,768]{2,1,0:T(8,128)}, u32[]{:S(2)}) copy-start(f32[2,180,768]{2,1,0:T(8,128)} %get-tuple-element.21.tracers_ref) | copy-start | bytes 3317764
  35.7 1.6 %copy-start.2 = (f32[2,180,840]{2,1,0:T(8,128)}, f32[2,180,840]{2,1,0:T(8,128)S(1)}, u32[]{:S(2)}) copy-start(f32[2,180,840]{2,1,0:T(8,128)S(1)} %constant_dynamic-update-slice_fusion) | copy-start | bytes 3628804
  37.3 11.9 %copy-start.4 = (f32[2,180,72]{2,1,0:T(8,128)S(1)}, f32[2,180,72]{2,1,0:T(8,128)}, u32[]{:S(2)}) copy-start(f32[2,180,72]{2,1,0:T(8,128)} %get-tuple-element.13) | copy-start | bytes 311044
  49.2 5.9 %copy-start.1 = (f32[2,180,768]{2,0,1:T(2,128)S(1)}, f32[2,180,768]{2,0,1:T(2,128)}, u32[]{:S(2)}) copy-start(f32[2,180,768]{2,0,1:T(2,128)} %param.16) | copy-start | bytes 3317764
  57.2 1.6 %copy-start.3 = (f32[128,180]{1,0:T(8,128)S(1)}, f32[128,180]{1,0:T(8,128)}, u32[]{:S(2)}) copy-start(f32[128,180]{1,0:T(8,128)} %get-tuple-element.15) | copy-start | bytes 276484

commit v14 on v12

--- a/solution.py
+++ b/solution.py
@@ -68,7 +68,8 @@
                   tracers_ref,
                   smooth_ref, zonal_ref, merid_ref, west_ref, east_ref, south_out, north_out,
                   out_ref, south_ref, north_ref, vsouth_ref, vnorth_ref,
-                  gathered, restored, send_a, recv_a, send_b, recv_b, halo_send, halo_recv, local_sem):
+                  gathered, restored, send_a, recv_a, send_b, recv_b, halo_send, halo_recv, local_sem,
+                  stage_up, stage_down, stage_sem):
     me = lax.axis_index("lon")
     band = lax.axis_index("lat")
     bands = lax.axis_size("lat")
@@ -92,14 +93,8 @@
         (tracers_ref.at[:, :, pl.ds(merged - lane_depth, lane_depth)], south_ref, (up, me)),
         (tracers_ref.at[:, :, pl.ds(0, lane_depth)], north_ref, (down, me)),
     ]
-    for level in range(2):
-        first = 2 * level_rows + level * level_rows
-        halo_plan.append(
-            (out_ref.at[pl.ds(first + level_rows - 1, 1)], vsouth_ref.at[pl.ds(level, 1)], (up, me))
-        )
-    for level in range(2):
-        first = 2 * level_rows + level * level_rows
-        halo_plan.append((out_ref.at[pl.ds(first, 1)], vnorth_ref.at[pl.ds(level, 1)], (down, me)))
+    halo_plan.append((stage_up, vsouth_ref, (up, me)))
+    halo_plan.append((stage_down, vnorth_ref, (down, me)))
     edge_rows = [2 * level_rows + k for k in (0, level_rows - 1, level_rows, 2 * level_rows - 1)]
 
     def halo_copy(index):
@@ -212,7 +207,18 @@
         def _():
             arrival(holder).wait_recv()
 
-    wind_halos = [halo_copy(i) for i in range(4, 8)]
+    staged = []
+    for level in range(2):
+        first = 2 * level_rows + level * level_rows
+        for slot, (row, stage) in enumerate(((first + level_rows - 1, stage_up), (first, stage_down))):
+            copy = pltpu.make_async_copy(
+                out_ref.at[pl.ds(row, 1)], stage.at[pl.ds(level, 1)], stage_sem.at[2 * level + slot]
+            )
+            copy.start()
+            staged.append(copy)
+    for copy in staged:
+        copy.wait()
+    wind_halos = [halo_copy(i) for i in range(4, 6)]
     for copy in wind_halos:
         copy.start()
     for k in range(1, n):
@@ -359,6 +365,9 @@
             pltpu.SemaphoreType.DMA((8,)),
             pltpu.SemaphoreType.DMA((8,)),
             pltpu.SemaphoreType.DMA((2,)),
+            pltpu.VMEM((levels, columns + 2), jnp.float32),
+            pltpu.VMEM((levels, columns + 2), jnp.float32),
+            pltpu.SemaphoreType.DMA((4,)),
         ],
         compiler_params=pltpu.CompilerParams(collective_id=0, has_side_effects=True),
     )(

time: 52 us -> 52 us (level)
  no operation moved by 1% of the time
where the time goes in v14:
time: 52 us; the launch traced here: 51.8 us
  Pallas kernels  36.9 us (71%)
  matrix products  6.21 us (12%)
  local copies, waits for them, and re-layouts  5.76 us (11%)
  other arithmetic  2.12 us (4%)
  between operations  0.76 us (1%)
    pallas_call x1, Pallas kernels, exchange_all(): pl.pallas_call(functools.partial(filter_kernel, n, rows), out_shape=[jax....  36.9 us
    dot_general x2, matrix products, spread(): return jnp.einsum('ljc,jm->lcm', values, pick, precision=EXACT_MODE)  6.21 us
    unnamed x15, local copies, waits for them, and re-layouts  4.64 us
    sub x1, other arithmetic, local(): advected = tracers - metric[None, None, :] * change  2.05 us

profile of v14, /device:TPU:1, one launch (start us, length us, event | category | flops | bytes accessed | tf_op | source)
XLA Modules:
  0.0 51.8 jit_solution(8330195738183812860)
XLA Ops:
  0.6 2.4 %constant_dynamic-update-slice_fusion.1 = (f32[2,180,840]{2,1,0:T(8,128)S(1)}, f32[2,180,768]{2,1,0:T(8,128)}) fusion(f32[2,180,768]{2,0,1:T(2,128)} %param.16), kind=kLoop, calls=%fused_computation.65 | loop fusion | bytes 3342336
  3.0 0.0 copy-start
  3.0 36.9 %shard_map.167 = (f32[128,180]{1,0:T(8,128)}, f32[2,32,181]{2,1,0:T(8,128)}, f32[2,33,180]{2,1,0:T(8,128)}, f32[2,4,768]{2,1,0:T(4,128)}, f32[2,8,768]{2,1,0:T(8...) custom-call(f32[128,180]{1,0:T(8,128)} %bitcast.10, f32[4096]{0:T(1024)} %constant.88.clone.scales_ref, ...), custom_call_target="tpu_custom_call" | custom-call | tf_op jit(solution)/shard_map/pallas_call | solution.py:346
  40.0 0.9 %constant_dynamic-update-slice_fusion = f32[2,180,840]{2,1,0:T(8,128)S(1)} fusion(f32[2,180,840]{2,1,0:T(8,128)S(1)} %get-tuple-element.20, f32[2,180,72]{2,1,0:T(8,128)} %get-tuple-element.14), kind=kLoop, calls=%fused_computation.64 | loop fusion | bytes 292096 | tf_op jit(solution)/shard_map/concatenate | solution.py:434
  40.9 0.0 copy-done
  40.9 0.0 copy-start.3
  41.0 0.0 copy-start.4
  41.0 0.0 copy-start.5
  41.0 4.4 %fusion.9 = f32[2,180,792]{2,1,0:T(8,128)} fusion(f32[2,180,768]{2,1,0:T(8,128)S(1)} %copy-done, f32[2,180,72]{2,1,0:T(8,128)} %get-tuple-element.13, f32[2,180,840]{2,1,0:T(8,128)S(1)} %constant_dynamic-update-slice_fusion, f32[2,33,180]{2,1,0:T(8,128)} %get-tuple-element.12, s32[792]{0:T(1024)S(1)} %add_select_fusion), kind=kOutput, calls=%fused_computation.17 | convolution fusion | flops 120917016 | bytes 5822208 | tf_op jit(solution)/shard_map/ljc,jm->lcm/dot_general | solution.py:408
  45.4 0.0 copy-done.3
  45.4 0.0 copy-done.4
  45.4 0.0 copy-done.5
  45.4 0.0 copy-start.1
  45.4 1.8 %fusion.27 = f32[2,181,768]{2,1,0:T(8,128)S(1)} fusion(f32[2,3,768]{2,1,0:T(4,128)S(1)} %slice.74, f32[2,3,768]{2,1,0:T(4,128)S(1)} %slice.78, f32[2,180,768]{2,1,0:T(8,128)S(1)} %copy-done, f32[2,32,181]{2,1,0:T(8,128)S(1)} %copy-done.5, s32[768]{0:T(1024)S(1)} %add_select_fusion.1), kind=kOutput, calls=%fused_computation.37 | convolution fusion | flops 115401216 | bytes 2304256 | tf_op jit(solution)/shard_map/ljc,jm->lcm/dot_general | solution.py:408
  47.3 0.1 broadcast.119
  47.4 0.1 reshape.40
  47.5 0.0 copy-done.1
  47.5 2.0 %fusion.30 = f32[2,180,768]{2,1,0:T(8,128)S(1)} fusion(f32[2,180,792]{2,1,0:T(8,128)} %fusion.9, f32[2,181,768]{2,1,0:T(8,128)S(1)} %fusion.27, f32[768]{0:T(1024)S(1)} %reshape.40, f32[2,180,768]{2,0,1:T(2,128)S(1)} %copy-done.1), kind=kLoop, calls=%fused_computation.41 | loop fusion | flops 1382400 | bytes 6638592 | tf_op jit(solution)/shard_map/sub | solution.py:441
  49.6 0.0 copy-start.2
  49.6 1.6 %copy.31 = f32[2,180,768]{2,0,1:T(2,128)} copy(f32[2,180,768]{2,1,0:T(8,128)S(1)} %fusion.30) | data formatting | bytes 2211840
  51.1 0.0 copy-done.2
  51.1 0.7 %copy.37 = f32[2,2,32,180]{3,2,1,0:T(8,128)} copy(f32[2,2,32,180]{3,2,1,0:T(8,128)S(1)} %bitcast.11) | data formatting | bytes 184320
  (5 shorter events, 0.1 us)
Async XLA Ops:
  3.0 37.9 %copy-start = (f32[2,180,768]{2,1,0:T(8,128)S(1)}, f32[2,180,768]{2,1,0:T(8,128)}, u32[]{:S(2)}) copy-start(f32[2,180,768]{2,1,0:T(8,128)} %get-tuple-element.21.tracers_ref) | copy-start | bytes 3317764
  40.9 4.4 %copy-start.3 = (f32[2,4,768]{2,1,0:T(4,128)S(1)}, f32[2,4,768]{2,1,0:T(4,128)}, u32[]{:S(2)}) copy-start(f32[2,4,768]{2,1,0:T(4,128)} %get-tuple-element.10) | copy-start | bytes 73732
  41.0 4.4 %copy-start.4 = (f32[2,8,768]{2,1,0:T(8,128)S(1)}, f32[2,8,768]{2,1,0:T(8,128)}, u32[]{:S(2)}) copy-start(f32[2,8,768]{2,1,0:T(8,128)} %get-tuple-element.11) | copy-start | bytes 147460
  41.0 4.5 %copy-start.5 = (f32[2,32,181]{2,1,0:T(8,128)S(1)}, f32[2,32,181]{2,1,0:T(8,128)}, u32[]{:S(2)}) copy-start(f32[2,32,181]{2,1,0:T(8,128)} %get-tuple-element.9) | copy-start | bytes 139012
  45.4 2.1 %copy-start.1 = (f32[2,180,768]{2,0,1:T(2,128)S(1)}, f32[2,180,768]{2,0,1:T(2,128)}, u32[]{:S(2)}) copy-start(f32[2,180,768]{2,0,1:T(2,128)} %param.16) | copy-start | bytes 3317764
  49.6 1.6 %copy-start.2 = (f32[128,180]{1,0:T(8,128)S(1)}, f32[128,180]{1,0:T(8,128)}, u32[]{:S(2)}) copy-start(f32[128,180]{1,0:T(8,128)} %get-tuple-element.15) | copy-start | bytes 276484

commit v15 on v12

--- a/solution.py
+++ b/solution.py
@@ -228,17 +228,8 @@
     for copy in sends:
         copy.wait_send()
     smooth_ref[...] = out_ref[:, : smooth_ref.shape[1]]
-    for copy in tracer_halos + wind_halos:
-        copy.wait_recv()
-    for copy in tracer_halos + wind_halos:
-        copy.wait_send()
-
     keep_south = jnp.where(band > 0, 1.0, 0.0)
     keep_north = jnp.where(band < bands - 1, 1.0, 0.0)
-    width = south_out.shape[2]
-    south = pltpu.roll(south_ref[...], width, 2)
-    south_out[...] = south[..., :width] * keep_south
-    north_out[...] = north_ref[..., :width] * keep_north
     band_rows = level_rows
     face_ids = lax.broadcasted_iota(jnp.int32, (band_rows + 1, 1), 0)
     half = jnp.zeros((band_rows + 1, 1), jnp.float32)
@@ -249,13 +240,25 @@
     face_weights = jnp.where((cells == faces - 1) | (cells == faces), half, 0.0)
     south_weight = jnp.where(face_ids == 0, half, 0.0)
     north_weight = jnp.where(face_ids == band_rows, half, 0.0)
+    inner = []
     for level in range(2):
         east_rows = out_ref[pl.ds(level * band_rows, band_rows), :]
         zonal_ref[level] = mm(east_rows, pairs_ref[...])
         first = 2 * level_rows + level * level_rows
-        north_rows = out_ref[pl.ds(first, band_rows), :]
+        inner.append(mm(face_weights, out_ref[pl.ds(first, band_rows), :]))
+    for copy in tracer_halos:
+        copy.wait_recv()
+    width = south_out.shape[2]
+    south = pltpu.roll(south_ref[...], width, 2)
+    south_out[...] = south[..., :width] * keep_south
+    north_out[...] = north_ref[..., :width] * keep_north
+    for copy in wind_halos:
+        copy.wait_recv()
+    for copy in tracer_halos + wind_halos:
+        copy.wait_send()
+    for level in range(2):
         merid = (
-            mm(face_weights, north_rows)
+            inner[level]
             + south_weight * (vsouth_ref[pl.ds(level, 1), :] * keep_south)
             + north_weight * (vnorth_ref[pl.ds(level, 1), :] * keep_north)
         )

time: 52 us -> 51.8 us (level)
  no operation moved by 1% of the time
where the time goes in v15:
time: 51.8 us; the launch traced here: 51.6 us
  Pallas kernels  36.7 us (71%)
  matrix products  6.22 us (12%)
  local copies, waits for them, and re-layouts  5.76 us (11%)
  other arithmetic  2.12 us (4%)
  between operations  0.76 us (1%)
    pallas_call x1, Pallas kernels, exchange_all(): pl.pallas_call(functools.partial(filter_kernel, n, rows), out_shape=[jax....  36.7 us
    dot_general x2, matrix products, spread(): return jnp.einsum('ljc,jm->lcm', values, pick, precision=EXACT_MODE)  6.22 us
    unnamed x15, local copies, waits for them, and re-layouts  4.64 us
    sub x1, other arithmetic, local(): advected = tracers - metric[None, None, :] * change  2.05 us

profile of v15, /device:TPU:1, one launch (start us, length us, event | category | flops | bytes accessed | tf_op | source)
XLA Modules:
  0.0 51.6 jit_solution(15702918456257171504)
XLA Ops:
  0.6 2.4 %constant_dynamic-update-slice_fusion.1 = (f32[2,180,840]{2,1,0:T(8,128)S(1)}, f32[2,180,768]{2,1,0:T(8,128)}) fusion(f32[2,180,768]{2,0,1:T(2,128)} %param.16), kind=kLoop, calls=%fused_computation.65 | loop fusion | bytes 3342336
  3.0 0.0 copy-start
  3.0 36.7 %shard_map.167 = (f32[128,180]{1,0:T(8,128)}, f32[2,32,181]{2,1,0:T(8,128)}, f32[2,33,180]{2,1,0:T(8,128)}, f32[2,4,768]{2,1,0:T(4,128)}, f32[2,8,768]{2,1,0:T(8...) custom-call(f32[128,180]{1,0:T(8,128)} %bitcast.10, f32[4096]{0:T(1024)} %constant.88.clone.scales_ref, ...), custom_call_target="tpu_custom_call" | custom-call | tf_op jit(solution)/shard_map/pallas_call | solution.py:343
  39.7 0.9 %constant_dynamic-update-slice_fusion = f32[2,180,840]{2,1,0:T(8,128)S(1)} fusion(f32[2,180,840]{2,1,0:T(8,128)S(1)} %get-tuple-element.20, f32[2,180,72]{2,1,0:T(8,128)} %get-tuple-element.14), kind=kLoop, calls=%fused_computation.64 | loop fusion | bytes 292096 | tf_op jit(solution)/shard_map/concatenate | solution.py:428
  40.7 0.0 copy-done
  40.7 0.0 copy-start.3
  40.7 0.0 copy-start.4
  40.7 0.0 copy-start.5
  40.7 4.4 %fusion.9 = f32[2,180,792]{2,1,0:T(8,128)} fusion(f32[2,180,768]{2,1,0:T(8,128)S(1)} %copy-done, f32[2,180,72]{2,1,0:T(8,128)} %get-tuple-element.13, f32[2,180,840]{2,1,0:T(8,128)S(1)} %constant_dynamic-update-slice_fusion, f32[2,33,180]{2,1,0:T(8,128)} %get-tuple-element.12, s32[792]{0:T(1024)S(1)} %add_select_fusion), kind=kOutput, calls=%fused_computation.17 | convolution fusion | flops 120917016 | bytes 5822208 | tf_op jit(solution)/shard_map/ljc,jm->lcm/dot_general | solution.py:402
  45.1 0.0 copy-done.3
  45.2 0.0 copy-done.4
  45.2 0.0 copy-done.5
  45.2 0.0 copy-start.1
  45.2 1.8 %fusion.27 = f32[2,181,768]{2,1,0:T(8,128)S(1)} fusion(f32[2,3,768]{2,1,0:T(4,128)S(1)} %slice.74, f32[2,3,768]{2,1,0:T(4,128)S(1)} %slice.78, f32[2,180,768]{2,1,0:T(8,128)S(1)} %copy-done, f32[2,32,181]{2,1,0:T(8,128)S(1)} %copy-done.5, s32[768]{0:T(1024)S(1)} %add_select_fusion.1), kind=kOutput, calls=%fused_computation.37 | convolution fusion | flops 115401216 | bytes 2304256 | tf_op jit(solution)/shard_map/ljc,jm->lcm/dot_general | solution.py:402
  47.1 0.1 broadcast.119
  47.2 0.1 reshape.40
  47.3 0.0 copy-done.1
  47.3 2.0 %fusion.30 = f32[2,180,768]{2,1,0:T(8,128)S(1)} fusion(f32[2,180,792]{2,1,0:T(8,128)} %fusion.9, f32[2,181,768]{2,1,0:T(8,128)S(1)} %fusion.27, f32[768]{0:T(1024)S(1)} %reshape.40, f32[2,180,768]{2,0,1:T(2,128)S(1)} %copy-done.1), kind=kLoop, calls=%fused_computation.41 | loop fusion | flops 1382400 | bytes 6638592 | tf_op jit(solution)/shard_map/sub | solution.py:435
  49.3 0.0 copy-start.2
  49.3 1.6 %copy.31 = f32[2,180,768]{2,0,1:T(2,128)} copy(f32[2,180,768]{2,1,0:T(8,128)S(1)} %fusion.30) | data formatting | bytes 2211840
  50.9 0.0 copy-done.2
  50.9 0.7 %copy.37 = f32[2,2,32,180]{3,2,1,0:T(8,128)} copy(f32[2,2,32,180]{3,2,1,0:T(8,128)S(1)} %bitcast.11) | data formatting | bytes 184320
  (5 shorter events, 0.1 us)
Async XLA Ops:
  3.0 37.7 %copy-start = (f32[2,180,768]{2,1,0:T(8,128)S(1)}, f32[2,180,768]{2,1,0:T(8,128)}, u32[]{:S(2)}) copy-start(f32[2,180,768]{2,1,0:T(8,128)} %get-tuple-element.21.tracers_ref) | copy-start | bytes 3317764
  40.7 4.4 %copy-start.3 = (f32[2,4,768]{2,1,0:T(4,128)S(1)}, f32[2,4,768]{2,1,0:T(4,128)}, u32[]{:S(2)}) copy-start(f32[2,4,768]{2,1,0:T(4,128)} %get-tuple-element.10) | copy-start | bytes 73732
  40.7 4.4 %copy-start.4 = (f32[2,8,768]{2,1,0:T(8,128)S(1)}, f32[2,8,768]{2,1,0:T(8,128)}, u32[]{:S(2)}) copy-start(f32[2,8,768]{2,1,0:T(8,128)} %get-tuple-element.11) | copy-start | bytes 147460
  40.7 4.5 %copy-start.5 = (f32[2,32,181]{2,1,0:T(8,128)S(1)}, f32[2,32,181]{2,1,0:T(8,128)}, u32[]{:S(2)}) copy-start(f32[2,32,181]{2,1,0:T(8,128)} %get-tuple-element.9) | copy-start | bytes 139012
  45.2 2.1 %copy-start.1 = (f32[2,180,768]{2,0,1:T(2,128)S(1)}, f32[2,180,768]{2,0,1:T(2,128)}, u32[]{:S(2)}) copy-start(f32[2,180,768]{2,0,1:T(2,128)} %param.16) | copy-start | bytes 3317764
  49.3 1.6 %copy-start.2 = (f32[128,180]{1,0:T(8,128)S(1)}, f32[128,180]{1,0:T(8,128)}, u32[]{:S(2)}) copy-start(f32[128,180]{1,0:T(8,128)} %get-tuple-element.15) | copy-start | bytes 276484

commit v16 on v15

--- a/solution.py
+++ b/solution.py
@@ -399,7 +399,7 @@
 def spread(values, rows, tracer_count):
     lanes = jnp.arange(rows * tracer_count, dtype=jnp.int32) // tracer_count
     pick = (jnp.arange(rows, dtype=jnp.int32)[:, None] == lanes[None, :]).astype(jnp.float32)
-    return jnp.einsum("ljc,jm->lcm", values, pick, precision=EXACT_MODE)
+    return jnp.einsum("ljc,jm->lcm", values, pick, precision=lax.Precision.HIGH)
 
 
 def local(tracers, wind_field):

time: 51.8 us -> 51.6 us (level)
  no operation moved by 1% of the time
where the time goes in v16:
time: 51.6 us; the launch traced here: 51.4 us
  Pallas kernels  36.7 us (71%)
  matrix products  6.01 us (12%)
  local copies, waits for them, and re-layouts  5.76 us (11%)
  other arithmetic  2.12 us (4%)
  between operations  0.76 us (1%)
    pallas_call x1, Pallas kernels, exchange_all(): pl.pallas_call(functools.partial(filter_kernel, n, rows), out_shape=[jax....  36.7 us
    dot_general x2, matrix products, spread(): return jnp.einsum('ljc,jm->lcm', values, pick, precision=lax.Precision.HIGH)  6.01 us
    unnamed x15, local copies, waits for them, and re-layouts  4.64 us
    sub x1, other arithmetic, local(): advected = tracers - metric[None, None, :] * change  2.05 us

profile of v16, /device:TPU:1, one launch (start us, length us, event | category | flops | bytes accessed | tf_op | source)
XLA Modules:
  0.0 51.4 jit_solution(7877763463757450758)
XLA Ops:
  0.6 2.4 %constant_dynamic-update-slice_fusion.1 = (f32[2,180,840]{2,1,0:T(8,128)S(1)}, f32[2,180,768]{2,1,0:T(8,128)}) fusion(f32[2,180,768]{2,0,1:T(2,128)} %param.16), kind=kLoop, calls=%fused_computation.65 | loop fusion | bytes 3342336
  3.0 0.0 copy-start
  3.0 36.7 %shard_map.167 = (f32[128,180]{1,0:T(8,128)}, f32[2,32,181]{2,1,0:T(8,128)}, f32[2,33,180]{2,1,0:T(8,128)}, f32[2,4,768]{2,1,0:T(4,128)}, f32[2,8,768]{2,1,0:T(8...) custom-call(f32[128,180]{1,0:T(8,128)} %bitcast.10, f32[4096]{0:T(1024)} %constant.88.clone.scales_ref, ...), custom_call_target="tpu_custom_call" | custom-call | tf_op jit(solution)/shard_map/pallas_call | solution.py:343
  39.7 0.9 %constant_dynamic-update-slice_fusion = f32[2,180,840]{2,1,0:T(8,128)S(1)} fusion(f32[2,180,840]{2,1,0:T(8,128)S(1)} %get-tuple-element.20, f32[2,180,72]{2,1,0:T(8,128)} %get-tuple-element.14), kind=kLoop, calls=%fused_computation.64 | loop fusion | bytes 292096 | tf_op jit(solution)/shard_map/concatenate | solution.py:428
  40.7 0.0 copy-done
  40.7 0.0 copy-start.3
  40.7 0.0 copy-start.4
  40.7 0.0 copy-start.5
  40.7 4.3 %fusion.9 = f32[2,180,792]{2,1,0:T(8,128)} fusion(f32[2,180,768]{2,1,0:T(8,128)S(1)} %copy-done, f32[2,180,72]{2,1,0:T(8,128)} %get-tuple-element.13, f32[2,180,840]{2,1,0:T(8,128)S(1)} %constant_dynamic-update-slice_fusion, f32[2,33,180]{2,1,0:T(8,128)} %get-tuple-element.12, s32[792]{0:T(1024)S(1)} %add_select_fusion), kind=kOutput, calls=%fused_computation.17 | convolution fusion | flops 64463256 | bytes 5822208 | tf_op jit(solution)/shard_map/ljc,jm->lcm/dot_general | solution.py:402
  45.1 0.0 copy-done.3
  45.1 0.0 copy-done.4
  45.1 0.0 copy-done.5
  45.2 0.0 copy-start.1
  45.2 1.7 %fusion.27 = f32[2,181,768]{2,1,0:T(8,128)S(1)} fusion(f32[2,3,768]{2,1,0:T(4,128)S(1)} %slice.74, f32[2,3,768]{2,1,0:T(4,128)S(1)} %slice.78, f32[2,180,768]{2,1,0:T(8,128)S(1)} %copy-done, f32[2,32,181]{2,1,0:T(8,128)S(1)} %copy-done.5, s32[768]{0:T(1024)S(1)} %add_select_fusion.1), kind=kOutput, calls=%fused_computation.37 | convolution fusion | flops 62022144 | bytes 2304256 | tf_op jit(solution)/shard_map/ljc,jm->lcm/dot_general | solution.py:402
  46.9 0.1 broadcast.119
  47.0 0.1 reshape.40
  47.1 0.0 copy-done.1
  47.1 2.0 %fusion.30 = f32[2,180,768]{2,1,0:T(8,128)S(1)} fusion(f32[2,180,792]{2,1,0:T(8,128)} %fusion.9, f32[2,181,768]{2,1,0:T(8,128)S(1)} %fusion.27, f32[768]{0:T(1024)S(1)} %reshape.40, f32[2,180,768]{2,0,1:T(2,128)S(1)} %copy-done.1), kind=kLoop, calls=%fused_computation.41 | loop fusion | flops 1382400 | bytes 6638592 | tf_op jit(solution)/shard_map/sub | solution.py:435
  49.1 0.0 copy-start.2
  49.1 1.6 %copy.31 = f32[2,180,768]{2,0,1:T(2,128)} copy(f32[2,180,768]{2,1,0:T(8,128)S(1)} %fusion.30) | data formatting | bytes 2211840
  50.7 0.0 copy-done.2
  50.7 0.7 %copy.37 = f32[2,2,32,180]{3,2,1,0:T(8,128)} copy(f32[2,2,32,180]{3,2,1,0:T(8,128)S(1)} %bitcast.11) | data formatting | bytes 184320
  (5 shorter events, 0.1 us)
Async XLA Ops:
  3.0 37.7 %copy-start = (f32[2,180,768]{2,1,0:T(8,128)S(1)}, f32[2,180,768]{2,1,0:T(8,128)}, u32[]{:S(2)}) copy-start(f32[2,180,768]{2,1,0:T(8,128)} %get-tuple-element.21.tracers_ref) | copy-start | bytes 3317764
  40.7 4.4 %copy-start.3 = (f32[2,4,768]{2,1,0:T(4,128)S(1)}, f32[2,4,768]{2,1,0:T(4,128)}, u32[]{:S(2)}) copy-start(f32[2,4,768]{2,1,0:T(4,128)} %get-tuple-element.10) | copy-start | bytes 73732
  40.7 4.4 %copy-start.4 = (f32[2,8,768]{2,1,0:T(8,128)S(1)}, f32[2,8,768]{2,1,0:T(8,128)}, u32[]{:S(2)}) copy-start(f32[2,8,768]{2,1,0:T(8,128)} %get-tuple-element.11) | copy-start | bytes 147460
  40.7 4.4 %copy-start.5 = (f32[2,32,181]{2,1,0:T(8,128)S(1)}, f32[2,32,181]{2,1,0:T(8,128)}, u32[]{:S(2)}) copy-start(f32[2,32,181]{2,1,0:T(8,128)} %get-tuple-element.9) | copy-start | bytes 139012
  45.2 1.9 %copy-start.1 = (f32[2,180,768]{2,0,1:T(2,128)S(1)}, f32[2,180,768]{2,0,1:T(2,128)}, u32[]{:S(2)}) copy-start(f32[2,180,768]{2,0,1:T(2,128)} %param.16) | copy-start | bytes 3317764
  49.1 1.6 %copy-start.2 = (f32[128,180]{1,0:T(8,128)S(1)}, f32[128,180]{1,0:T(8,128)}, u32[]{:S(2)}) copy-start(f32[128,180]{1,0:T(8,128)} %get-tuple-element.15) | copy-start | bytes 276484

commit v17 on v15

--- a/solution.py
+++ b/solution.py
@@ -421,7 +421,7 @@
     east = east[:, :3]
     smoothed = smoothed.reshape(2, levels, lat_rows, lon_cols)
     zonal_rep = spread(zonal_speed, lat_rows, tracer_count)
-    merid_rep = spread(merid_speed, lat_rows + 1, tracer_count)
+    merid_rep = lax.optimization_barrier(spread(merid_speed, lat_rows + 1, tracer_count))
     zonal_pad = jnp.concatenate([west, tracers, east], axis=1)
     left_x, right_x = stencil(zonal_pad, 1, lon_cols + 1, 1)
     zonal_flux = upwind(zonal_rep, left_x, right_x)

time: 51.8 us -> 50.7 us (0.979)
  matrix products: 6.22 us -> 3.45 us
  other arithmetic: 2.12 us -> 3.76 us
    dot_general x2, matrix products: 6.22 us -> 3.45 us  [spread(): return jnp.einsum('ljc,jm->lcm', values, pick, precision=EXACT_MODE)]
    add x0 -> x1, other arithmetic: none -> 2.02 us  [upwind(): return jnp.maximum(speed, 0.0) * left + jnp.minimum(speed, 0.0) * right]
where the time goes in v17:
time: 50.7 us; the launch traced here: 50.4 us
  Pallas kernels  36.6 us (72%)
  local copies, waits for them, and re-layouts  5.86 us (12%)
  other arithmetic  3.76 us (7%)
  matrix products  3.45 us (7%)
  between operations  0.8 us (2%)
    pallas_call x1, Pallas kernels, exchange_all(): pl.pallas_call(functools.partial(filter_kernel, n, rows), out_shape=[jax....  36.6 us
    unnamed x15, local copies, waits for them, and re-layouts  4.64 us
    dot_general x2, matrix products, spread(): return jnp.einsum('ljc,jm->lcm', values, pick, precision=EXACT_MODE)  3.45 us
    add x1, other arithmetic, upwind(): return jnp.maximum(speed, 0.0) * left + jnp.minimum(speed, 0.0) * right  2.02 us
    sub x1, other arithmetic, local(): advected = tracers - metric[None, None, :] * change  1.67 us
    concatenate x1, local copies, waits for them, and re-layouts, local(): merid_pad = jnp.concatenate([south, tracers, north], axis=2)  1.04 us

profile of v17, /device:TPU:1, one launch (start us, length us, event | category | flops | bytes accessed | tf_op | source)
XLA Modules:
  0.0 50.4 jit_solution(4638850058304900569)
XLA Ops:
  0.6 2.4 %constant_dynamic-update-slice_fusion.1 = (f32[2,180,840]{2,1,0:T(8,128)S(1)}, f32[2,180,768]{2,1,0:T(8,128)}) fusion(f32[2,180,768]{2,0,1:T(2,128)} %param.16), kind=kLoop, calls=%fused_computation.66 | loop fusion | bytes 3342336
  3.0 36.6 %shard_map.167 = (f32[128,180]{1,0:T(8,128)}, f32[2,32,181]{2,1,0:T(8,128)}, f32[2,33,180]{2,1,0:T(8,128)}, f32[2,4,768]{2,1,0:T(4,128)}, f32[2,8,768]{2,1,0:T(8...) custom-call(f32[128,180]{1,0:T(8,128)} %bitcast.10, f32[4096]{0:T(1024)} %constant.88.clone.scales_ref, ...), custom_call_target="tpu_custom_call" | custom-call | tf_op jit(solution)/shard_map/pallas_call | solution.py:343
  39.6 0.0 copy-start
  39.6 0.0 copy-start.1
  39.6 1.0 %constant_dynamic-update-slice_fusion = f32[2,180,840]{2,1,0:T(8,128)S(1)} fusion(f32[2,180,840]{2,1,0:T(8,128)S(1)} %get-tuple-element.20, f32[2,180,72]{2,1,0:T(8,128)} %get-tuple-element.14), kind=kLoop, calls=%fused_computation.65 | loop fusion | bytes 292096 | tf_op jit(solution)/shard_map/concatenate | solution.py:428
  40.7 1.6 %fusion.39 = f32[2,180,792]{2,1,0:T(8,128)S(1)} fusion(f32[2,33,180]{2,1,0:T(8,128)} %get-tuple-element.12, s32[792]{0:T(1024)S(1)} %add_select_fusion), kind=kOutput, calls=%fused_computation.54 | convolution fusion | flops 112933656 | bytes 1191168 | tf_op jit(solution)/shard_map/ljc,jm->lcm/dot_general | solution.py:402
  42.3 0.0 copy-done
  42.3 0.0 copy-done.1
  42.3 0.0 copy-start.3
  42.3 0.0 copy-start.4
  42.4 0.0 copy-start.5
  42.4 2.0 %fusion.9 = f32[2,180,792]{2,1,0:T(8,128)S(1)} fusion(f32[2,180,768]{2,1,0:T(8,128)S(1)} %copy-done, f32[2,180,72]{2,1,0:T(8,128)S(1)} %copy-done.1, f32[2,180,840]{2,1,0:T(8,128)S(1)} %constant_dynamic-update-slice_fusion, f32[2,180,792]{2,1,0:T(8,128)S(1)} %fusion.39), kind=kLoop, calls=%fused_computation.17 | loop fusion | flops 7983360 | bytes 6912000 | tf_op jit(solution)/shard_map/add | solution.py:63
  44.4 0.0 copy-done.3
  44.4 0.0 copy-done.4
  44.5 0.0 copy-done.5
  44.5 1.8 %fusion.27 = f32[2,181,768]{2,1,0:T(8,128)S(1)} fusion(f32[2,3,768]{2,1,0:T(4,128)S(1)} %slice.74, f32[2,3,768]{2,1,0:T(4,128)S(1)} %slice.78, f32[2,180,768]{2,1,0:T(8,128)S(1)} %copy-done, f32[2,32,181]{2,1,0:T(8,128)S(1)} %copy-done.5, s32[768]{0:T(1024)S(1)} %add_select_fusion.1), kind=kOutput, calls=%fused_computation.37 | convolution fusion | flops 115401216 | bytes 2304256 | tf_op jit(solution)/shard_map/ljc,jm->lcm/dot_general | solution.py:402
  46.4 0.1 broadcast.119
  46.4 0.1 reshape.40
  46.5 1.7 %fusion.30 = f32[2,180,768]{2,1,0:T(8,128)S(1)} fusion(f32[2,180,792]{2,1,0:T(8,128)S(1)} %fusion.9, f32[2,181,768]{2,1,0:T(8,128)S(1)} %fusion.27, f32[768]{0:T(1024)S(1)} %reshape.40, f32[2,180,768]{2,0,1:T(2,128)} %param.16), kind=kLoop, calls=%fused_computation.41 | loop fusion | flops 1382400 | bytes 6638592 | tf_op jit(solution)/shard_map/sub | solution.py:435
  48.2 0.0 copy-start.2
  48.2 1.6 %copy.31 = f32[2,180,768]{2,0,1:T(2,128)} copy(f32[2,180,768]{2,1,0:T(8,128)S(1)} %fusion.30) | data formatting | bytes 2211840
  49.8 0.0 copy-done.2
  49.8 0.7 %copy.37 = f32[2,2,32,180]{3,2,1,0:T(8,128)} copy(f32[2,2,32,180]{3,2,1,0:T(8,128)S(1)} %bitcast.11) | data formatting | bytes 184320
  (5 shorter events, 0.1 us)
Async XLA Ops:
  39.6 2.7 %copy-start = (f32[2,180,768]{2,1,0:T(8,128)S(1)}, f32[2,180,768]{2,1,0:T(8,128)}, u32[]{:S(2)}) copy-start(f32[2,180,768]{2,1,0:T(8,128)} %get-tuple-element.21.tracers_ref) | copy-start | bytes 3317764
  39.6 2.7 %copy-start.1 = (f32[2,180,72]{2,1,0:T(8,128)S(1)}, f32[2,180,72]{2,1,0:T(8,128)}, u32[]{:S(2)}) copy-start(f32[2,180,72]{2,1,0:T(8,128)} %get-tuple-element.13) | copy-start | bytes 311044
  42.3 2.1 %copy-start.3 = (f32[2,4,768]{2,1,0:T(4,128)S(1)}, f32[2,4,768]{2,1,0:T(4,128)}, u32[]{:S(2)}) copy-start(f32[2,4,768]{2,1,0:T(4,128)} %get-tuple-element.10) | copy-start | bytes 73732
  42.3 2.1 %copy-start.4 = (f32[2,8,768]{2,1,0:T(8,128)S(1)}, f32[2,8,768]{2,1,0:T(8,128)}, u32[]{:S(2)}) copy-start(f32[2,8,768]{2,1,0:T(8,128)} %get-tuple-element.11) | copy-start | bytes 147460
  42.4 2.1 %copy-start.5 = (f32[2,32,181]{2,1,0:T(8,128)S(1)}, f32[2,32,181]{2,1,0:T(8,128)}, u32[]{:S(2)}) copy-start(f32[2,32,181]{2,1,0:T(8,128)} %get-tuple-element.9) | copy-start | bytes 139012
  48.2 1.6 %copy-start.2 = (f32[128,180]{1,0:T(8,128)S(1)}, f32[128,180]{1,0:T(8,128)}, u32[]{:S(2)}) copy-start(f32[128,180]{1,0:T(8,128)} %get-tuple-element.15) | copy-start | bytes 276484

commit v18 on v17

--- a/solution.py
+++ b/solution.py
@@ -420,7 +420,7 @@
     west = west[:, west.shape[1] - 3 :]
     east = east[:, :3]
     smoothed = smoothed.reshape(2, levels, lat_rows, lon_cols)
-    zonal_rep = spread(zonal_speed, lat_rows, tracer_count)
+    zonal_rep = lax.optimization_barrier(spread(zonal_speed, lat_rows, tracer_count))
     merid_rep = lax.optimization_barrier(spread(merid_speed, lat_rows + 1, tracer_count))
     zonal_pad = jnp.concatenate([west, tracers, east], axis=1)
     left_x, right_x = stencil(zonal_pad, 1, lon_cols + 1, 1)

time: 50.7 us -> 51.1 us (level)
  other arithmetic: 3.76 us -> 5.21 us
  matrix products: 3.45 us -> 2.28 us
    add x1 -> x2, other arithmetic: 2.02 us -> 3.47 us  [upwind(): return jnp.maximum(speed, 0.0) * left + jnp.minimum(speed, 0.0) * right]
    dot_general x2, matrix products: 3.45 us -> 2.28 us  [spread(): return jnp.einsum('ljc,jm->lcm', values, pick, precision=EXACT_MODE)]
where the time goes in v18:
time: 51.1 us; the launch traced here: 50.8 us
  Pallas kernels  36.6 us (72%)
  local copies, waits for them, and re-layouts  5.94 us (12%)
  other arithmetic  5.21 us (10%)
  matrix products  2.28 us (4%)
  between operations  0.78 us (2%)
    pallas_call x1, Pallas kernels, exchange_all(): pl.pallas_call(functools.partial(filter_kernel, n, rows), out_shape=[jax....  36.6 us
    unnamed x15, local copies, waits for them, and re-layouts  4.73 us
    add x2, other arithmetic, upwind(): return jnp.maximum(speed, 0.0) * left + jnp.minimum(speed, 0.0) * right  3.47 us
    dot_general x2, matrix products, spread(): return jnp.einsum('ljc,jm->lcm', values, pick, precision=EXACT_MODE)  2.28 us
    sub x1, other arithmetic, local(): advected = tracers - metric[None, None, :] * change  1.67 us
    concatenate x1, local copies, waits for them, and re-layouts, local(): merid_pad = jnp.concatenate([south, tracers, north], axis=2)  1.04 us

profile of v18, /device:TPU:1, one launch (start us, length us, event | category | flops | bytes accessed | tf_op | source)
XLA Modules:
  0.0 50.8 jit_solution(4442063249089480026)
XLA Ops:
  0.6 2.4 %constant_dynamic-update-slice_fusion.1 = (f32[2,180,840]{2,1,0:T(8,128)S(1)}, f32[2,180,768]{2,1,0:T(8,128)}) fusion(f32[2,180,768]{2,0,1:T(2,128)} %param.16), kind=kLoop, calls=%fused_computation.67 | loop fusion | bytes 3342336
  3.0 36.6 %shard_map.167 = (f32[128,180]{1,0:T(8,128)}, f32[2,32,181]{2,1,0:T(8,128)}, f32[2,33,180]{2,1,0:T(8,128)}, f32[2,4,768]{2,1,0:T(4,128)}, f32[2,8,768]{2,1,0:T(8...) custom-call(f32[128,180]{1,0:T(8,128)} %bitcast.10, f32[4096]{0:T(1024)} %constant.88.clone.scales_ref, ...), custom_call_target="tpu_custom_call" | custom-call | tf_op jit(solution)/shard_map/pallas_call | solution.py:343
  39.6 0.0 copy-start
  39.6 0.0 copy-start.1
  39.6 1.0 %constant_dynamic-update-slice_fusion = f32[2,180,840]{2,1,0:T(8,128)S(1)} fusion(f32[2,180,840]{2,1,0:T(8,128)S(1)} %get-tuple-element.20, f32[2,180,72]{2,1,0:T(8,128)} %get-tuple-element.14), kind=kLoop, calls=%fused_computation.66 | loop fusion | bytes 292096 | tf_op jit(solution)/shard_map/concatenate | solution.py:428
  40.7 1.6 %fusion.39 = f32[2,180,792]{2,1,0:T(8,128)S(1)} fusion(f32[2,33,180]{2,1,0:T(8,128)} %get-tuple-element.12, s32[792]{0:T(1024)S(1)} %add_select_fusion), kind=kOutput, calls=%fused_computation.54 | convolution fusion | flops 112933656 | bytes 1191168 | tf_op jit(solution)/shard_map/ljc,jm->lcm/dot_general | solution.py:402
  42.3 0.0 copy-done
  42.3 0.0 copy-done.1
  42.3 0.0 copy-start.3
  42.3 2.0 %fusion.9 = f32[2,180,792]{2,1,0:T(8,128)S(1)} fusion(f32[2,180,768]{2,1,0:T(8,128)S(1)} %copy-done, f32[2,180,72]{2,1,0:T(8,128)S(1)} %copy-done.1, f32[2,180,840]{2,1,0:T(8,128)S(1)} %constant_dynamic-update-slice_fusion, f32[2,180,792]{2,1,0:T(8,128)S(1)} %fusion.39), kind=kLoop, calls=%fused_computation.17 | loop fusion | flops 7983360 | bytes 6912000 | tf_op jit(solution)/shard_map/add | solution.py:63
  44.4 0.0 copy-start.4
  44.4 0.0 copy-start.5
  44.4 0.0 copy-done.3
  44.4 0.7 %fusion.42 = f32[2,181,768]{2,1,0:T(8,128)S(1)} fusion(f32[2,32,181]{2,1,0:T(8,128)S(1)} %copy-done.3, s32[768]{0:T(1024)S(1)} %add_select_fusion.1), kind=kOutput, calls=%fused_computation.57 | convolution fusion | flops 106782720 | bytes 1161472 | tf_op jit(solution)/shard_map/ljc,jm->lcm/dot_general | solution.py:402
  45.1 0.0 copy-done.4
  45.1 0.1 copy-done.5
  45.2 1.4 %fusion.27 = f32[2,181,768]{2,1,0:T(8,128)S(1)} fusion(f32[2,3,768]{2,1,0:T(4,128)S(1)} %slice.74, f32[2,3,768]{2,1,0:T(4,128)S(1)} %slice.78, f32[2,180,768]{2,1,0:T(8,128)S(1)} %copy-done, f32[2,181,768]{2,1,0:T(8,128)S(1)} %fusion.42), kind=kLoop, calls=%fused_computation.37 | loop fusion | flops 8618496 | bytes 3366912 | tf_op jit(solution)/shard_map/add | solution.py:63
  46.7 0.1 broadcast.119
  46.8 0.1 reshape.40
  46.9 1.7 %fusion.30 = f32[2,180,768]{2,1,0:T(8,128)S(1)} fusion(f32[2,180,792]{2,1,0:T(8,128)S(1)} %fusion.9, f32[2,181,768]{2,1,0:T(8,128)S(1)} %fusion.27, f32[768]{0:T(1024)S(1)} %reshape.40, f32[2,180,768]{2,0,1:T(2,128)} %param.16), kind=kLoop, calls=%fused_computation.41 | loop fusion | flops 1382400 | bytes 6638592 | tf_op jit(solution)/shard_map/sub | solution.py:435
  48.6 0.0 copy-start.2
  48.6 1.6 %copy.31 = f32[2,180,768]{2,0,1:T(2,128)} copy(f32[2,180,768]{2,1,0:T(8,128)S(1)} %fusion.30) | data formatting | bytes 2211840
  50.1 0.0 copy-done.2
  50.1 0.7 %copy.37 = f32[2,2,32,180]{3,2,1,0:T(8,128)} copy(f32[2,2,32,180]{3,2,1,0:T(8,128)S(1)} %bitcast.11) | data formatting | bytes 184320
  (5 shorter events, 0.1 us)
Async XLA Ops:
  39.6 2.7 %copy-start = (f32[2,180,768]{2,1,0:T(8,128)S(1)}, f32[2,180,768]{2,1,0:T(8,128)}, u32[]{:S(2)}) copy-start(f32[2,180,768]{2,1,0:T(8,128)} %get-tuple-element.21.tracers_ref) | copy-start | bytes 3317764
  39.6 2.7 %copy-start.1 = (f32[2,180,72]{2,1,0:T(8,128)S(1)}, f32[2,180,72]{2,1,0:T(8,128)}, u32[]{:S(2)}) copy-start(f32[2,180,72]{2,1,0:T(8,128)} %get-tuple-element.13) | copy-start | bytes 311044
  42.3 2.1 %copy-start.3 = (f32[2,32,181]{2,1,0:T(8,128)S(1)}, f32[2,32,181]{2,1,0:T(8,128)}, u32[]{:S(2)}) copy-start(f32[2,32,181]{2,1,0:T(8,128)} %get-tuple-element.9) | copy-start | bytes 139012
  44.4 0.7 %copy-start.4 = (f32[2,4,768]{2,1,0:T(4,128)S(1)}, f32[2,4,768]{2,1,0:T(4,128)}, u32[]{:S(2)}) copy-start(f32[2,4,768]{2,1,0:T(4,128)} %get-tuple-element.10) | copy-start | bytes 73732
  44.4 0.8 %copy-start.5 = (f32[2,8,768]{2,1,0:T(8,128)S(1)}, f32[2,8,768]{2,1,0:T(8,128)}, u32[]{:S(2)}) copy-start(f32[2,8,768]{2,1,0:T(8,128)} %get-tuple-element.11) | copy-start | bytes 147460
  48.6 1.6 %copy-start.2 = (f32[128,180]{1,0:T(8,128)S(1)}, f32[128,180]{1,0:T(8,128)}, u32[]{:S(2)}) copy-start(f32[128,180]{1,0:T(8,128)} %get-tuple-element.15) | copy-start | bytes 276484
